TPU v7x, 32 devices: a whole 2x2x4 slice. The times are simulated.
32 devices in a mesh: dp: 16 (over z, y, x), tile: 2 (over core).
Axes of the slice: x: 2, y: 2, z: 4, core: 2. Of those that a mesh axis runs over, the one named last changes fastest.
Arguments:
- snapshots: bfloat16 [8208, 3, 32, 128], P('dp', None, 'tile'), may hold values from -16 to 16, as said below
- pair_start: int32 [8192], P('dp'), may hold values from 0 to 511
- bath_class: int32 [32, 128], P('tile'), may hold values from 0 to 3
- stencil_w: float32 [3, 3, 3, 9], replicated, may hold values from -1.25 to 1.25
- depth_gain: float32 [3, 4], replicated, may hold values from 0.5 to 2
- stencil_bias: float32 [3, 3], replicated, may hold values from -2 to 2
- readout: float32 [3], replicated, may hold values from -3.5 to 3.5
- panel_order: int32 [8], replicated, may hold values from 0 to 7, each once
Outputs:
- chol_panels: float32 [2, 2048, 1024], P('tile', 'dp')
- cross_whitened: float32 [2, 2048, 1024], P('tile', 'dp')
- ridge_shift: float32 [], replicated
Inputs may be any that keep to these rules, and one draw needn't show every extreme that they name: snapshots stay within the range. The pair's second snapshot is the next one, pair_start + 1, of the same index of dp. `panel_order`: each block number appears once.
All inputs are finite; a program needn't handle non-finite values.
Results may differ from a plain program's by a relative error of at most 0.0032.
Values may be sent and summed in bfloat16 or wider, within the bound.
No kernel may reach another device: no remote copies, remote signals or barrier semaphores. Data moves between devices by JAX's collectives and lax.ppermute only.
A program may use at most 192 MiB of HBM per device.

v0:
```python
import jax
import jax.numpy as jnp
from jax import lax
from jax.sharding import PartitionSpec as P

PANEL = 512


ridge_factor = 0.5


def extended(block, sides, width):
    for axis, dim in sides:
        count = lax.axis_size(axis)
        forward = [(i, i + 1) for i in range(count - 1)]
        backward = [(target, source) for source, target in forward]
        low = lax.ppermute(
            lax.slice_in_dim(block, block.shape[dim] - width, None, axis=dim), axis, forward
        )
        high = lax.ppermute(lax.slice_in_dim(block, 0, width, axis=dim), axis, backward)
        block = jnp.concatenate([low, block, high], axis=dim)
    return block


def gain_field(classes, gains):
    field = jnp.zeros(classes.shape, jnp.float32)
    for class_idx in range(gains.shape[0]):
        field = field + jnp.where(
            classes == class_idx, gains[class_idx], jnp.zeros((), jnp.float32)
        )
    return field


def layer_step(padded_rows, gains_map, weights, bias):
    fields_count = padded_rows.shape[1]
    kernel = weights.reshape(fields_count, fields_count, 3, 3)
    stencil_sum = lax.conv_general_dilated(
        padded_rows,
        kernel,
        (1, 1),
        ((0, 0), (1, 1)),
        dimension_numbers=("NCHW", "OIHW", "NCHW"),
        precision=lax.Precision.HIGHEST,
        preferred_element_type=jnp.float32,
    )
    centre = padded_rows[:, :, 1:-1, :]
    return centre + jnp.tanh(gains_map[None, None] * stencil_sum + bias[None, :, None, None])


def readout_sum(fields, readout):
    result = jnp.zeros((fields.shape[0], fields.shape[2], fields.shape[3]), jnp.float32)
    for field_idx in range(fields.shape[1]):
        result = result + readout[field_idx] * fields[:, field_idx]
    return result


def right_solve(lower_factor, rows_in):
    return lax.linalg.triangular_solve(
        lower_factor, rows_in, left_side=False, lower=True, transpose_a=True
    )


def panel_factor(diag_rows):
    lead = jnp.linalg.cholesky(diag_rows[:PANEL, :PANEL])
    below = right_solve(lead, diag_rows[PANEL:, :PANEL])
    rest = diag_rows[PANEL:, PANEL:] - jnp.dot(below, below.T, precision=lax.Precision.HIGHEST)
    tail = jnp.linalg.cholesky(rest)
    return (lead, below, tail)


def apply_factor(rows_in, lead, below, tail):
    left = right_solve(lead, rows_in[:, :PANEL])
    inner = rows_in[:, PANEL:] - jnp.dot(left, below.T, precision=lax.Precision.HIGHEST)
    right = right_solve(tail, inner)
    return jnp.concatenate([left, right], axis=1)


def contract(source, panel, row_count):
    part_cols = lax.slice_in_dim(source, 0, row_count, axis=1)
    return lax.dot_general(
        part_cols, panel, (((0,), (0,)), ((), ())), preferred_element_type=jnp.float32
    )


def on_device(
    snapshots, pair_start, bath_class, stencil_w, depth_gain, stencil_bias, readout, panel_order
):
    tile_pos = lax.axis_index("tile")
    dp_pos = lax.axis_index("dp")
    tile_count = lax.axis_size("tile")
    dp_count = lax.axis_size("dp")
    layer_count = stencil_w.shape[0]
    tile_rows = bath_class.shape[0]
    grid_cols = bath_class.shape[1]
    tile_obs = tile_rows * grid_cols
    own_rows = tile_obs // dp_count
    width = 2 * PANEL
    snap_count = snapshots.shape[0]
    fields = snapshots.astype(jnp.float32)
    for layer_idx in range(layer_count):
        padded = extended(fields, (("tile", 2),), 1)
        gains_map = gain_field(bath_class, depth_gain[layer_idx])
        fields = layer_step(padded, gains_map, stencil_w[layer_idx], stencil_bias[layer_idx])
    encoded = readout_sum(fields, readout).reshape(snap_count, tile_obs).astype(jnp.bfloat16)
    earlier = jnp.take(encoded, pair_start, axis=0)
    later = jnp.take(encoded, pair_start + 1, axis=0)
    first_block = panel_order[0]
    second_block = panel_order[1]
    every_col = lax.all_gather(earlier, "tile", axis=1, tiled=True)
    panel = jnp.concatenate(
        [
            lax.dynamic_slice_in_dim(every_col, first_block * PANEL, PANEL, 1),
            lax.dynamic_slice_in_dim(every_col, second_block * PANEL, PANEL, 1),
        ],
        axis=1,
    )
    energy_sum = lax.psum(jnp.sum(jnp.square(earlier.astype(jnp.float32))), ("dp", "tile"))
    pairs_total = float(pair_start.shape[0] * dp_count)
    shift_value = ridge_factor * (energy_sum / pairs_total) / float(tile_obs * tile_count)
    grow_start = tile_pos * tile_obs + dp_pos * own_rows
    own_block = grow_start // PANEL
    offset = grow_start - own_block * PANEL
    gram_own = (
        lax.psum_scatter(
            contract(earlier, panel, lax.axis_size("dp") * own_rows),
            "dp",
            scatter_dimension=0,
            tiled=True,
        )
        / pairs_total
    )
    placed = lax.dynamic_update_slice_in_dim(
        jnp.zeros((PANEL, width), jnp.float32), gram_own, offset, 0
    )
    diag_part = jnp.concatenate(
        [
            jnp.where(own_block == first_block, placed, 0.0),
            jnp.where(own_block == second_block, placed, 0.0),
        ],
        axis=0,
    )
    diag_rows = lax.psum(diag_part, ("dp", "tile"))
    cross_own = (
        lax.psum_scatter(
            contract(later, panel, lax.axis_size("dp") * own_rows),
            "dp",
            scatter_dimension=0,
            tiled=True,
        )
        / pairs_total
    )
    diag_rows = diag_rows + shift_value * jnp.eye(width, dtype=jnp.float32)
    row_obs = grow_start + jnp.arange(own_rows, dtype=jnp.int32)[:, None]
    col_obs = jnp.concatenate(
        [
            first_block * PANEL + jnp.arange(PANEL, dtype=jnp.int32),
            second_block * PANEL + jnp.arange(PANEL, dtype=jnp.int32),
        ]
    )[None, :]
    shifted = gram_own + shift_value * (row_obs == col_obs).astype(jnp.float32)
    lead, below, tail = panel_factor(diag_rows)
    computed = apply_factor(shifted, lead, below, tail)
    panel_full = jnp.concatenate(
        [
            jnp.concatenate([lead, jnp.zeros_like(lead)], axis=1),
            jnp.concatenate([below, tail], axis=1),
        ],
        axis=0,
    )
    first_piece = lax.dynamic_slice_in_dim(panel_full, offset, own_rows, 0)
    second_piece = lax.dynamic_slice_in_dim(panel_full, PANEL + offset, own_rows, 0)
    factor_rows = jnp.where(
        own_block == first_block,
        first_piece,
        jnp.where(own_block == second_block, second_piece, computed),
    )
    whitened = apply_factor(cross_own, lead, below, tail)
    return (factor_rows[None], whitened[None], shift_value)


def solution(mesh):
    placed = (P("dp", None, "tile", None), P("dp"), P("tile", None), P(), P(), P(), P(), P())
    return jax.shard_map(
        on_device,
        mesh=mesh,
        in_specs=placed,
        out_specs=(P("tile", "dp", None), P("tile", "dp", None), P()),
        check_vma=False,
    )
```

profile of v0, /device:TPU:0, one launch (start us, length us, event | category | flops | bytes accessed | tf_op | source)
XLA Modules:
  0.0 1661.3 jit_solution(145919323454137758)
XLA Ops:
  7.2 3.9 fusion.152
  11.1 2.4 collective-permute-start
  16.2 8.4 convert_element_type.14
  25.9 3.1 select_add_fusion.2
  29.0 5.6 select_add_fusion.3
  34.6 12.8 pad_maximum_fusion
  47.5 21.0 %copy.141 = f32[513,3,18,128]{0,1,3,2:T(4,128)} copy(f32[513,3,18,128]{3,2,1,0:T(8,128)} %pad_maximum_fusion) | data formatting | bytes 28366848 | tf_op jit(solution)/shard_map/concatenate | solution.py:21
  68.5 171.2 %fusion.157 = f32[513,3,16,128]{0,1,3,2:T(4,128)} fusion(f32[513,3,18,128]{0,1,3,2:T(4,128)} %copy.141, f32[3,3,3,3]{1,0,3,2:T(4,128)S(1)} %bitcast.202), kind=kOutput, calls=%fused_computation.288 | convolution fusion | flops 1015887744 | bytes 26791236 | tf_op jit(solution)/shard_map/conv_general_dilated | solution.py:37
  239.6 16.2 copy.143
  255.9 7.9 tanh_add_fusion.2
  263.8 4.5 copy-done.1
  269.3 3.1 collective-permute-start.2
  274.3 2.3 collective-permute-done.3
  276.6 12.8 pad_maximum_fusion.1
  289.5 21.0 %copy.144 = f32[513,3,18,128]{0,1,3,2:T(4,128)} copy(f32[513,3,18,128]{3,2,1,0:T(8,128)} %pad_maximum_fusion.1) | data formatting | bytes 28366848 | tf_op jit(solution)/shard_map/concatenate | solution.py:21
  310.4 170.7 %fusion.158 = f32[513,3,16,128]{0,1,3,2:T(4,128)} fusion(f32[513,3,18,128]{0,1,3,2:T(4,128)} %copy.144, f32[3,3,3,3]{1,0,3,2:T(4,128)S(1)} %bitcast.204), kind=kOutput, calls=%fused_computation.289 | convolution fusion | flops 1015887744 | bytes 26791236 | tf_op jit(solution)/shard_map/conv_general_dilated | solution.py:37
  481.1 16.3 copy.146
  497.4 9.7 tanh_add_fusion.1
  507.1 4.5 copy-done
  518.9 12.8 pad_maximum_fusion.2
  531.8 21.0 %copy.147 = f32[513,3,18,128]{0,1,3,2:T(4,128)} copy(f32[513,3,18,128]{3,2,1,0:T(8,128)} %pad_maximum_fusion.2) | data formatting | bytes 28366848 | tf_op jit(solution)/shard_map/concatenate | solution.py:21
  552.7 170.7 %fusion.159 = f32[513,3,16,128]{0,1,3,2:T(4,128)} fusion(f32[513,3,18,128]{0,1,3,2:T(4,128)} %copy.147, f32[3,3,3,3]{1,0,3,2:T(4,128)S(1)} %bitcast.203), kind=kOutput, calls=%fused_computation.290 | convolution fusion | flops 1015887744 | bytes 26791236 | tf_op jit(solution)/shard_map/conv_general_dilated | solution.py:37
  723.4 16.3 copy.149
  739.6 9.4 tanh_add_fusion
  749.1 2.8 fusion.3
  752.8 3.3 gather_fusion
  756.1 4.0 multiply_reduce_fusion
  762.1 14.0 all-gather.2.cloned.1.call-done
  777.3 7.2 fusion.18
  784.6 3.3 gather_fusion.1
  787.9 7.3 fusion.4
  796.6 45.6 %psum.15 = f32[]{:T(128)} all-reduce(f32[]{:T(128)} %get-tuple-element.74), channel_id=1, replica_groups=mesh['dp'=16,'tile'=2] {'dp','tile'}, use_global_device_ids=true, to_apply=%region_3.5 | all-reduce | flops 1 | bytes 8 | tf_op jit(solution)/shard_map/psum | solution.py:117
  842.9 122.0 %reduce-scatter.3.cloned.1.call-done = f32[128,1024]{0,1:T(8,128)} async-done(((f32[2048,1024]{0,1:T(8,128)}), f32[128,1024]{0,1:T(8,128)}) %reduce-scatter.3.cloned.1.call-update) | async-done | bytes 524304 | tf_op jit(solution)/shard_map/reduce_scatter | solution.py:124
  967.7 2.3 pad_maximum_fusion.3
  970.1 178.3 %reduce-scatter.5.cloned.1.call-done = f32[128,1024]{0,1:T(8,128)} async-done(((f32[2048,1024]{0,1:T(8,128)}), f32[128,1024]{0,1:T(8,128)}) %reduce-scatter.5.cloned.1.call-update) | async-done | bytes 524304 | tf_op jit(solution)/shard_map/reduce_scatter | solution.py:144
  1150.3 147.7 %all-reduce.4.cloned.1.call-done = f32[1024,1024]{0,1:T(8,128)} async-done(((f32[1024,1024]{0,1:T(8,128)}), f32[1024,1024]{0,1:T(8,128)}) %all-reduce.4.cloned.1.call-update) | async-done | bytes 4194320 | tf_op jit(solution)/shard_map/psum | solution.py:142
  1298.0 2.6 select_add_fusion
  1304.4 11.7 cholesky.286
  1316.3 9.8 custom-call.33
  1326.7 12.2 cholesky.305
  1340.3 9.8 custom-call.34
  1350.7 11.7 cholesky.326
  1363.2 9.8 custom-call.35
  1373.6 11.8 cholesky.343
  1389.9 7.8 while.9
  1397.7 39.3 %custom-call.26 = f32[4,128,128]{1,2,0:T(8,128)S(1)} custom-call(f32[4,128,128]{2,1,0:T(8,128)S(1)} %get-tuple-element.21), custom_call_target="InvertDiagBlocksLowerTriangular" | custom-call | tf_op jit(solution)/shard_map/triangular_solve | solution.py:58
  1444.0 3.1 convolution_subtract_fusion
  1450.8 11.7 cholesky.358
  1463.2 9.8 custom-call.36
  1475.1 2.1 convolution_subtract_fusion.6
  1485.7 12.3 cholesky.377
  1501.3 10.4 custom-call.37
  1514.8 12.3 cholesky.398
  1528.7 10.6 custom-call.38
  1541.6 12.3 cholesky.415
  1567.1 13.7 while.10
  1567.7 2.8 bitcast_dynamic-update-slice_fusion.5
  1571.2 2.8 bitcast_dynamic-update-slice_fusion.5
  1574.6 2.8 bitcast_dynamic-update-slice_fusion.5
  1578.1 2.7 bitcast_dynamic-update-slice_fusion.5
  1580.8 41.0 %custom-call.40 = f32[4,128,128]{1,2,0:T(8,128)} custom-call(f32[4,128,128]{2,1,0:T(8,128)} %get-tuple-element.41), custom_call_target="InvertDiagBlocksLowerTriangular" | custom-call | tf_op jit(solution)/shard_map/triangular_solve/custom-call.8 | solution.py:58
  1626.0 2.8 convolution_subtract_fusion.5
  1638.5 2.8 convolution_subtract_fusion.4
  1650.3 2.2 select_maximum_fusion
  (209 shorter events, 108.3 us)
Async XLA Ops:
  7.2 768.9 %all-gather.2.cloned.1.call-start = ((), (), s32[]{:S(2)}) async-start(), calls=%async_computation.2 | async-start | bytes 6291456 | tf_op jit(solution)/shard_map/all_gather | solution.py:109
  11.1 23.5 %collective-permute-start = (f32[513,3,1,128]{3,2,1,0:T(1,128)S(1)}, f32[513,3,1,128]{3,2,1,0:T(1,128)S(1)}, u32[]{:S(2)}, u32[]{:S(2)}) collective-permute-start(f32[513,3,1,128]{3,2,1,0:T(1,128)S(1)} %get-tuple-element.89), channel_id=1, source_target_pairs={{0,1},{2,3},{4,5},{6,7},{8,9},{10,11},{12,13},{14,15},{16,17},{18,... | collective-permute-start | bytes 2363912 | tf_op jit(solution)/shard_map/ppermute | solution.py:17
  13.6 21.1 %collective-permute-start.1 = (f32[513,3,1,128]{3,2,1,0:T(1,128)S(1)}, f32[513,3,1,128]{3,2,1,0:T(1,128)S(1)}, u32[]{:S(2)}, u32[]{:S(2)}) collective-permute-start(f32[513,3,1,128]{3,2,1,0:T(1,128)S(1)} %get-tuple-element.90), channel_id=1, source_target_pairs={{1,0},{3,2},{5,4},{7,6},{9,8},{11,10},{13,12},{15,14},{17,16},{19,... | collective-permute-start | bytes 2363912 | tf_op jit(solution)/shard_map/ppermute | solution.py:20
  16.2 8.5 copy-start.19
  16.2 9.2 copy-start.26
  16.2 9.7 copy-start.21
  263.8 4.5 copy-start.1
  269.3 5.0 collective-permute-start.2
  272.5 4.2 collective-permute-start.3
  481.1 16.3 copy-start.16
  481.1 16.3 copy-start.24
  497.4 18.7 %copy-start.18 = (f32[1,3,3,9]{3,2,1,0:T(4,128)S(1)}, f32[1,3,3,9]{3,2,1,0:T(4,128)}, u32[]{:S(2)}) copy-start(f32[1,3,3,9]{3,2,1,0:T(4,128)} %get-tuple-element.119) | copy-start | bytes 976
  497.4 18.8 %copy-start.20 = (s32[512]{0:T(512)S(1)}, s32[512]{0:T(512)}, u32[]{:S(2)}) copy-start(s32[512]{0:T(512)} %param.14) | copy-start | bytes 6148
  497.4 18.8 %copy-start.22 = (f32[3]{0:T(128)S(1)}, f32[3]{0:T(128)}, u32[]{:S(2)}) copy-start(f32[3]{0:T(128)} %param.19) | copy-start | bytes 40
  507.1 4.5 copy-start
  512.6 4.2 collective-permute-start.4
  514.7 4.2 collective-permute-start.5
  723.4 16.3 copy-start.17
  723.4 16.3 copy-start.23
  756.1 4.1 copy-start.25
  760.1 204.7 %reduce-scatter.3.cloned.1.call-start = ((), (), s32[]{:S(2)}) async-start(), calls=%async_computation.3 | async-start | bytes 8912896 | tf_op jit(solution)/shard_map/reduce_scatter | solution.py:124
  784.6 363.8 %reduce-scatter.5.cloned.1.call-start = ((), (), s32[]{:S(2)}) async-start(), calls=%async_computation.5 | async-start | bytes 8912896 | tf_op jit(solution)/shard_map/reduce_scatter | solution.py:144
  795.2 502.8 %all-reduce.4.cloned.1.call-start = ((), (), s32[]{:S(2)}) async-start(), calls=%async_computation.4 | async-start | bytes 8388608 | tf_op jit(solution)/shard_map/psum | solution.py:142
  1300.5 1.9 copy-start.2
  1449.8 1.0 copy-start.5
  1462.6 0.6 copy-start.14
  1514.2 0.7 copy-start.11
  1580.8 49.8 %copy-start.3 = (f32[512,512]{1,0:T(8,128)S(1)}, f32[512,512]{1,0:T(8,128)}, u32[]{:S(2)}) copy-start(f32[512,512]{1,0:T(8,128)} %get-tuple-element.253) | copy-start | bytes 3145732
  1624.4 1.6 copy-start.9
  1626.0 2.8 copy-start.12
  1628.8 1.2 copy-start.15
  1630.0 0.6 copy-start.8
  1633.0 8.2 copy-start.6
  1638.2 12.1 copy-start.4
  1646.6 5.8 copy-start.7
  1646.7 5.8 copy-start.10
  1646.7 5.8 copy-start.13
Sparse Core Ops, SparseCore 0:
  760.3 15.7 all-gather.1
  784.7 180.1 reduce-scatter.2
  967.2 181.1 reduce-scatter.4
  1153.8 144.1 all-reduce.3
where the time goes:
time: 1670 us; the launch traced here: 1660 us
  matrix products  575 us (34%)
  waiting for transfers between devices  467 us (28%)
  other arithmetic  353 us (21%)
  local copies, waits for them, and re-layouts  186 us (11%)
  blocking collectives  45.6 us (3%)
  between operations  24.3 us (1%)
    conv_general_dilated x3, matrix products, layer_step(): lax.conv_general_dilated(padded_rows, kernel, (1, 1), ((0, 0), (1, 1)), d...  512 us
    reduce_scatter x1, waiting for transfers between devices, on_device(): lax.psum_scatter(contract(later, panel, lax.axis_size('dp') * own_rows),...  178 us
    psum x1, waiting for transfers between devices, on_device(): diag_rows = lax.psum(diag_part, ('dp', 'tile'))  148 us
    reduce_scatter x1, waiting for transfers between devices, on_device(): lax.psum_scatter(contract(earlier, panel, lax.axis_size('dp') * own_rows)...  122 us
    another operation x15, other arithmetic, panel_factor(): tail = jnp.linalg.cholesky(rest)  84.9 us
    another operation x4, other arithmetic, right_solve(): lax.linalg.triangular_solve(lower_factor, rows_in, left_side=False, lower...  81.6 us
    another operation x15, other arithmetic, panel_factor(): lead = jnp.linalg.cholesky(diag_rows[:PANEL, :PANEL])  79.7 us
    concatenate x3, local copies, waits for them, and re-layouts, extended(): block = jnp.concatenate([low, block, high], axis=dim)  62.9 us
  transfers between devices with their start and end apart: 10, of which 7 were waited for; matrix products, arithmetic and copies ran while one was open for 2% of the time, Pallas kernels for 0%

commit v1 on v0

v1 whole, which is shorter than its diff:
```python
import jax
import jax.numpy as jnp
from jax import lax
from jax.experimental import pallas as pl
from jax.experimental.pallas import tpu as pltpu
from jax.sharding import PartitionSpec as P

F32 = jnp.float32
BF16 = jnp.bfloat16


EDGE = 128
PANEL = 512


def halo_kernel(tile_ref, own_ref, out_ref):
    block = own_ref.shape[0]
    row = lax.broadcasted_iota(jnp.int32, (16, 48), 0)
    col = lax.broadcasted_iota(jnp.int32, (16, 48), 1)
    dist = lax.div(row, 3)
    source = jnp.where(tile_ref[0] == 0, 15 - dist, dist)
    pick = jnp.where((row < 9) & (col == lax.rem(row, 3) * 16 + source), 1.0, 0.0).astype(BF16)
    for base in range(0, block, 3):
        cells = jnp.concatenate(
            [own_ref[base + k].reshape(48, 128) for k in range(3)], axis=1
        )
        rows = jnp.dot(pick, cells, preferred_element_type=F32).astype(BF16)
        for k in range(3):
            out_ref[base + k] = rows[:, 128 * k : 128 * (k + 1)]


def halo_rows(tile_idx, snapshots):
    count = snapshots.shape[0]
    block = next(b for b in (57, 27, 9, 3) if count % b == 0)
    return pl.pallas_call(
        halo_kernel,
        grid=(count // block,),
        in_specs=[
            pl.BlockSpec(memory_space=pltpu.SMEM),
            pl.BlockSpec((block, 3, 16, 128), lambda i: (i, 0, 0, 0)),
        ],
        out_specs=pl.BlockSpec((block, 16, 128), lambda i: (i, 0, 0)),
        out_shape=jax.ShapeDtypeStruct((count, 16, 128), BF16),
        name="halo_rows",
    )(tile_idx, snapshots)


GROUP = 32
BLOCK = 32


def encode_kernel(
    tile_ref, w_ref, gain_ref, bias_ref, readout_ref,
    own_ref, halo_ref, cls_ref, ncls_ref, out_ref,
    mat_ref, gmap_ref, bmap_ref, enc_ref, *, count,
):
    @pl.when(pl.program_id(0) == 0)
    def _():
        tile = tile_ref[0]
        r_out = lax.broadcasted_iota(jnp.int32, (56, 64), 0)
        r_in = lax.broadcasted_iota(jnp.int32, (56, 64), 1)

        def place(r):
            h = r - 48
            outside = jnp.where(tile == 0, 16 + lax.div(h, 3), -1 - lax.div(h, 3))
            return jnp.where(r < 48, lax.div(r, 16), lax.rem(h, 3)), jnp.where(r < 48, lax.rem(r, 16), outside)

        o_idx, o_pos = place(r_out)
        i_idx, i_pos = place(r_in)
        tap = i_pos - o_pos + 1
        good = (tap >= 0) & (tap <= 2) & (r_in < 57) & (r_out < 54)
        code = jnp.where(good, (o_idx * 3 + i_idx) * 3 + tap, -1)
        hits = [code == k for k in range(27)]
        for layer in range(3):
            for b in range(3):
                acc = jnp.zeros((56, 64), F32)
                for k in range(27):
                    weight = w_ref[((layer * 9 + k // 3) * 3 + k % 3) * 3 + b]
                    acc = jnp.where(hits[k], weight, acc)
                high = acc.astype(BF16).astype(F32)
                low = acc - high
                full = jnp.concatenate([high, low, high], axis=1).astype(BF16)
                mat_ref[layer, 56 * b : 56 * (b + 1), :] = full
        own_cls = cls_ref[...]
        near = ncls_ref[...]
        h0 = jnp.where(tile == 0, near[0:1], near[15:16])
        h1 = jnp.where(tile == 0, near[1:2], near[14:15])
        cls = jnp.concatenate([own_cls] * 3 + [h0, h0, h0, h1, h1, h1, h1, h1], axis=0)
        row = lax.broadcasted_iota(jnp.int32, (56, 128), 0)
        field = jnp.where(row < 48, lax.div(row, 16), lax.rem(row - 48, 3))
        for layer in range(3):
            gmap = jnp.zeros((56, 128), F32)
            for c in range(4):
                gmap = jnp.where(cls == c, gain_ref[layer * 4 + c], gmap)
            gmap_ref[layer] = gmap
            bmap = jnp.zeros((56, 128), F32)
            for f in range(3):
                bmap = jnp.where(field == f, bias_ref[layer * 3 + f], bmap)
            bmap_ref[layer] = bmap

    lane = lax.broadcasted_iota(jnp.int32, (56, 128), 1)
    first_lane = lane == 0
    last_lane = lane == 127
    blank = jnp.zeros((8, 128), F32)
    ro = [readout_ref[f] for f in range(3)]

    def group(g, carry):
        base = g * GROUP
        high = []
        low = []
        fields = []
        for k in range(GROUP):
            own = own_ref[base + k].reshape(48, 128)
            halo = halo_ref[base + k]
            high.append(jnp.concatenate([own, halo], axis=0))
            fields.append(
                jnp.concatenate([own.astype(F32), halo.astype(F32)[:8]], axis=0)
            )
        for layer in range(3):
            top = jnp.concatenate(high, axis=1)
            if layer == 0:
                stacked = jnp.concatenate([top, top], axis=0)
                mat = mat_ref[layer, :, 0:128]
            else:
                stacked = jnp.concatenate([top, top, jnp.concatenate(low, axis=1)], axis=0)
                mat = mat_ref[layer]
            sums = jnp.dot(mat, stacked, preferred_element_type=F32)
            high = []
            low = []
            for k in range(GROUP):
                part = sums[:, 128 * k : 128 * (k + 1)]
                left = jnp.where(first_lane, 0.0, pltpu.roll(part[0:56], 1, 1))
                right = jnp.where(last_lane, 0.0, pltpu.roll(part[112:168], 127, 1))
                total = left + part[56:112] + right
                fields[k] = fields[k] + jnp.tanh(gmap_ref[layer] * total + bmap_ref[layer])
                if layer < 2:
                    wide = jnp.concatenate([fields[k], blank], axis=0)
                    upper = wide.astype(BF16)
                    high.append(upper)
                    low.append((wide - upper.astype(F32)).astype(BF16))
        for k in range(GROUP):
            f = fields[k]
            value = ro[0] * f[0:16] + ro[1] * f[16:32] + ro[2] * f[32:48]
            enc_ref[pl.ds((base + k) * 16, 16), :] = value
        return carry

    lax.fori_loop(0, BLOCK // GROUP, group, 0, unroll=True)
    snap = lax.broadcasted_iota(jnp.int32, (BLOCK, 128), 0) + pl.program_id(0) * BLOCK
    for r in range(16):
        rows = enc_ref[pl.ds(r, BLOCK, stride=16), :]
        out_ref[r] = jnp.where(snap < count, rows, 0.0).astype(BF16)


def encode(tile_idx, snapshots, halo, classes, near_classes, stencil_w, depth_gain, bias, readout):
    count = snapshots.shape[0]
    smem = pl.BlockSpec(memory_space=pltpu.SMEM)
    whole = pl.BlockSpec((16, 128), lambda i: (0, 0))

    def body(*refs):
        encode_kernel(*refs, count=count)

    return pl.pallas_call(
        body,
        grid=(pl.cdiv(count, BLOCK),),
        in_specs=[
            smem, smem, smem, smem, smem,
            pl.BlockSpec((BLOCK, 3, 16, 128), lambda i: (i, 0, 0, 0)),
            pl.BlockSpec((BLOCK, 16, 128), lambda i: (i, 0, 0)),
            whole, whole,
        ],
        out_specs=pl.BlockSpec((16, BLOCK, 128), lambda i: (0, i, 0)),
        out_shape=jax.ShapeDtypeStruct((16, pl.cdiv(count, BLOCK) * BLOCK, 128), BF16),
        scratch_shapes=[
            pltpu.VMEM((3, 168, 192), BF16),
            pltpu.VMEM((3, 56, 128), F32),
            pltpu.VMEM((3, 56, 128), F32),
            pltpu.VMEM((BLOCK * 16, 128), F32),
        ],
        name="encode",
    )(
        tile_idx, stencil_w.reshape(-1), depth_gain.reshape(-1), bias.reshape(-1), readout,
        snapshots, halo, classes, near_classes,
    )


def split(x):
    high = x.astype(BF16)
    return high, (x - high.astype(F32)).astype(BF16)


def lhs3(x):
    high, low = split(x)
    return jnp.concatenate([high, high, low], axis=1)


def rhs3(x):
    high, low = split(x)
    return jnp.concatenate([high, low, high], axis=1)


def dot_nt(a, b):
    return lax.dot_general(a, b, (((1,), (1,)), ((), ())), preferred_element_type=F32)


def factor_diag(block, eye):
    row8 = lax.broadcasted_iota(jnp.int32, (8, EDGE), 0)
    groups = EDGE // 8
    a = [block[8 * g : 8 * (g + 1)] for g in range(groups)]
    b = [eye[8 * g : 8 * (g + 1)] for g in range(groups)]
    for j in range(EDGE):
        home, inner = divmod(j, 8)
        row = jnp.broadcast_to(a[home][inner : inner + 1, :], (8, EDGE))
        pivot = jnp.broadcast_to(row[:, j : j + 1], (8, EDGE))
        invert = 1.0 / pivot
        scaled = row * invert
        brow = jnp.broadcast_to(b[home][inner : inner + 1, :], (8, EDGE)) * invert
        for g in range(home, groups):
            if g == home and inner == 7:
                continue
            col = jnp.broadcast_to(a[g][:, j : j + 1], (8, EDGE))
            if g == home:
                col = jnp.where(row8 > inner, col, 0.0)
            a[g] = a[g] - col * scaled
            b[g] = b[g] - col * brow
    return jnp.concatenate(a, axis=0), jnp.concatenate(b, axis=0)


def pick_kernel(start_ref, enc_ref, keep_ref, near_ref, out_ref):
    snaps = enc_ref.shape[1]
    pairs = start_ref.shape[1]
    snap_idx = lax.broadcasted_iota(jnp.int32, (snaps, pairs), 0)
    hit = jnp.where(snap_idx == start_ref[...], 1.0, 0.0).astype(BF16)
    panel = jnp.concatenate(
        [keep_ref[r] + near_ref[r] for r in range(keep_ref.shape[0])], axis=1
    )
    tn = (((0,), (0,)), ((), ()))
    out_ref[0:PANEL, :] = lax.dot_general(
        panel, hit, tn, preferred_element_type=F32
    ).astype(BF16)
    norms = jnp.zeros(enc_ref.shape[1:], F32)
    for r in range(enc_ref.shape[0]):
        value = enc_ref[r].astype(F32)
        norms = norms + value * value
    total = jnp.zeros((enc_ref.shape[2], pairs), F32)
    for _ in range(3):
        high = norms.astype(BF16)
        total = total + lax.dot_general(high, hit, tn, preferred_element_type=F32)
        norms = norms - high.astype(F32)
    total = jnp.sum(jnp.sum(total, axis=0, keepdims=True), axis=1, keepdims=True)
    rest = jnp.broadcast_to(total, (16, pairs))
    row = lax.broadcasted_iota(jnp.int32, (16, pairs), 0)
    packed = jnp.zeros((16, pairs), BF16)
    for k in range(3):
        high = rest.astype(BF16)
        packed = jnp.where(row == k, high.astype(F32), packed.astype(F32)).astype(BF16)
        rest = rest - high.astype(F32)
    out_ref[PANEL:, :] = packed


def pick(starts, enc, keep, near):
    pairs = starts.shape[1]
    return pl.pallas_call(
        pick_kernel,
        out_shape=jax.ShapeDtypeStruct((PANEL + 16, pairs), BF16),
        compiler_params=pltpu.CompilerParams(vmem_limit_bytes=40 * 2**20),
        name="pick_pairs",
    )(starts, enc, keep, near)


def factor_kernel(tile_ref, mine_ref, near_ref, low_ref, inv_ref, shift_ref, *, pairs_total, obs):
    step = pl.program_id(0)
    width = 2 * PANEL

    @pl.when(step == 0)
    def _():
        low_ref[...] = jnp.zeros((width, width), F32)
        shift_ref[...] = jnp.zeros(shift_ref.shape, F32)

    flip = tile_ref[0] == 1
    mine = mine_ref[0, 0:PANEL, :]
    near = near_ref[0, 0:PANEL, :]
    lead = jnp.where(flip, near, mine)
    tail = jnp.where(flip, mine, near)
    low_ref[0:PANEL, 0:PANEL] += dot_nt(lead, lead)
    low_ref[PANEL:, 0:PANEL] += dot_nt(tail, lead)
    low_ref[PANEL:, PANEL:] += dot_nt(tail, tail)
    parts = mine_ref[0, PANEL:, 0:128].astype(F32) + 0.0
    parts_near = near_ref[0, PANEL:, 0:128].astype(F32) + 0.0
    both = jnp.sum(parts, axis=0, keepdims=True) + jnp.sum(parts_near, axis=0, keepdims=True)
    shift_ref[...] += jnp.broadcast_to(both, shift_ref.shape)

    @pl.when(step == pl.num_programs(0) - 1)
    def _():
        shift = 0.5 * (shift_ref[...] / pairs_total) / float(obs)
        shift_ref[...] = shift
        factor(low_ref, inv_ref, shift, 1.0 / pairs_total)


def factor(low_ref, inv_ref, shift, scale):
    width = low_ref.shape[0]
    row = lax.broadcasted_iota(jnp.int32, (EDGE, EDGE), 0)
    col = lax.broadcasted_iota(jnp.int32, (EDGE, EDGE), 1)
    eye = jnp.where(row == col, 1.0, 0.0)
    blocks = width // EDGE
    shift_wide = jnp.concatenate([shift] * (EDGE // 8), axis=0)

    for i in range(blocks):
        rows = pl.ds(EDGE * i, EDGE)
        low_ref[rows, :] = low_ref[rows, :] * scale
        low_ref[rows, EDGE * i : EDGE * (i + 1)] += jnp.where(row == col, shift_wide, 0.0)
        if EDGE * (i + 1) < width:
            low_ref[rows, EDGE * (i + 1) :] = jnp.zeros((EDGE, width - EDGE * (i + 1)), F32)

    def update(k):
        here = EDGE * k
        rest = EDGE * (k + 1)
        below = dot_nt(lhs3(low_ref[rest:, here:rest]), rhs3(inv_ref[here:rest, :]))
        low_ref[rest:, here:rest] = below
        left = lhs3(below)
        right = rhs3(below)
        start = rest
        while start < width:
            stop = start + (2 * EDGE if (width - start) % (2 * EDGE) == 0 else EDGE)
            low_ref[start:, start:stop] -= dot_nt(
                left[start - rest :], right[start - rest : stop - rest]
            )
            start = stop

    def step(k, carry):
        at = pl.ds(pl.multiple_of(k * EDGE, EDGE), EDGE)
        upper, unit = factor_diag(low_ref[at, at], eye)
        pivots = jnp.sum(jnp.where(row == col, upper, 0.0), axis=1, keepdims=True)
        root = lax.rsqrt(pivots)
        low_ref[at, at] = (jnp.where(col >= row, upper, 0.0) * root).T
        inv_ref[at, :] = unit * root
        for static in range(blocks - 1):
            @pl.when(k == static)
            def _():
                update(static)
        return carry

    lax.fori_loop(0, blocks, step, 0)
    for i in range(blocks - 1):
        low_ref[EDGE * i : EDGE * (i + 1), EDGE * (i + 1) : EDGE * (i + 2)] = jnp.zeros((EDGE, EDGE), F32)


def gram_factor(tile_idx, mine, near, obs):
    steps, rows, pairs = mine.shape
    width = 2 * PANEL
    piece = pl.BlockSpec((1, rows, pairs), lambda i: (i, 0, 0))

    def body(*refs):
        factor_kernel(*refs, pairs_total=float(steps * pairs), obs=obs)

    return pl.pallas_call(
        body,
        grid=(steps,),
        in_specs=[pl.BlockSpec(memory_space=pltpu.SMEM), piece, piece],
        out_specs=[
            pl.BlockSpec((width, width), lambda i: (0, 0)),
            pl.BlockSpec((width, EDGE), lambda i: (0, 0)),
            pl.BlockSpec((8, EDGE), lambda i: (0, 0)),
        ],
        out_shape=[
            jax.ShapeDtypeStruct((width, width), F32),
            jax.ShapeDtypeStruct((width, EDGE), F32),
            jax.ShapeDtypeStruct((8, EDGE), F32),
        ],
        compiler_params=pltpu.CompilerParams(vmem_limit_bytes=48 * 2**20),
        name="gram_factor",
    )(tile_idx, mine, near)


def rows_kernel(
    info_ref, start_ref, enc_ref, mine_ref, near_ref, low_ref, inv_ref,
    chol_ref, white_ref, sums_ref, *, pairs_total,
):
    step = pl.program_id(0)
    own = chol_ref.shape[0]
    width = 2 * PANEL

    @pl.when(step == 0)
    def _():
        sums_ref[...] = jnp.zeros(sums_ref.shape, F32)

    snaps = enc_ref.shape[1]
    pairs = start_ref.shape[2]
    snap_idx = lax.broadcasted_iota(jnp.int32, (snaps, pairs), 0)
    starts = start_ref[0]
    first = jnp.where(snap_idx == starts, 1.0, 0.0).astype(BF16)
    second = jnp.where(snap_idx == starts + 1, 1.0, 0.0).astype(BF16)
    tn = (((0,), (0,)), ((), ()))
    picked = jnp.concatenate(
        [
            lax.dot_general(enc_ref[0], first, tn, preferred_element_type=F32),
            lax.dot_general(enc_ref[0], second, tn, preferred_element_type=F32),
        ],
        axis=0,
    ).astype(BF16)
    flip = info_ref[0] == 1
    mine = mine_ref[0, 0:PANEL, :]
    near = near_ref[0, 0:PANEL, :]
    sums_ref[:, 0:PANEL] += dot_nt(picked, jnp.where(flip, near, mine))
    sums_ref[:, PANEL:] += dot_nt(picked, jnp.where(flip, mine, near))

    @pl.when(step == pl.num_programs(0) - 1)
    def _():
        sums_ref[...] = sums_ref[...] * (1.0 / pairs_total)
        for k in range(width // EDGE):
            here = EDGE * k
            rest = EDGE * (k + 1)
            solved = dot_nt(lhs3(sums_ref[:, here:rest]), rhs3(inv_ref[here:rest, :]))
            sums_ref[:, here:rest] = solved
            if rest < width:
                sums_ref[:, rest:] -= dot_nt(lhs3(solved), rhs3(low_ref[rest:, here:rest]))
        offset = info_ref[3]
        first_rows = low_ref[pl.ds(pl.multiple_of(offset, 8), own), :]
        second_rows = low_ref[pl.ds(pl.multiple_of(PANEL + offset, 8), own), :]
        chol_ref[...] = jnp.where(
            info_ref[1] == 1,
            first_rows,
            jnp.where(info_ref[2] == 1, second_rows, sums_ref[0:own, :]),
        )
        white_ref[...] = sums_ref[own:, :]


def whiten_rows(info, starts, enc, mine, near, low, inv):
    steps, snaps, own = enc.shape
    pairs = mine.shape[2]
    width = 2 * PANEL
    piece = pl.BlockSpec((1, mine.shape[1], pairs), lambda i: (i, 0, 0))

    def body(*refs):
        rows_kernel(*refs, pairs_total=float(steps * pairs))

    return pl.pallas_call(
        body,
        grid=(steps,),
        in_specs=[
            pl.BlockSpec(memory_space=pltpu.SMEM),
            pl.BlockSpec((1, 1, pairs), lambda i: (i, 0, 0)),
            pl.BlockSpec((1, snaps, own), lambda i: (i, 0, 0)),
            piece,
            piece,
            pl.BlockSpec((width, width), lambda i: (0, 0)),
            pl.BlockSpec((width, EDGE), lambda i: (0, 0)),
        ],
        out_specs=[
            pl.BlockSpec((own, width), lambda i: (0, 0)),
            pl.BlockSpec((own, width), lambda i: (0, 0)),
        ],
        out_shape=[jax.ShapeDtypeStruct((own, width), F32)] * 2,
        scratch_shapes=[pltpu.VMEM((2 * own, width), F32)],
        compiler_params=pltpu.CompilerParams(vmem_limit_bytes=48 * 2**20),
        name="whiten_rows",
    )(info, starts, enc, mine, near, low, inv)


def on_device(
    snapshots, pair_start, bath_class, stencil_w, depth_gain, stencil_bias, readout, panel_order
):
    tile_pos = lax.axis_index("tile")
    dp_pos = lax.axis_index("dp")
    tile_count = lax.axis_size("tile")
    dp_count = lax.axis_size("dp")
    grid_rows, grid_cols = bath_class.shape
    tile_obs = grid_rows * grid_cols
    own_rows = tile_obs // dp_count
    swap = [(0, 1), (1, 0)]
    tile_idx = tile_pos[None].astype(jnp.int32)

    starts = lax.all_gather(pair_start, "dp", axis=0, tiled=False)[:, None, :]
    near_class = lax.ppermute(bath_class, "tile", swap)
    halo = lax.ppermute(halo_rows(tile_idx, snapshots), "tile", swap)
    encoded = encode(
        tile_idx, snapshots, halo, bath_class, near_class,
        stencil_w, depth_gain, stencil_bias, readout,
    )
    snaps = encoded.shape[1]

    block_rows = PANEL // grid_cols
    tile_blocks = tile_obs // PANEL

    def block_part(block):
        at = (block % tile_blocks) * block_rows
        part = lax.dynamic_slice_in_dim(encoded, at, block_rows, 0)
        return jnp.where(block // tile_blocks == tile_pos, part, jnp.zeros((), BF16))

    keep = block_part(jnp.where(tile_pos == 0, panel_order[0], panel_order[1]))
    send = block_part(jnp.where(tile_pos == 0, panel_order[1], panel_order[0]))
    picked = pick(pair_start[None, :], encoded, keep, lax.ppermute(send, "tile", swap))
    mine = lax.all_gather(picked, "dp", axis=0, tiled=False)
    near = lax.ppermute(mine, "tile", swap)

    by_owner = encoded
    if own_rows != grid_cols:
        by_owner = encoded.reshape(grid_rows, snaps, grid_cols // own_rows, own_rows)
        by_owner = by_owner.transpose(0, 2, 1, 3).reshape(dp_count, snaps, own_rows)
    own_enc = lax.all_to_all(by_owner, "dp", 0, 0, tiled=False)

    low, inv, shift = gram_factor(tile_idx, mine, near, tile_obs * tile_count)
    grow_start = tile_pos * tile_obs + dp_pos * own_rows
    own_block = grow_start // PANEL
    info = jnp.stack(
        [
            tile_pos,
            (own_block == panel_order[0]).astype(jnp.int32),
            (own_block == panel_order[1]).astype(jnp.int32),
            grow_start - own_block * PANEL,
        ]
    ).astype(jnp.int32)
    factor_rows, whitened = whiten_rows(info, starts, own_enc, mine, near, low, inv)
    return (factor_rows[None], whitened[None], shift[0, 0])


def solution(mesh):
    placed = (P("dp", None, "tile", None), P("dp"), P("tile", None), P(), P(), P(), P(), P())
    return jax.shard_map(
        on_device,
        mesh=mesh,
        in_specs=placed,
        out_specs=(P("tile", "dp", None), P("tile", "dp", None), P()),
        check_vma=False,
    )
```

time: 1670 us -> 455 us (0.27)
  matrix products: 575 us -> 0 us
  other arithmetic: 353 us -> 1.39 us
  waiting for transfers between devices: 467 us -> 120 us
  Pallas kernels: 0 us -> 230 us
  local copies, waits for them, and re-layouts: 186 us -> 7.01 us
  blocking collectives: 45.6 us -> 71 us
    conv_general_dilated x3 -> x0, matrix products: 512 us -> none  [layer_step(): lax.conv_general_dilated(padded_rows, kernel, (1, 1), ((0, 0), (1, 1)), d...]
    reduce_scatter x2 -> x0, waiting for transfers between devices: 300 us -> none  [the longest x1 178 us: on_device(): lax.psum_scatter(contract(later, panel, lax.axis_size('dp') * own_rows),...]
    another operation x34 -> x1, other arithmetic: 246 us -> 0.08 us  [on_device(): jnp.stack([tile_pos, (own_block == panel_order[0]).astype(jnp.int32), (ow...]
    pallas_call x0 -> x5, Pallas kernels: none -> 230 us  [the longest x1 162 us: gram_factor(): pl.pallas_call(body, grid=(steps,), in_specs=[pl.BlockSpec(memory_space=p...]
    psum x1 -> x0, waiting for transfers between devices: 148 us -> none  [on_device(): diag_rows = lax.psum(diag_part, ('dp', 'tile'))]
    all_gather x1, waiting for transfers between devices: 14 us -> 118 us  [on_device(): mine = lax.all_gather(picked, 'dp', axis=0, tiled=False)]
    all_gather x0 -> x1, blocking collectives: none -> 71 us  [on_device(): starts = lax.all_gather(pair_start, 'dp', axis=0, tiled=False)[:, None, :]]
    concatenate x3 -> x0, local copies, waits for them, and re-layouts: 62.9 us -> none  [extended(): block = jnp.concatenate([low, block, high], axis=dim)]
  transfers between devices with their start and end apart: 10 -> 6, of which waited for: 7 -> 2; matrix products, arithmetic and copies ran while one was open for 2% -> 1% of each run, Pallas kernels for 0% -> 36%
where the time goes in v1:
time: 455 us; the launch traced here: 452 us
  Pallas kernels  230 us (51%)
  waiting for transfers between devices  120 us (26%)
  blocking collectives  71 us (16%)
  between operations  17.9 us (4%)
  local copies, waits for them, and re-layouts  7.01 us (2%)
  starting transfers between devices  4.89 us (1%)
    pallas_call x1, Pallas kernels, gram_factor(): pl.pallas_call(body, grid=(steps,), in_specs=[pl.BlockSpec(memory_space=p...  162 us
    all_gather x1, waiting for transfers between devices, on_device(): mine = lax.all_gather(picked, 'dp', axis=0, tiled=False)  118 us
    all_gather x1, blocking collectives, on_device(): starts = lax.all_gather(pair_start, 'dp', axis=0, tiled=False)[:, None, :]  71 us
    pallas_call x1, Pallas kernels, encode(): pl.pallas_call(body, grid=(pl.cdiv(count, BLOCK),), in_specs=[smem, smem,...  32.8 us
    pallas_call x1, Pallas kernels, whiten_rows(): pl.pallas_call(body, grid=(steps,), in_specs=[pl.BlockSpec(memory_space=p...  22.9 us
  transfers between devices with their start and end apart: 6, of which 2 were waited for; matrix products, arithmetic and copies ran while one was open for 1% of the time, Pallas kernels for 36%

profile of v1, /device:TPU:0, one launch (start us, length us, event | category | flops | bytes accessed | tf_op | source)
XLA Modules:
  0.0 451.6 jit_solution(15000916518744263117)
XLA Ops:
  7.2 0.0 all-gather.5.cloned.1.call-start
  7.2 0.0 copy-start.4
  7.2 0.0 copy-start.8
  7.2 0.0 copy-start.6
  7.2 0.0 copy-start.7
  7.3 0.0 copy-start.3
  7.3 8.1 %halo_rows.1 = bf16[513,16,128]{2,1,0:T(8,128)(2,1)} custom-call(s32[1]{0:T(128)} %bitcast.tile_ref.refs_0_, bf16[513,3,16,128]{3,2,1,0:T(8,128)(2,1)} %refs_5_.1), custom_call_target="tpu_custom_call" | custom-call | tf_op jit(solution)/shard_map/halo_rows/pallas_call | solution.py:35
  15.3 0.5 collective-permute-start
  15.8 0.0 copy-done.4
  15.8 0.0 collective-permute-start.1
  15.8 0.0 copy-done.8
  15.8 0.6 fusion
  19.0 0.0 copy-done.6
  19.0 0.7 reshape.16.refs_2_
  19.6 0.0 copy-done.7
  19.6 0.7 reshape.17.refs_3_
  20.3 0.0 copy-done.3
  20.3 0.7 reshape.15.refs_1_
  21.0 0.0 collective-permute-done.1.refs_8_
  21.0 0.0 copy-start.5
  21.0 0.0 collective-permute-done.refs_6_
  21.0 0.6 copy-done.5
  21.6 0.0 copy-start.2
  21.6 1.3 copy-done.2
  22.9 32.8 %encode.1.enc_ref = bf16[16,544,128]{2,1,0:T(8,128)(2,1)} custom-call(s32[1]{0:T(128)} %bitcast.tile_ref.refs_0_, f32[243]{0:T(256)} %reshape.15.refs_1_, f32[12]{0:T(128)} %reshape.16.refs_2_, f32[9]{0:T(128)} %reshape.17.refs_3_, f32[3]{0:T(128)} %refs_4_.1, bf16[513,3,16,128]{3,2,1,0:T(8,128)(2,1)} %refs_5_.1, bf16[513,16,128]{2,1,0:T(8,128)(2,1)} %copy-done.2, ...), custom_call_target="tpu_custom_call" | custom-call | tf_op jit(solution)/shard_map/encode/pallas_call | solution.py:162
  55.8 0.0 copy-start.1
  55.8 1.3 dynamic-slice_select_fusion
  57.1 0.5 collective-permute-start.2
  57.6 1.6 collective-permute-done.2.near_ref
  59.2 0.0 copy-done.1
  59.2 3.8 pick_pairs.1
  63.0 0.0 all-gather.5.cloned.1.call-update
  63.0 118.2 %all-gather.5.cloned.1.call-done = bf16[8448,512]{1,0:T(8,128)(2,1)} async-done(((bf16[528,512]{1,0:T(8,128)(2,1)}), bf16[8448,512]{1,0:T(8,128)(2,1)}) %all-gather.5.cloned.1.call-update) | async-done | bytes 8650768 | tf_op jit(solution)/shard_map/all_gather | solution.py:492
  181.2 0.0 collective-permute-start.3
  181.2 3.8 all-to-all-start
  186.3 71.0 %all-gather.2.refs_1_ = s32[16,1,512]{2,1,0:T(1,128)S(1)} all-gather(s32[1,1,512]{2,1,0:T(1,128)S(1)} %bitcast.13), channel_id=2, replica_groups=mesh['dp'=16,'tile'=2] {'dp'}, dimensions={0}, use_global_device_ids=true | all-gather | bytes 34816 | tf_op jit(solution)/shard_map/all_gather | solution.py:472
  257.3 0.1 pad_add_fusion.refs_0_
  257.3 0.0 collective-permute-done.3.refs_2_.refs_4_
  257.3 162.0 %gram_factor.1 = (f32[1024,1024]{1,0:T(8,128)S(1)}, f32[1024,128]{1,0:T(8,128)S(1)}, f32[8,128]{1,0:T(8,128)S(1)}) custom-call(s32[1]{0:T(128)} %bitcast.tile_ref.refs_0_, bf16[16,528,512]{2,1,0:T(8,128)(2,1)} %bitcast.15, bf16[16,528,512]{2,1,0:T(8,128)(2,1)} %collective-permute-done.3.refs_2_.refs_4_), custom_call_target="tpu_custom_call" | custom-call | tf_op jit(solution)/shard_map/gram_factor/pallas_call | solution.py:355
  419.4 0.0 copy-start
  419.4 2.0 copy-done
  421.4 0.5 slice.15
  421.9 0.0 all-to-all-done.refs_2_
  421.9 22.9 %whiten_rows.1 = (f32[128,1024]{1,0:T(8,128)}, f32[128,1024]{1,0:T(8,128)}) custom-call(s32[4]{0:T(128)S(1)} %pad_add_fusion.refs_0_, s32[16,1,512]{2,1,0:T(1,128)S(1)} %all-gather.2.refs_1_, bf16[16,544,128]{2,1,0:T(8,128)(2,1)S(1)} %all-to-all-done.refs_2_, bf16[16,528,512]{2,1,0:T(8,128)(2,1)} %bitcast.16, ...), custom_call_target="tpu_custom_call" | custom-call | tf_op jit(solution)/shard_map/whiten_rows/pallas_call | solution.py:436
Async XLA Ops:
  7.2 174.0 %all-gather.5.cloned.1.call-start = ((), (), s32[]{:S(2)}) async-start(), calls=%async_computation.1 | async-start | bytes 9191424 | tf_op jit(solution)/shard_map/all_gather | solution.py:492
  7.2 8.6 %copy-start.4 = (s32[16,128]{1,0:T(8,128)S(1)}, s32[16,128]{1,0:T(8,128)}, u32[]{:S(2)}) copy-start(s32[16,128]{1,0:T(8,128)} %refs_7_.1) | copy-start | bytes 24580
  7.2 8.6 %copy-start.8 = (s32[8]{0:T(128)S(1)}, s32[8]{0:T(128)}, u32[]{:S(2)}) copy-start(s32[8]{0:T(128)} %param.15) | copy-start | bytes 100
  7.2 11.7 %copy-start.6 = (f32[3,4]{1,0:T(4,128)S(1)}, f32[3,4]{1,0:T(4,128)}, u32[]{:S(2)}) copy-start(f32[3,4]{1,0:T(4,128)} %param.12) | copy-start | bytes 148
  7.2 12.4 %copy-start.7 = (f32[3,3]{1,0:T(4,128)S(1)}, f32[3,3]{1,0:T(4,128)}, u32[]{:S(2)}) copy-start(f32[3,3]{1,0:T(4,128)} %param.13) | copy-start | bytes 112
  7.3 13.1 %copy-start.3 = (f32[3,3,3,9]{3,2,1,0:T(4,128)S(1)}, f32[3,3,3,9]{3,2,1,0:T(4,128)}, u32[]{:S(2)}) copy-start(f32[3,3,3,9]{3,2,1,0:T(4,128)} %param.11) | copy-start | bytes 2920
  15.3 5.7 %collective-permute-start = (bf16[513,16,128]{2,1,0:T(8,128)(2,1)}, bf16[513,16,128]{2,1,0:T(8,128)(2,1)S(1)}, u32[]{:S(2)}, u32[]{:S(2)}) collective-permute-start(bf16[513,16,128]{2,1,0:T(8,128)(2,1)} %halo_rows.1), channel_id=1, source_target_pairs={{0,1},{1,0},{2,3},{3,2},{4,5},{5,4},{6,7},{7,6},{8,9},{9,8},{10,11... | collective-permute-start | bytes 6303752 | tf_op jit(solution)/shard_map/ppermute | solution.py:474
  15.8 5.2 %collective-permute-start.1 = (s32[16,128]{1,0:T(8,128)S(1)}, s32[16,128]{1,0:T(8,128)S(1)}, u32[]{:S(2)}, u32[]{:S(2)}) collective-permute-start(s32[16,128]{1,0:T(8,128)S(1)} %copy-done.4), channel_id=1, source_target_pairs={{0,1},{1,0},{2,3},{3,2},{4,5},{5,4},{6,7},{7,6},{8,9},{9,8},{10,11... | collective-permute-start | bytes 24584 | tf_op jit(solution)/shard_map/ppermute | solution.py:473
  21.0 0.6 copy-start.5
  21.6 1.3 copy-start.2
  55.8 3.4 copy-start.1
  57.1 2.1 collective-permute-start.2
  181.2 76.1 %collective-permute-start.3 = (bf16[16,528,512]{2,1,0:T(8,128)(2,1)}, bf16[16,528,512]{2,1,0:T(8,128)(2,1)}, u32[]{:S(2)}, u32[]{:S(2)}) collective-permute-start(bf16[16,528,512]{2,1,0:T(8,128)(2,1)} %bitcast.14), channel_id=1, source_target_pairs={{0,1},{1,0},{2,3},{3,2},{4,5},{5,4},{6,7},{7,6},{8,9},{9,8},{10,11... | collective-permute-start | bytes 25952264 | tf_op jit(solution)/shard_map/ppermute | solution.py:493
  181.2 240.7 %all-to-all-start = ((bf16[16,544,128]{2,1,0:T(8,128)(2,1)}), bf16[16,544,128]{2,1,0:T(8,128)(2,1)S(1)}, u32[]{:S(2)}, u32[]{:S(2)}) async-start(bf16[16,544,128]{2,1,0:T(8,128)(2,1)} %encode.1.enc_ref), calls=%async_computation | async-start | bytes 4456448 | tf_op jit(solution)/shard_map/all_to_all | solution.py:499
  419.4 2.0 copy-start
Sparse Core Ops, SparseCore 0:
  63.2 117.9 all-gather.4

commit v2 on v1

--- a/solution.py
+++ b/solution.py
@@ -11,6 +11,7 @@
 
 EDGE = 128
 PANEL = 512
+HALF = PANEL // 2
 
 
 def halo_kernel(tile_ref, own_ref, out_ref):
@@ -207,25 +208,56 @@
     groups = EDGE // 8
     a = [block[8 * g : 8 * (g + 1)] for g in range(groups)]
     b = [eye[8 * g : 8 * (g + 1)] for g in range(groups)]
-    for j in range(EDGE):
-        home, inner = divmod(j, 8)
-        row = jnp.broadcast_to(a[home][inner : inner + 1, :], (8, EDGE))
-        pivot = jnp.broadcast_to(row[:, j : j + 1], (8, EDGE))
-        invert = 1.0 / pivot
-        scaled = row * invert
-        brow = jnp.broadcast_to(b[home][inner : inner + 1, :], (8, EDGE)) * invert
-        for g in range(home, groups):
-            if g == home and inner == 7:
-                continue
-            col = jnp.broadcast_to(a[g][:, j : j + 1], (8, EDGE))
-            if g == home:
-                col = jnp.where(row8 > inner, col, 0.0)
-            a[g] = a[g] - col * scaled
-            b[g] = b[g] - col * brow
+
+    def lanes(x, j):
+        return jnp.broadcast_to(x[:, j : j + 1], (8, EDGE))
+
+    def sublanes(x, i):
+        return jnp.broadcast_to(x[i : i + 1, :], (8, EDGE))
+
+    for home in range(groups):
+        at = 8 * home
+        cols = [lanes(a[home], at + k) for k in range(8)]
+        e = [[sublanes(cols[k], i) for k in range(i + 1)] for i in range(8)]
+        invert = []
+        mult = [[None] * 8 for _ in range(8)]
+        for k in range(8):
+            invert.append(1.0 / e[k][k])
+            for i in range(k + 1, 8):
+                mult[i][k] = e[i][k] * invert[k]
+            for i in range(k + 1, 8):
+                for j in range(k + 1, i + 1):
+                    e[i][j] = e[i][j] - mult[i][k] * e[j][k]
+
+        def forward(rows):
+            for k in range(8):
+                for m in range(k):
+                    rows[k] = rows[k] - mult[k][m] * rows[m]
+            return rows
+
+        def pack(rows):
+            out = rows[0]
+            for k in range(1, 8):
+                out = jnp.where(row8 == k, rows[k], out)
+            return out
+
+        u = forward([sublanes(a[home], k) for k in range(8)])
+        v = forward([sublanes(b[home], k) for k in range(8)])
+        a[home] = pack(u)
+        b[home] = pack(v)
+        if home + 1 == groups:
+            break
+        us = [u[k] * invert[k] for k in range(8)]
+        vs = [v[k] * invert[k] for k in range(8)]
+        for g in range(home + 1, groups):
+            c = forward([lanes(a[g], at + k) for k in range(8)])
+            for k in range(8):
+                a[g] = a[g] - c[k] * us[k]
+                b[g] = b[g] - c[k] * vs[k]
     return jnp.concatenate(a, axis=0), jnp.concatenate(b, axis=0)
 
 
-def pick_kernel(start_ref, enc_ref, keep_ref, near_ref, out_ref):
+def pick_kernel(start_ref, enc_ref, keep_ref, near_ref, top_ref, bottom_ref):
     snaps = enc_ref.shape[1]
     pairs = start_ref.shape[1]
     snap_idx = lax.broadcasted_iota(jnp.int32, (snaps, pairs), 0)
@@ -234,9 +266,9 @@
         [keep_ref[r] + near_ref[r] for r in range(keep_ref.shape[0])], axis=1
     )
     tn = (((0,), (0,)), ((), ()))
-    out_ref[0:PANEL, :] = lax.dot_general(
-        panel, hit, tn, preferred_element_type=F32
-    ).astype(BF16)
+    chosen = lax.dot_general(panel, hit, tn, preferred_element_type=F32).astype(BF16)
+    top_ref[...] = chosen[0:HALF]
+    bottom_ref[0:HALF, :] = chosen[HALF:]
     norms = jnp.zeros(enc_ref.shape[1:], F32)
     for r in range(enc_ref.shape[0]):
         value = enc_ref[r].astype(F32)
@@ -254,42 +286,74 @@
         high = rest.astype(BF16)
         packed = jnp.where(row == k, high.astype(F32), packed.astype(F32)).astype(BF16)
         rest = rest - high.astype(F32)
-    out_ref[PANEL:, :] = packed
+    starts = start_ref[...]
+    coarse = lax.shift_right_logical(starts, 2)
+    for k, value in ((3, coarse), (4, starts - 4 * coarse)):
+        packed = jnp.where(row == k, value.astype(F32), packed.astype(F32)).astype(BF16)
+    bottom_ref[HALF:, :] = packed
 
 
 def pick(starts, enc, keep, near):
     pairs = starts.shape[1]
     return pl.pallas_call(
         pick_kernel,
-        out_shape=jax.ShapeDtypeStruct((PANEL + 16, pairs), BF16),
+        out_shape=[
+            jax.ShapeDtypeStruct((HALF, pairs), BF16),
+            jax.ShapeDtypeStruct((HALF + 16, pairs), BF16),
+        ],
         compiler_params=pltpu.CompilerParams(vmem_limit_bytes=40 * 2**20),
         name="pick_pairs",
     )(starts, enc, keep, near)
 
 
-def factor_kernel(tile_ref, mine_ref, near_ref, low_ref, inv_ref, shift_ref, *, pairs_total, obs):
-    step = pl.program_id(0)
-    width = 2 * PANEL
-
-    @pl.when(step == 0)
-    def _():
-        low_ref[...] = jnp.zeros((width, width), F32)
-        shift_ref[...] = jnp.zeros(shift_ref.shape, F32)
-
+def blocks_of(flip, refs):
+    top, bottom, near_top, near_bottom = refs
+    mine = jnp.concatenate([top[0], bottom[0, 0:HALF, :]], axis=0)
+    near = jnp.concatenate([near_top[0], near_bottom[0, 0:HALF, :]], axis=0)
+    return jnp.where(flip, near, mine), jnp.where(flip, mine, near)
+
+
+def gram_step(tile_ref, pieces, low_ref, power_ref):
     flip = tile_ref[0] == 1
-    mine = mine_ref[0, 0:PANEL, :]
-    near = near_ref[0, 0:PANEL, :]
-    lead = jnp.where(flip, near, mine)
-    tail = jnp.where(flip, mine, near)
+    pairs = [blocks_of(flip, refs) for refs in pieces]
+    lead = jnp.concatenate([pair[0] for pair in pairs], axis=1)
+    tail = jnp.concatenate([pair[1] for pair in pairs], axis=1)
     low_ref[0:PANEL, 0:PANEL] += dot_nt(lead, lead)
     low_ref[PANEL:, 0:PANEL] += dot_nt(tail, lead)
     low_ref[PANEL:, PANEL:] += dot_nt(tail, tail)
-    parts = mine_ref[0, PANEL:, 0:128].astype(F32) + 0.0
-    parts_near = near_ref[0, PANEL:, 0:128].astype(F32) + 0.0
-    both = jnp.sum(parts, axis=0, keepdims=True) + jnp.sum(parts_near, axis=0, keepdims=True)
-    shift_ref[...] += jnp.broadcast_to(both, shift_ref.shape)
-
-    @pl.when(step == pl.num_programs(0) - 1)
+    for refs in pieces:
+        for ref in (refs[1], refs[3]):
+            part = ref[0, HALF:, 0:EDGE].astype(F32)
+            part = part[0:1] + part[1:2] + part[2:3]
+            power_ref[...] += jnp.broadcast_to(part, power_ref.shape)
+
+
+def grouped(refs):
+    return [refs[4 * k : 4 * (k + 1)] for k in range(len(refs) // 4)]
+
+
+def gram_kernel(tile_ref, *refs):
+    pieces, (low_ref, power_ref) = refs[:-2], refs[-2:]
+
+    @pl.when(pl.program_id(0) == 0)
+    def _():
+        low_ref[...] = jnp.zeros(low_ref.shape, F32)
+        power_ref[...] = jnp.zeros(power_ref.shape, F32)
+
+    gram_step(tile_ref, grouped(pieces), low_ref, power_ref)
+
+
+def factor_kernel(tile_ref, sums_ref, energy_ref, *refs, pairs_total, obs):
+    pieces, (low_ref, inv_ref, shift_ref) = refs[:-3], refs[-3:]
+
+    @pl.when(pl.program_id(0) == 0)
+    def _():
+        low_ref[...] = sums_ref[...]
+        shift_ref[...] = energy_ref[...]
+
+    gram_step(tile_ref, grouped(pieces), low_ref, shift_ref)
+
+    @pl.when(pl.program_id(0) == pl.num_programs(0) - 1)
     def _():
         shift = 0.5 * (shift_ref[...] / pairs_total) / float(obs)
         shift_ref[...] = shift
@@ -344,37 +408,54 @@
         low_ref[EDGE * i : EDGE * (i + 1), EDGE * (i + 1) : EDGE * (i + 2)] = jnp.zeros((EDGE, EDGE), F32)
 
 
-def gram_factor(tile_idx, mine, near, obs):
-    steps, rows, pairs = mine.shape
-    width = 2 * PANEL
-    piece = pl.BlockSpec((1, rows, pairs), lambda i: (i, 0, 0))
-
+def whole(shape):
+    return pl.BlockSpec(shape, lambda i: (0,) * len(shape))
+
+
+def piece_specs(pieces):
+    return [pl.BlockSpec((1,) + piece.shape[1:], lambda i: (i, 0, 0)) for piece in pieces]
+
+
+SUMS = jax.ShapeDtypeStruct((2 * PANEL, 2 * PANEL), F32)
+POWER = jax.ShapeDtypeStruct((8, EDGE), F32)
+LIMIT = pltpu.CompilerParams(vmem_limit_bytes=56 * 2**20)
+
+
+def gram_part(tile_idx, pieces):
+    return pl.pallas_call(
+        gram_kernel,
+        grid=(pieces[0].shape[0],),
+        in_specs=[pl.BlockSpec(memory_space=pltpu.SMEM)] + piece_specs(pieces),
+        out_specs=[whole(SUMS.shape), whole(POWER.shape)],
+        out_shape=[SUMS, POWER],
+        compiler_params=LIMIT,
+        cost_estimate=pl.CostEstimate(
+            flops=6 * PANEL**2 * 4 * pieces[0].shape[0] * PANEL,
+            transcendentals=0,
+            bytes_accessed=sum(2 * x.size for x in pieces) + 4 * SUMS.size,
+        ),
+        name="gram_part",
+    )(tile_idx, *pieces)
+
+
+def gram_factor(tile_idx, sums, energy, pieces, pairs_total, obs):
     def body(*refs):
-        factor_kernel(*refs, pairs_total=float(steps * pairs), obs=obs)
+        factor_kernel(*refs, pairs_total=pairs_total, obs=obs)
 
     return pl.pallas_call(
         body,
-        grid=(steps,),
-        in_specs=[pl.BlockSpec(memory_space=pltpu.SMEM), piece, piece],
-        out_specs=[
-            pl.BlockSpec((width, width), lambda i: (0, 0)),
-            pl.BlockSpec((width, EDGE), lambda i: (0, 0)),
-            pl.BlockSpec((8, EDGE), lambda i: (0, 0)),
-        ],
-        out_shape=[
-            jax.ShapeDtypeStruct((width, width), F32),
-            jax.ShapeDtypeStruct((width, EDGE), F32),
-            jax.ShapeDtypeStruct((8, EDGE), F32),
-        ],
-        compiler_params=pltpu.CompilerParams(vmem_limit_bytes=48 * 2**20),
+        grid=(pieces[0].shape[0],),
+        in_specs=[pl.BlockSpec(memory_space=pltpu.SMEM), whole(SUMS.shape), whole(POWER.shape)]
+        + piece_specs(pieces),
+        out_specs=[whole(SUMS.shape), whole((2 * PANEL, EDGE)), whole(POWER.shape)],
+        out_shape=[SUMS, jax.ShapeDtypeStruct((2 * PANEL, EDGE), F32), POWER],
+        compiler_params=LIMIT,
         name="gram_factor",
-    )(tile_idx, mine, near)
-
-
-def rows_kernel(
-    info_ref, start_ref, enc_ref, mine_ref, near_ref, low_ref, inv_ref,
-    chol_ref, white_ref, sums_ref, *, pairs_total,
-):
+    )(tile_idx, sums, energy, *pieces)
+
+
+def rows_kernel(info_ref, enc_ref, low_ref, inv_ref, *refs, pairs_total):
+    pieces, (chol_ref, white_ref, sums_ref) = refs[:-3], refs[-3:]
     step = pl.program_id(0)
     own = chol_ref.shape[0]
     width = 2 * PANEL
@@ -384,24 +465,33 @@
         sums_ref[...] = jnp.zeros(sums_ref.shape, F32)
 
     snaps = enc_ref.shape[1]
-    pairs = start_ref.shape[2]
+    pairs = pieces[0].shape[2]
     snap_idx = lax.broadcasted_iota(jnp.int32, (snaps, pairs), 0)
-    starts = start_ref[0]
-    first = jnp.where(snap_idx == starts, 1.0, 0.0).astype(BF16)
-    second = jnp.where(snap_idx == starts + 1, 1.0, 0.0).astype(BF16)
     tn = (((0,), (0,)), ((), ()))
-    picked = jnp.concatenate(
-        [
-            lax.dot_general(enc_ref[0], first, tn, preferred_element_type=F32),
-            lax.dot_general(enc_ref[0], second, tn, preferred_element_type=F32),
-        ],
-        axis=0,
-    ).astype(BF16)
     flip = info_ref[0] == 1
-    mine = mine_ref[0, 0:PANEL, :]
-    near = near_ref[0, 0:PANEL, :]
-    sums_ref[:, 0:PANEL] += dot_nt(picked, jnp.where(flip, near, mine))
-    sums_ref[:, PANEL:] += dot_nt(picked, jnp.where(flip, mine, near))
+    top_bit = enc_ref.shape[0] // 2
+    parts = grouped(pieces)
+    picked = []
+    for k in range(len(parts)):
+        source = jnp.bitwise_xor(info_ref[4], (k // 4) * top_bit + step * 4 + k % 4)
+        values = enc_ref[source]
+        packed = parts[k][1][0, HALF:, :].astype(F32)
+        starts = (4.0 * packed[3:4] + packed[4:5]).astype(jnp.int32)
+        first = jnp.where(snap_idx == starts, 1.0, 0.0).astype(BF16)
+        second = jnp.where(snap_idx == starts + 1, 1.0, 0.0).astype(BF16)
+        picked.append(
+            jnp.concatenate(
+                [
+                    lax.dot_general(values, first, tn, preferred_element_type=F32),
+                    lax.dot_general(values, second, tn, preferred_element_type=F32),
+                ],
+                axis=0,
+            ).astype(BF16)
+        )
+    both = [blocks_of(flip, part) for part in parts]
+    picked = jnp.concatenate(picked, axis=1)
+    sums_ref[:, 0:PANEL] += dot_nt(picked, jnp.concatenate([b[0] for b in both], axis=1))
+    sums_ref[:, PANEL:] += dot_nt(picked, jnp.concatenate([b[1] for b in both], axis=1))
 
     @pl.when(step == pl.num_programs(0) - 1)
     def _():
@@ -424,36 +514,74 @@
         white_ref[...] = sums_ref[own:, :]
 
 
-def whiten_rows(info, starts, enc, mine, near, low, inv):
-    steps, snaps, own = enc.shape
-    pairs = mine.shape[2]
+def whiten_rows(info, enc, low, inv, pieces, pairs_total):
+    own = enc.shape[2]
     width = 2 * PANEL
-    piece = pl.BlockSpec((1, mine.shape[1], pairs), lambda i: (i, 0, 0))
 
     def body(*refs):
-        rows_kernel(*refs, pairs_total=float(steps * pairs))
+        rows_kernel(*refs, pairs_total=pairs_total)
 
     return pl.pallas_call(
         body,
-        grid=(steps,),
-        in_specs=[
-            pl.BlockSpec(memory_space=pltpu.SMEM),
-            pl.BlockSpec((1, 1, pairs), lambda i: (i, 0, 0)),
-            pl.BlockSpec((1, snaps, own), lambda i: (i, 0, 0)),
-            piece,
-            piece,
-            pl.BlockSpec((width, width), lambda i: (0, 0)),
-            pl.BlockSpec((width, EDGE), lambda i: (0, 0)),
-        ],
-        out_specs=[
-            pl.BlockSpec((own, width), lambda i: (0, 0)),
-            pl.BlockSpec((own, width), lambda i: (0, 0)),
-        ],
+        grid=(pieces[0].shape[0],),
+        in_specs=[pl.BlockSpec(memory_space=pltpu.SMEM)]
+        + [whole(x.shape) for x in (enc, low, inv)]
+        + piece_specs(pieces),
+        out_specs=[whole((own, width))] * 2,
         out_shape=[jax.ShapeDtypeStruct((own, width), F32)] * 2,
         scratch_shapes=[pltpu.VMEM((2 * own, width), F32)],
-        compiler_params=pltpu.CompilerParams(vmem_limit_bytes=48 * 2**20),
+        compiler_params=LIMIT,
         name="whiten_rows",
-    )(info, starts, enc, mine, near, low, inv)
+    )(info, enc, low, inv, *pieces)
+
+
+def after_kernel(value_ref, *refs):
+    del value_ref, refs
+
+
+def after(value, *earlier):
+    hbm = pl.BlockSpec(memory_space=pl.ANY)
+    return pl.pallas_call(
+        after_kernel,
+        in_specs=[hbm] * (1 + len(earlier)),
+        out_specs=hbm,
+        out_shape=jax.ShapeDtypeStruct(value.shape, value.dtype),
+        input_output_aliases={0: 0},
+        name="after",
+    )(value, *earlier)
+
+
+def gather_pieces(parts, dp_count, swap, tile_idx):
+    def across(arrays, bit):
+        pairs = [(i, i ^ bit) for i in range(dp_count)]
+        return [lax.ppermute(x, "dp", pairs) for x in arrays]
+
+    top_bit = dp_count // 2
+    chunks = []
+    sums = None
+    for start in (parts, across(parts, top_bit)):
+        bit = 4
+        while bit < top_bit:
+            far = across(start, bit)
+            start = [jnp.concatenate(pair, axis=0) for pair in zip(start, far)]
+            bit *= 2
+        top, bottom = start
+        (top_x,) = across([top], 1)
+        (bottom_y,) = across([bottom], 2)
+        (top_y,) = across([top], 2)
+        (bottom_x,) = across([bottom], 1)
+        (top_xy,) = across([top_x], 2)
+        (bottom_xy,) = across([bottom_y], 1)
+        if sums is not None:
+            top_xy = after(top_xy, *sums)
+        pieces = []
+        for pair in ((top, bottom), (top_x, bottom_x), (top_y, bottom_y), (top_xy, bottom_xy)):
+            pieces.extend(pair)
+            pieces.extend(lax.ppermute(x, "tile", swap) for x in pair)
+        chunks.append(pieces)
+        if sums is None:
+            sums = gram_part(tile_idx, pieces)
+    return chunks, sums
 
 
 def on_device(
@@ -469,7 +597,6 @@
     swap = [(0, 1), (1, 0)]
     tile_idx = tile_pos[None].astype(jnp.int32)
 
-    starts = lax.all_gather(pair_start, "dp", axis=0, tiled=False)[:, None, :]
     near_class = lax.ppermute(bath_class, "tile", swap)
     halo = lax.ppermute(halo_rows(tile_idx, snapshots), "tile", swap)
     encoded = encode(
@@ -488,17 +615,20 @@
 
     keep = block_part(jnp.where(tile_pos == 0, panel_order[0], panel_order[1]))
     send = block_part(jnp.where(tile_pos == 0, panel_order[1], panel_order[0]))
-    picked = pick(pair_start[None, :], encoded, keep, lax.ppermute(send, "tile", swap))
-    mine = lax.all_gather(picked, "dp", axis=0, tiled=False)
-    near = lax.ppermute(mine, "tile", swap)
+    own_parts = pick(pair_start[None, :], encoded, keep, lax.ppermute(send, "tile", swap))
+    chunks, sums = gather_pieces([part[None] for part in own_parts], dp_count, swap, tile_idx)
 
     by_owner = encoded
     if own_rows != grid_cols:
         by_owner = encoded.reshape(grid_rows, snaps, grid_cols // own_rows, own_rows)
         by_owner = by_owner.transpose(0, 2, 1, 3).reshape(dp_count, snaps, own_rows)
+    by_owner = after(by_owner, *chunks[0], *chunks[1])
     own_enc = lax.all_to_all(by_owner, "dp", 0, 0, tiled=False)
 
-    low, inv, shift = gram_factor(tile_idx, mine, near, tile_obs * tile_count)
+    pairs_total = float(pair_start.shape[0] * dp_count)
+    low, inv, shift = gram_factor(
+        tile_idx, *sums, chunks[1], pairs_total, tile_obs * tile_count
+    )
     grow_start = tile_pos * tile_obs + dp_pos * own_rows
     own_block = grow_start // PANEL
     info = jnp.stack(
@@ -507,9 +637,12 @@
             (own_block == panel_order[0]).astype(jnp.int32),
             (own_block == panel_order[1]).astype(jnp.int32),
             grow_start - own_block * PANEL,
+            dp_pos,
         ]
     ).astype(jnp.int32)
-    factor_rows, whitened = whiten_rows(info, starts, own_enc, mine, near, low, inv)
+    factor_rows, whitened = whiten_rows(
+        info, own_enc, low, inv, chunks[0] + chunks[1], pairs_total
+    )
     return (factor_rows[None], whitened[None], shift[0, 0])
 
 

time: 455 us -> 257 us (0.56)
  Pallas kernels: 230 us -> 125 us
  blocking collectives: 71 us -> 0 us
  waiting for transfers between devices: 120 us -> 80.4 us
  starting transfers between devices: 4.89 us -> 33.8 us
  between operations: 17.9 us -> 5.09 us
    all_gather x1 -> x0, waiting for transfers between devices: 118 us -> none  [on_device(): mine = lax.all_gather(picked, 'dp', axis=0, tiled=False)]
    pallas_call x3 -> x6, Pallas kernels: 189 us -> 84.3 us  [the longest x1 52.4 us: gram_factor(): pl.pallas_call(body, grid=(pieces[0].shape[0],), in_specs=[pl.BlockSpec(m...]
    ppermute x1 -> x34, waiting for transfers between devices: 0.01 us -> 78.8 us  [the longest x18 76.6 us: across(): return [lax.ppermute(x, 'dp', pairs) for x in arrays]]
    all_gather x1 -> x0, blocking collectives: 71 us -> none  [on_device(): starts = lax.all_gather(pair_start, 'dp', axis=0, tiled=False)[:, None, :]]
    ppermute x1 -> x34, starting transfers between devices: 0.01 us -> 27 us  [the longest x18 24.1 us: across(): return [lax.ppermute(x, 'dp', pairs) for x in arrays]]
  transfers between devices with their start and end apart: 6 -> 38, of which waited for: 2 -> 12; matrix products, arithmetic and copies ran while one was open for 1% -> 2% of each run, Pallas kernels for 36% -> 25%
where the time goes in v2:
time: 257 us
  Pallas kernels  125 us (49%)
  waiting for transfers between devices  80.4 us (31%)
  starting transfers between devices  33.8 us (13%)
  local copies, waits for them, and re-layouts  10.5 us (4%)
  between operations  5.09 us (2%)
    ppermute x18, waiting for transfers between devices, across(): return [lax.ppermute(x, 'dp', pairs) for x in arrays]  76.6 us
    pallas_call x1, Pallas kernels, gram_factor(): pl.pallas_call(body, grid=(pieces[0].shape[0],), in_specs=[pl.BlockSpec(m...  52.4 us
    pallas_call x1, Pallas kernels, encode(): pl.pallas_call(body, grid=(pl.cdiv(count, BLOCK),), in_specs=[smem, smem,...  32.9 us
    ppermute x18, starting transfers between devices, across(): return [lax.ppermute(x, 'dp', pairs) for x in arrays]  24.1 us
    pallas_call x1, Pallas kernels, whiten_rows(): pl.pallas_call(body, grid=(pieces[0].shape[0],), in_specs=[pl.BlockSpec(m...  19.1 us
    pallas_call x1, Pallas kernels, gram_part(): pl.pallas_call(gram_kernel, grid=(pieces[0].shape[0],), in_specs=[pl.Bloc...  11.5 us
    pallas_call x1, Pallas kernels, halo_rows(): pl.pallas_call(halo_kernel, grid=(count // block,), in_specs=[pl.BlockSpe...  8.11 us
    unnamed x72, local copies, waits for them, and re-layouts  6.04 us
  transfers between devices with their start and end apart: 38, of which 12 were waited for; matrix products, arithmetic and copies ran while one was open for 2% of the time, Pallas kernels for 25%

profile of v2, /device:TPU:0, one launch (start us, length us, event | category | flops | bytes accessed | tf_op | source)
XLA Modules:
  0.0 256.6 jit_solution(12769956454317902477)
XLA Ops:
  0.7 8.1 %halo_rows.1 = bf16[513,16,128]{2,1,0:T(8,128)(2,1)} custom-call(s32[1]{0:T(128)} %bitcast.tile_ref.refs_0_, bf16[513,3,16,128]{3,2,1,0:T(8,128)(2,1)} %refs_5_.1), custom_call_target="tpu_custom_call" | custom-call | tf_op jit(solution)/shard_map/halo_rows/pallas_call | solution.py:36
  8.8 0.4 collective-permute-start
  9.3 0.1 collective-permute-start.1
  9.3 0.6 fusion
  12.5 0.7 reshape.16.refs_2_
  13.2 0.7 reshape.17.refs_3_
  13.9 0.7 reshape.15.refs_1_
  14.5 0.6 copy-done.31
  15.1 1.3 copy-done.21
  16.4 32.9 %encode.1.enc_ref.value_ref = bf16[16,544,128]{2,1,0:T(8,128)(2,1)} custom-call(s32[1]{0:T(128)} %bitcast.tile_ref.refs_0_, f32[243]{0:T(256)} %reshape.15.refs_1_, f32[12]{0:T(128)} %reshape.16.refs_2_, f32[9]{0:T(128)} %reshape.17.refs_3_, f32[3]{0:T(128)} %refs_4_.1, bf16[513,3,16,128]{3,2,1,0:T(8,128)(2,1)} %refs_5_.1, bf16[513,16,128]{2,1,0:T(8,128)(2,1)} %copy-done.21, ...), custom_call_target="tpu_custom_call" | custom-call | tf_op jit(solution)/shard_map/encode/pallas_call | solution.py:163
  49.3 1.5 dynamic-slice_select_fusion
  50.8 0.5 collective-permute-start.2
  51.3 1.6 collective-permute-done.2.near_ref
  52.9 1.4 pick_pairs.1
  54.2 3.0 %collective-permute-start.3 = (bf16[1,256,512]{2,1,0:T(8,128)(2,1)S(1)}, bf16[1,256,512]{2,1,0:T(8,128)(2,1)S(1)}, u32[]{:S(2)}, u32[]{:S(2)}) collective-permute-start(bf16[1,256,512]{2,1,0:T(8,128)(2,1)S(1)} %bitcast.16), channel_id=1, source_target_pairs={{0,8},{2,10},{4,12},{6,14},{8,0},{10,2},{12,4},{14,6},{16,24},{18,... | collective-permute-start | bytes 786440 | tf_op jit(solution)/shard_map/ppermute | solution.py:557
  57.2 2.6 %collective-permute-start.19 = (bf16[1,256,512]{2,1,0:T(8,128)(2,1)S(1)}, bf16[1,256,512]{2,1,0:T(8,128)(2,1)S(1)}, u32[]{:S(2)}, u32[]{:S(2)}) collective-permute-start(bf16[1,256,512]{2,1,0:T(8,128)(2,1)S(1)} %bitcast.17), channel_id=1, source_target_pairs={{0,16},{2,18},{4,20},{6,22},{8,24},{10,26},{12,28},{14,30},{16,0},... | collective-permute-start | bytes 786440 | tf_op jit(solution)/shard_map/ppermute | solution.py:557
  59.8 0.3 collective-permute-start.21
  60.1 9.1 %collective-permute-done.3 = bf16[1,256,512]{2,1,0:T(8,128)(2,1)S(1)} collective-permute-done((bf16[1,256,512]{2,1,0:T(8,128)(2,1)S(1)}, bf16[1,256,512]{2,1,0:T(8,128)(2,1)S(1)}, u32[]{:S(2)}, u32[]{:S(2)}) %collective-permute-start.3) | collective-permute-done | bytes 262176 | tf_op jit(solution)/shard_map/ppermute | solution.py:557
  69.3 0.1 pad_maximum_fusion.1.refs_0_.refs_4_
  69.3 1.8 collective-permute-start.11
  71.2 12.7 %collective-permute-done.21 = bf16[1,272,512]{2,1,0:T(8,128)(2,1)S(1)} collective-permute-done((bf16[1,272,512]{2,1,0:T(8,128)(2,1)S(1)}, bf16[1,272,512]{2,1,0:T(8,128)(2,1)S(1)}, u32[]{:S(2)}, u32[]{:S(2)}) %collective-permute-start.21) | collective-permute-done | bytes 278560 | tf_op jit(solution)/shard_map/ppermute | solution.py:557
  83.9 2.0 collective-permute-start.20
  85.9 1.5 collective-permute-start.7
  87.4 0.1 pad_maximum_fusion.refs_1_.refs_5_
  87.5 1.5 collective-permute-start.12
  88.9 8.1 %collective-permute-done.20 = bf16[1,256,512]{2,1,0:T(8,128)(2,1)S(1)} collective-permute-done((bf16[1,256,512]{2,1,0:T(8,128)(2,1)S(1)}, bf16[1,256,512]{2,1,0:T(8,128)(2,1)S(1)}, u32[]{:S(2)}, u32[]{:S(2)}) %collective-permute-start.20) | collective-permute-done | bytes 262176 | tf_op jit(solution)/shard_map/ppermute | solution.py:557
  97.0 1.5 collective-permute-start.8
  98.5 0.5 collective-permute-start.6
  99.1 1.6 collective-permute-start.29
  100.7 1.2 collective-permute-start.30
  101.9 0.5 collective-permute-start.25
  102.5 10.1 %collective-permute-done.8.refs_5_.refs_9_ = bf16[2,272,512]{2,1,0:T(8,128)(2,1)S(1)} collective-permute-done((bf16[2,272,512]{2,1,0:T(8,128)(2,1)S(1)}, bf16[2,272,512]{2,1,0:T(8,128)(2,1)S(1)}, u32[]{:S(2)}, u32[]{:S(2)}) %collective-permute-start.8) | collective-permute-done | bytes 557088 | tf_op jit(solution)/shard_map/ppermute | solution.py:557
  112.6 1.5 collective-permute-start.26
  114.2 0.2 collective-permute-start.24
  114.3 9.6 %collective-permute-done.25.refs_20_.refs_7_.refs_24_ = bf16[2,256,512]{2,1,0:T(8,128)(2,1)} collective-permute-done((bf16[2,256,512]{2,1,0:T(8,128)(2,1)S(1)}, bf16[2,256,512]{2,1,0:T(8,128)(2,1)}, u32[]{:S(2)}, u32[]{:S(2)}) %collective-permute-start.25) | collective-permute-done | bytes 524320 | tf_op jit(solution)/shard_map/ppermute | solution.py:557
  123.9 1.5 collective-permute-start.16
  125.4 1.6 collective-permute-start.15
  127.0 8.8 %collective-permute-done.26.refs_21_.refs_8_.refs_25_ = bf16[2,272,512]{2,1,0:T(8,128)(2,1)S(1)} collective-permute-done((bf16[2,272,512]{2,1,0:T(8,128)(2,1)S(1)}, bf16[2,272,512]{2,1,0:T(8,128)(2,1)S(1)}, u32[]{:S(2)}, u32[]{:S(2)}) %collective-permute-start.26) | collective-permute-done | bytes 557088 | tf_op jit(solution)/shard_map/ppermute | solution.py:557
  135.8 0.5 collective-permute-start.14
  136.3 0.1 collective-permute-start.10
  136.4 3.4 %collective-permute-done.15.refs_12_.refs_16_ = bf16[2,256,512]{2,1,0:T(8,128)(2,1)S(1)} collective-permute-done((bf16[2,256,512]{2,1,0:T(8,128)(2,1)S(1)}, bf16[2,256,512]{2,1,0:T(8,128)(2,1)S(1)}, u32[]{:S(2)}, u32[]{:S(2)}) %collective-permute-start.15) | collective-permute-done | bytes 524320 | tf_op jit(solution)/shard_map/ppermute | solution.py:557
  139.8 0.6 collective-permute-start.34
  140.3 7.4 %collective-permute-done.16.refs_13_.refs_17_ = bf16[2,272,512]{2,1,0:T(8,128)(2,1)S(1)} collective-permute-done((bf16[2,272,512]{2,1,0:T(8,128)(2,1)S(1)}, bf16[2,272,512]{2,1,0:T(8,128)(2,1)S(1)}, u32[]{:S(2)}, u32[]{:S(2)}) %collective-permute-start.16) | collective-permute-done | bytes 557088 | tf_op jit(solution)/shard_map/ppermute | solution.py:557
  147.7 0.5 collective-permute-start.17
  148.2 0.1 collective-permute-start.31
  148.3 1.5 collective-permute-start.33
  149.9 7.4 %collective-permute-done.34.refs_29_.refs_16_.refs_33_ = bf16[2,272,512]{2,1,0:T(8,128)(2,1)} collective-permute-done((bf16[2,272,512]{2,1,0:T(8,128)(2,1)S(1)}, bf16[2,272,512]{2,1,0:T(8,128)(2,1)}, u32[]{:S(2)}, u32[]{:S(2)}) %collective-permute-start.34) | collective-permute-done | bytes 557088 | tf_op jit(solution)/shard_map/ppermute | solution.py:557
  157.3 0.5 collective-permute-start.28
  157.8 0.2 copy-done.28
  158.0 0.8 copy-done.20
  158.8 0.5 collective-permute-start.36
  159.4 11.5 %gram_part.1 = (f32[1024,1024]{1,0:T(8,128)}, f32[8,128]{1,0:T(8,128)}) custom-call(s32[1]{0:T(128)} %bitcast.tile_ref.refs_0_, bf16[2,256,512]{2,1,0:T(8,128)(2,1)} %copy-done.13, bf16[2,272,512]{2,1,0:T(8,128)(2,1)} %copy-done.9, bf16[2,256,512]{2,1,0:T(8,128)(2,1)} %copy-done.24, bf16[2,272,512]{2,1,0:T(8,128)(2,1)} %copy-done.16, ...), custom_call_target="tpu_custom_call" | custom-call | flops 6442450944 | bytes 12845056 | tf_op jit(solution)/shard_map/gram_part/pallas_call | solution.py:425
  170.9 0.1 collective-permute-start.27
  171.0 0.7 copy-done.3
  171.8 1.4 collective-permute-done.27.refs_22_.refs_9_.refs_26_
  173.2 0.7 collective-permute-done.35.refs_30_.refs_17_.refs_34_
  173.9 0.0 copy-done.11
  173.9 0.8 copy-done.12
  174.7 5.7 %all-to-all-start = ((bf16[16,544,128]{2,1,0:T(8,128)(2,1)}), bf16[16,544,128]{2,1,0:T(8,128)(2,1)S(1)}, u32[]{:S(2)}, u32[]{:S(2)}) async-start(bf16[16,544,128]{2,1,0:T(8,128)(2,1)} %after.3), calls=%async_computation | async-start | bytes 4456448 | tf_op jit(solution)/shard_map/all_to_all | solution.py:626
  181.7 0.6 stack.31.refs_0_
  182.4 52.4 %gram_factor.1 = (f32[1024,1024]{1,0:T(8,128)}, f32[1024,128]{1,0:T(8,128)}, f32[8,128]{1,0:T(8,128)}) custom-call(s32[1]{0:T(128)} %bitcast.tile_ref.refs_0_, f32[1024,1024]{1,0:T(8,128)} %get-tuple-element.14.refs_0_.refs_1_, f32[8,128]{1,0:T(8,128)} %get-tuple-element.15.refs_1_.refs_2_, bf16[2,256,512]{2,1,0:T(8,128)(2,1)} %copy-done.5, ...), custom_call_target="tpu_custom_call" | custom-call | tf_op jit(solution)/shard_map/gram_factor/pallas_call | solution.py:445
  234.7 1.2 slice.15
  235.9 1.4 copy-done.2
  237.3 19.1 %whiten_rows.1 = (f32[128,1024]{1,0:T(8,128)}, f32[128,1024]{1,0:T(8,128)}) custom-call(s32[5]{0:T(128)} %stack.31.refs_0_, bf16[16,544,128]{2,1,0:T(8,128)(2,1)} %copy-done.2, f32[1024,1024]{1,0:T(8,128)} %get-tuple-element.16.refs_2_, f32[1024,128]{1,0:T(8,128)} %get-tuple-element.17.refs_3_, bf16[2,256,512]{2,1,0:T(8,128)(2,1)} %copy-done.13, ...), custom_call_target="tpu_custom_call" | custom-call | tf_op jit(solution)/shard_map/whiten_rows/pallas_call | solution.py:524
  (103 shorter events, 0.3 us)
Async XLA Ops:
  0.6 8.6 %copy-start.30 = (s32[16,128]{1,0:T(8,128)S(1)}, s32[16,128]{1,0:T(8,128)}, u32[]{:S(2)}) copy-start(s32[16,128]{1,0:T(8,128)} %refs_7_.1) | copy-start | bytes 24580
  0.6 8.7 %copy-start.34 = (s32[8]{0:T(128)S(1)}, s32[8]{0:T(128)}, u32[]{:S(2)}) copy-start(s32[8]{0:T(128)} %param.15) | copy-start | bytes 100
  0.7 11.8 %copy-start.32 = (f32[3,4]{1,0:T(4,128)S(1)}, f32[3,4]{1,0:T(4,128)}, u32[]{:S(2)}) copy-start(f32[3,4]{1,0:T(4,128)} %param.12) | copy-start | bytes 148
  0.7 12.5 %copy-start.33 = (f32[3,3]{1,0:T(4,128)S(1)}, f32[3,3]{1,0:T(4,128)}, u32[]{:S(2)}) copy-start(f32[3,3]{1,0:T(4,128)} %param.13) | copy-start | bytes 112
  0.7 13.2 %copy-start.29 = (f32[3,3,3,9]{3,2,1,0:T(4,128)S(1)}, f32[3,3,3,9]{3,2,1,0:T(4,128)}, u32[]{:S(2)}) copy-start(f32[3,3,3,9]{3,2,1,0:T(4,128)} %param.11) | copy-start | bytes 2920
  8.8 5.7 %collective-permute-start = (bf16[513,16,128]{2,1,0:T(8,128)(2,1)}, bf16[513,16,128]{2,1,0:T(8,128)(2,1)S(1)}, u32[]{:S(2)}, u32[]{:S(2)}) collective-permute-start(bf16[513,16,128]{2,1,0:T(8,128)(2,1)} %halo_rows.1), channel_id=1, source_target_pairs={{0,1},{1,0},{2,3},{3,2},{4,5},{5,4},{6,7},{7,6},{8,9},{9,8},{10,11... | collective-permute-start | bytes 6303752 | tf_op jit(solution)/shard_map/ppermute | solution.py:601
  9.3 5.3 %collective-permute-start.1 = (s32[16,128]{1,0:T(8,128)S(1)}, s32[16,128]{1,0:T(8,128)S(1)}, u32[]{:S(2)}, u32[]{:S(2)}) collective-permute-start(s32[16,128]{1,0:T(8,128)S(1)} %copy-done.30), channel_id=1, source_target_pairs={{0,1},{1,0},{2,3},{3,2},{4,5},{5,4},{6,7},{7,6},{8,9},{9,8},{10,11... | collective-permute-start | bytes 24584 | tf_op jit(solution)/shard_map/ppermute | solution.py:600
  49.3 3.6 %copy-start.1 = (s32[512]{0:T(512)S(1)}, s32[512]{0:T(512)}, u32[]{:S(2)}) copy-start(s32[512]{0:T(512)} %param.9) | copy-start | bytes 6148
  50.8 2.1 collective-permute-start.2
  54.2 15.0 %collective-permute-start.3 = (bf16[1,256,512]{2,1,0:T(8,128)(2,1)S(1)}, bf16[1,256,512]{2,1,0:T(8,128)(2,1)S(1)}, u32[]{:S(2)}, u32[]{:S(2)}) collective-permute-start(bf16[1,256,512]{2,1,0:T(8,128)(2,1)S(1)} %bitcast.16), channel_id=1, source_target_pairs={{0,8},{2,10},{4,12},{6,14},{8,0},{10,2},{12,4},{14,6},{16,24},{18,... | collective-permute-start | bytes 786440 | tf_op jit(solution)/shard_map/ppermute | solution.py:557
  57.2 26.7 %collective-permute-start.19 = (bf16[1,256,512]{2,1,0:T(8,128)(2,1)S(1)}, bf16[1,256,512]{2,1,0:T(8,128)(2,1)S(1)}, u32[]{:S(2)}, u32[]{:S(2)}) collective-permute-start(bf16[1,256,512]{2,1,0:T(8,128)(2,1)S(1)} %bitcast.17), channel_id=1, source_target_pairs={{0,16},{2,18},{4,20},{6,22},{8,24},{10,26},{12,28},{14,30},{16,0},... | collective-permute-start | bytes 786440 | tf_op jit(solution)/shard_map/ppermute | solution.py:557
  59.8 24.1 %collective-permute-start.21 = (bf16[1,272,512]{2,1,0:T(8,128)(2,1)S(1)}, bf16[1,272,512]{2,1,0:T(8,128)(2,1)S(1)}, u32[]{:S(2)}, u32[]{:S(2)}) collective-permute-start(bf16[1,272,512]{2,1,0:T(8,128)(2,1)S(1)} %bitcast.13), channel_id=1, source_target_pairs={{0,16},{2,18},{4,20},{6,22},{8,24},{10,26},{12,28},{14,30},{16,0},... | collective-permute-start | bytes 835592 | tf_op jit(solution)/shard_map/ppermute | solution.py:557
  69.3 90.0 %copy-start.13 = (bf16[2,256,512]{2,1,0:T(8,128)(2,1)}, bf16[2,256,512]{2,1,0:T(8,128)(2,1)S(1)}, u32[]{:S(2)}) copy-start(bf16[2,256,512]{2,1,0:T(8,128)(2,1)S(1)} %pad_maximum_fusion.1.refs_0_.refs_4_) | copy-start | bytes 1572868
  69.3 29.2 %collective-permute-start.11 = (bf16[2,256,512]{2,1,0:T(8,128)(2,1)S(1)}, bf16[2,256,512]{2,1,0:T(8,128)(2,1)S(1)}, u32[]{:S(2)}, u32[]{:S(2)}) collective-permute-start(bf16[2,256,512]{2,1,0:T(8,128)(2,1)S(1)} %pad_maximum_fusion.1.refs_0_.refs_4_), channel_id=1, source_target_pairs={{0,4},{2,6},{4,0},{6,2},{8,12},{10,14},{12,8},{14,10},{16,20},{18,... | collective-permute-start | bytes 1572872 | tf_op jit(solution)/shard_map/ppermute | solution.py:557
  71.2 16.2 %collective-permute-start.4 = (bf16[1,272,512]{2,1,0:T(8,128)(2,1)S(1)}, bf16[1,272,512]{2,1,0:T(8,128)(2,1)S(1)}, u32[]{:S(2)}, u32[]{:S(2)}) collective-permute-start(bf16[1,272,512]{2,1,0:T(8,128)(2,1)S(1)} %bitcast.14), channel_id=1, source_target_pairs={{0,8},{2,10},{4,12},{6,14},{8,0},{10,2},{12,4},{14,6},{16,24},{18,... | collective-permute-start | bytes 835592 | tf_op jit(solution)/shard_map/ppermute | solution.py:557
  83.9 14.6 %collective-permute-start.22 = (bf16[1,272,512]{2,1,0:T(8,128)(2,1)S(1)}, bf16[1,272,512]{2,1,0:T(8,128)(2,1)S(1)}, u32[]{:S(2)}, u32[]{:S(2)}) collective-permute-start(bf16[1,272,512]{2,1,0:T(8,128)(2,1)S(1)} %collective-permute-done.21), channel_id=1, source_target_pairs={{0,8},{2,10},{4,12},{6,14},{8,0},{10,2},{12,4},{14,6},{16,24},{18,... | collective-permute-start | bytes 835592 | tf_op jit(solution)/shard_map/ppermute | solution.py:557
  83.9 13.1 %collective-permute-start.20 = (bf16[1,256,512]{2,1,0:T(8,128)(2,1)S(1)}, bf16[1,256,512]{2,1,0:T(8,128)(2,1)S(1)}, u32[]{:S(2)}, u32[]{:S(2)}) collective-permute-start(bf16[1,256,512]{2,1,0:T(8,128)(2,1)S(1)} %collective-permute-done.19), channel_id=1, source_target_pairs={{0,8},{2,10},{4,12},{6,14},{8,0},{10,2},{12,4},{14,6},{16,24},{18,... | collective-permute-start | bytes 786440 | tf_op jit(solution)/shard_map/ppermute | solution.py:557
  85.9 13.2 %collective-permute-start.7 = (bf16[2,256,512]{2,1,0:T(8,128)(2,1)S(1)}, bf16[2,256,512]{2,1,0:T(8,128)(2,1)S(1)}, u32[]{:S(2)}, u32[]{:S(2)}) collective-permute-start(bf16[2,256,512]{2,1,0:T(8,128)(2,1)S(1)} %pad_maximum_fusion.1.refs_0_.refs_4_), channel_id=1, source_target_pairs={{0,2},{2,0},{4,6},{6,4},{8,10},{10,8},{12,14},{14,12},{16,18},{18,... | collective-permute-start | bytes 1572872 | tf_op jit(solution)/shard_map/ppermute | solution.py:557
  87.4 71.9 %copy-start.9 = (bf16[2,272,512]{2,1,0:T(8,128)(2,1)}, bf16[2,272,512]{2,1,0:T(8,128)(2,1)S(1)}, u32[]{:S(2)}) copy-start(bf16[2,272,512]{2,1,0:T(8,128)(2,1)S(1)} %pad_maximum_fusion.refs_1_.refs_5_) | copy-start | bytes 1671172
  87.5 14.5 %collective-permute-start.12 = (bf16[2,272,512]{2,1,0:T(8,128)(2,1)S(1)}, bf16[2,272,512]{2,1,0:T(8,128)(2,1)S(1)}, u32[]{:S(2)}, u32[]{:S(2)}) collective-permute-start(bf16[2,272,512]{2,1,0:T(8,128)(2,1)S(1)} %pad_maximum_fusion.refs_1_.refs_5_), channel_id=1, source_target_pairs={{0,4},{2,6},{4,0},{6,2},{8,12},{10,14},{12,8},{14,10},{16,20},{18,... | collective-permute-start | bytes 1671176 | tf_op jit(solution)/shard_map/ppermute | solution.py:557
  97.0 15.6 %collective-permute-start.8 = (bf16[2,272,512]{2,1,0:T(8,128)(2,1)S(1)}, bf16[2,272,512]{2,1,0:T(8,128)(2,1)S(1)}, u32[]{:S(2)}, u32[]{:S(2)}) collective-permute-start(bf16[2,272,512]{2,1,0:T(8,128)(2,1)S(1)} %pad_maximum_fusion.refs_1_.refs_5_), channel_id=1, source_target_pairs={{0,2},{2,0},{4,6},{6,4},{8,10},{10,8},{12,14},{14,12},{16,18},{18,... | collective-permute-start | bytes 1671176 | tf_op jit(solution)/shard_map/ppermute | solution.py:557
  98.5 2.2 collective-permute-start.5
  98.5 59.2 %copy-start.22 = (bf16[2,256,512]{2,1,0:T(8,128)(2,1)}, bf16[2,256,512]{2,1,0:T(8,128)(2,1)S(1)}, u32[]{:S(2)}) copy-start(bf16[2,256,512]{2,1,0:T(8,128)(2,1)S(1)} %collective-permute-done.11.refs_8_.refs_12_) | copy-start | bytes 1572868
  98.5 14.1 %collective-permute-start.6 = (bf16[2,272,512]{2,1,0:T(8,128)(2,1)S(1)}, bf16[2,272,512]{2,1,0:T(8,128)(2,1)S(1)}, u32[]{:S(2)}, u32[]{:S(2)}) collective-permute-start(bf16[2,272,512]{2,1,0:T(8,128)(2,1)S(1)} %pad_maximum_fusion.refs_1_.refs_5_), channel_id=1, source_target_pairs={{0,1},{1,0},{2,3},{3,2},{4,5},{5,4},{6,7},{7,6},{8,9},{9,8},{10,11... | collective-permute-start | bytes 1671176 | tf_op jit(solution)/shard_map/ppermute | solution.py:580
  99.1 71.8 %copy-start.5 = (bf16[2,256,512]{2,1,0:T(8,128)(2,1)}, bf16[2,256,512]{2,1,0:T(8,128)(2,1)S(1)}, u32[]{:S(2)}) copy-start(bf16[2,256,512]{2,1,0:T(8,128)(2,1)S(1)} %constant_dynamic-update-slice_fusion.refs_16_.refs_3_.refs_20_) | copy-start | bytes 1572868
  99.1 58.6 %copy-start.23 = (bf16[2,256,512]{2,1,0:T(8,128)(2,1)}, bf16[2,256,512]{2,1,0:T(8,128)(2,1)S(1)}, u32[]{:S(2)}) copy-start(bf16[2,256,512]{2,1,0:T(8,128)(2,1)S(1)} %collective-permute-done.7.refs_4_.refs_8_) | copy-start | bytes 1572868
  99.1 15.0 %collective-permute-start.29 = (bf16[2,256,512]{2,1,0:T(8,128)(2,1)S(1)}, bf16[2,256,512]{2,1,0:T(8,128)(2,1)}, u32[]{:S(2)}, u32[]{:S(2)}) collective-permute-start(bf16[2,256,512]{2,1,0:T(8,128)(2,1)S(1)} %constant_dynamic-update-slice_fusion.refs_16_.refs_3_.refs_20_), channel_id=1, source_target_pairs={{0,4},{2,6},{4,0},{6,2},{8,12},{10,14},{12,8},{14,10},{16,20},{18,... | collective-permute-start | bytes 1572872 | tf_op jit(solution)/shard_map/ppermute | solution.py:557
  100.7 70.2 %copy-start.4 = (bf16[2,272,512]{2,1,0:T(8,128)(2,1)}, bf16[2,272,512]{2,1,0:T(8,128)(2,1)S(1)}, u32[]{:S(2)}) copy-start(bf16[2,272,512]{2,1,0:T(8,128)(2,1)S(1)} %constant_dynamic-update-slice_fusion.2.refs_17_.refs_4_.refs_21_) | copy-start | bytes 1671172
  100.7 57.0 %copy-start.24 = (bf16[2,256,512]{2,1,0:T(8,128)(2,1)}, bf16[2,256,512]{2,1,0:T(8,128)(2,1)S(1)}, u32[]{:S(2)}) copy-start(bf16[2,256,512]{2,1,0:T(8,128)(2,1)S(1)} %collective-permute-done.5.refs_2_.refs_6_) | copy-start | bytes 1572868
  100.7 24.7 %collective-permute-start.30 = (bf16[2,272,512]{2,1,0:T(8,128)(2,1)S(1)}, bf16[2,272,512]{2,1,0:T(8,128)(2,1)S(1)}, u32[]{:S(2)}, u32[]{:S(2)}) collective-permute-start(bf16[2,272,512]{2,1,0:T(8,128)(2,1)S(1)} %constant_dynamic-update-slice_fusion.2.refs_17_.refs_4_.refs_21_), channel_id=1, source_target_pairs={{0,4},{2,6},{4,0},{6,2},{8,12},{10,14},{12,8},{14,10},{16,20},{18,... | collective-permute-start | bytes 1671176 | tf_op jit(solution)/shard_map/ppermute | solution.py:557
  101.9 57.4 %copy-start.14 = (bf16[2,272,512]{2,1,0:T(8,128)(2,1)}, bf16[2,272,512]{2,1,0:T(8,128)(2,1)S(1)}, u32[]{:S(2)}) copy-start(bf16[2,272,512]{2,1,0:T(8,128)(2,1)S(1)} %collective-permute-done.12.refs_9_.refs_13_) | copy-start | bytes 1671172
  101.9 22.0 %collective-permute-start.25 = (bf16[2,256,512]{2,1,0:T(8,128)(2,1)S(1)}, bf16[2,256,512]{2,1,0:T(8,128)(2,1)}, u32[]{:S(2)}, u32[]{:S(2)}) collective-permute-start(bf16[2,256,512]{2,1,0:T(8,128)(2,1)S(1)} %constant_dynamic-update-slice_fusion.refs_16_.refs_3_.refs_20_), channel_id=1, source_target_pairs={{0,2},{2,0},{4,6},{6,4},{8,10},{10,8},{12,14},{14,12},{16,18},{18,... | collective-permute-start | bytes 1572872 | tf_op jit(solution)/shard_map/ppermute | solution.py:557
  112.6 46.8 %copy-start.15 = (bf16[2,272,512]{2,1,0:T(8,128)(2,1)}, bf16[2,272,512]{2,1,0:T(8,128)(2,1)S(1)}, u32[]{:S(2)}) copy-start(bf16[2,272,512]{2,1,0:T(8,128)(2,1)S(1)} %collective-permute-done.8.refs_5_.refs_9_) | copy-start | bytes 1671172
  112.6 12.8 %collective-permute-start.23 = (bf16[2,256,512]{2,1,0:T(8,128)(2,1)S(1)}, bf16[2,256,512]{2,1,0:T(8,128)(2,1)S(1)}, u32[]{:S(2)}, u32[]{:S(2)}) collective-permute-start(bf16[2,256,512]{2,1,0:T(8,128)(2,1)S(1)} %constant_dynamic-update-slice_fusion.refs_16_.refs_3_.refs_20_), channel_id=1, source_target_pairs={{0,1},{1,0},{2,3},{3,2},{4,5},{5,4},{6,7},{7,6},{8,9},{9,8},{10,11... | collective-permute-start | bytes 1572872 | tf_op jit(solution)/shard_map/ppermute | solution.py:580
  112.6 46.8 %copy-start.16 = (bf16[2,272,512]{2,1,0:T(8,128)(2,1)}, bf16[2,272,512]{2,1,0:T(8,128)(2,1)S(1)}, u32[]{:S(2)}) copy-start(bf16[2,272,512]{2,1,0:T(8,128)(2,1)S(1)} %collective-permute-done.6.refs_3_.refs_7_) | copy-start | bytes 1671172
  112.6 23.2 %collective-permute-start.26 = (bf16[2,272,512]{2,1,0:T(8,128)(2,1)S(1)}, bf16[2,272,512]{2,1,0:T(8,128)(2,1)S(1)}, u32[]{:S(2)}, u32[]{:S(2)}) collective-permute-start(bf16[2,272,512]{2,1,0:T(8,128)(2,1)S(1)} %constant_dynamic-update-slice_fusion.2.refs_17_.refs_4_.refs_21_), channel_id=1, source_target_pairs={{0,2},{2,0},{4,6},{6,4},{8,10},{10,8},{12,14},{14,12},{16,18},{18,... | collective-permute-start | bytes 1671176 | tf_op jit(solution)/shard_map/ppermute | solution.py:557
  114.2 21.6 %collective-permute-start.24 = (bf16[2,272,512]{2,1,0:T(8,128)(2,1)S(1)}, bf16[2,272,512]{2,1,0:T(8,128)(2,1)S(1)}, u32[]{:S(2)}, u32[]{:S(2)}) collective-permute-start(bf16[2,272,512]{2,1,0:T(8,128)(2,1)S(1)} %constant_dynamic-update-slice_fusion.2.refs_17_.refs_4_.refs_21_), channel_id=1, source_target_pairs={{0,1},{1,0},{2,3},{3,2},{4,5},{5,4},{6,7},{7,6},{8,9},{9,8},{10,11... | collective-permute-start | bytes 1671176 | tf_op jit(solution)/shard_map/ppermute | solution.py:580
  123.9 23.8 %collective-permute-start.16 = (bf16[2,272,512]{2,1,0:T(8,128)(2,1)S(1)}, bf16[2,272,512]{2,1,0:T(8,128)(2,1)S(1)}, u32[]{:S(2)}, u32[]{:S(2)}) collective-permute-start(bf16[2,272,512]{2,1,0:T(8,128)(2,1)S(1)} %collective-permute-done.12.refs_9_.refs_13_), channel_id=1, source_target_pairs={{0,2},{2,0},{4,6},{6,4},{8,10},{10,8},{12,14},{14,12},{16,18},{18,... | collective-permute-start | bytes 1671176 | tf_op jit(solution)/shard_map/ppermute | solution.py:557
  125.4 22.9 %copy-start.10 = (bf16[2,256,512]{2,1,0:T(8,128)(2,1)}, bf16[2,256,512]{2,1,0:T(8,128)(2,1)S(1)}, u32[]{:S(2)}) copy-start(bf16[2,256,512]{2,1,0:T(8,128)(2,1)S(1)} %collective-permute-done.23.refs_18_.refs_5_.refs_22_) | copy-start | bytes 1572868
  125.4 10.9 %collective-permute-start.13 = (bf16[2,256,512]{2,1,0:T(8,128)(2,1)S(1)}, bf16[2,256,512]{2,1,0:T(8,128)(2,1)S(1)}, u32[]{:S(2)}, u32[]{:S(2)}) collective-permute-start(bf16[2,256,512]{2,1,0:T(8,128)(2,1)S(1)} %collective-permute-done.11.refs_8_.refs_12_), channel_id=1, source_target_pairs={{0,1},{1,0},{2,3},{3,2},{4,5},{5,4},{6,7},{7,6},{8,9},{9,8},{10,11... | collective-permute-start | bytes 1572872 | tf_op jit(solution)/shard_map/ppermute | solution.py:580
  125.4 45.5 %copy-start.6 = (bf16[2,272,512]{2,1,0:T(8,128)(2,1)}, bf16[2,272,512]{2,1,0:T(8,128)(2,1)S(1)}, u32[]{:S(2)}) copy-start(bf16[2,272,512]{2,1,0:T(8,128)(2,1)S(1)} %collective-permute-done.30.refs_25_.refs_12_.refs_29_) | copy-start | bytes 1671172
  125.4 14.3 %collective-permute-start.15 = (bf16[2,256,512]{2,1,0:T(8,128)(2,1)S(1)}, bf16[2,256,512]{2,1,0:T(8,128)(2,1)S(1)}, u32[]{:S(2)}, u32[]{:S(2)}) collective-permute-start(bf16[2,256,512]{2,1,0:T(8,128)(2,1)S(1)} %collective-permute-done.7.refs_4_.refs_8_), channel_id=1, source_target_pairs={{0,4},{2,6},{4,0},{6,2},{8,12},{10,14},{12,8},{14,10},{16,20},{18,... | collective-permute-start | bytes 1572872 | tf_op jit(solution)/shard_map/ppermute | solution.py:557
  135.8 35.1 %copy-start.7 = (bf16[2,272,512]{2,1,0:T(8,128)(2,1)}, bf16[2,272,512]{2,1,0:T(8,128)(2,1)S(1)}, u32[]{:S(2)}) copy-start(bf16[2,272,512]{2,1,0:T(8,128)(2,1)S(1)} %collective-permute-done.26.refs_21_.refs_8_.refs_25_) | copy-start | bytes 1671172
  135.8 11.9 %collective-permute-start.9 = (bf16[2,256,512]{2,1,0:T(8,128)(2,1)S(1)}, bf16[2,256,512]{2,1,0:T(8,128)(2,1)S(1)}, u32[]{:S(2)}, u32[]{:S(2)}) collective-permute-start(bf16[2,256,512]{2,1,0:T(8,128)(2,1)S(1)} %collective-permute-done.7.refs_4_.refs_8_), channel_id=1, source_target_pairs={{0,1},{1,0},{2,3},{3,2},{4,5},{5,4},{6,7},{7,6},{8,9},{9,8},{10,11... | collective-permute-start | bytes 1572872 | tf_op jit(solution)/shard_map/ppermute | solution.py:580
  135.8 35.1 %copy-start.8 = (bf16[2,272,512]{2,1,0:T(8,128)(2,1)}, bf16[2,272,512]{2,1,0:T(8,128)(2,1)S(1)}, u32[]{:S(2)}) copy-start(bf16[2,272,512]{2,1,0:T(8,128)(2,1)S(1)} %collective-permute-done.24.refs_19_.refs_6_.refs_23_) | copy-start | bytes 1671172
  135.8 12.4 %collective-permute-start.14 = (bf16[2,272,512]{2,1,0:T(8,128)(2,1)S(1)}, bf16[2,272,512]{2,1,0:T(8,128)(2,1)S(1)}, u32[]{:S(2)}, u32[]{:S(2)}) collective-permute-start(bf16[2,272,512]{2,1,0:T(8,128)(2,1)S(1)} %collective-permute-done.12.refs_9_.refs_13_), channel_id=1, source_target_pairs={{0,1},{1,0},{2,3},{3,2},{4,5},{5,4},{6,7},{7,6},{8,9},{9,8},{10,11... | collective-permute-start | bytes 1671176 | tf_op jit(solution)/shard_map/ppermute | solution.py:580
  136.3 21.5 %copy-start.25 = (bf16[2,256,512]{2,1,0:T(8,128)(2,1)}, bf16[2,256,512]{2,1,0:T(8,128)(2,1)S(1)}, u32[]{:S(2)}) copy-start(bf16[2,256,512]{2,1,0:T(8,128)(2,1)S(1)} %collective-permute-done.13.refs_10_.refs_14_) | copy-start | bytes 1572868
  136.3 12.0 %collective-permute-start.10 = (bf16[2,272,512]{2,1,0:T(8,128)(2,1)S(1)}, bf16[2,272,512]{2,1,0:T(8,128)(2,1)S(1)}, u32[]{:S(2)}, u32[]{:S(2)}) collective-permute-start(bf16[2,272,512]{2,1,0:T(8,128)(2,1)S(1)} %collective-permute-done.8.refs_5_.refs_9_), channel_id=1, source_target_pairs={{0,1},{1,0},{2,3},{3,2},{4,5},{5,4},{6,7},{7,6},{8,9},{9,8},{10,11... | collective-permute-start | bytes 1671176 | tf_op jit(solution)/shard_map/ppermute | solution.py:580
  139.8 18.0 %copy-start.26 = (bf16[2,256,512]{2,1,0:T(8,128)(2,1)}, bf16[2,256,512]{2,1,0:T(8,128)(2,1)S(1)}, u32[]{:S(2)}) copy-start(bf16[2,256,512]{2,1,0:T(8,128)(2,1)S(1)} %collective-permute-done.15.refs_12_.refs_16_) | copy-start | bytes 1572868
  139.8 17.5 %collective-permute-start.34 = (bf16[2,272,512]{2,1,0:T(8,128)(2,1)S(1)}, bf16[2,272,512]{2,1,0:T(8,128)(2,1)}, u32[]{:S(2)}, u32[]{:S(2)}) collective-permute-start(bf16[2,272,512]{2,1,0:T(8,128)(2,1)S(1)} %collective-permute-done.30.refs_25_.refs_12_.refs_29_), channel_id=1, source_target_pairs={{0,2},{2,0},{4,6},{6,4},{8,10},{10,8},{12,14},{14,12},{16,18},{18,... | collective-permute-start | bytes 1671176 | tf_op jit(solution)/shard_map/ppermute | solution.py:557
  147.7 11.7 %copy-start.17 = (bf16[2,272,512]{2,1,0:T(8,128)(2,1)}, bf16[2,272,512]{2,1,0:T(8,128)(2,1)S(1)}, u32[]{:S(2)}) copy-start(bf16[2,272,512]{2,1,0:T(8,128)(2,1)S(1)} %collective-permute-done.16.refs_13_.refs_17_) | copy-start | bytes 1671172
  147.7 10.1 %collective-permute-start.18 = (bf16[2,272,512]{2,1,0:T(8,128)(2,1)S(1)}, bf16[2,272,512]{2,1,0:T(8,128)(2,1)S(1)}, u32[]{:S(2)}, u32[]{:S(2)}) collective-permute-start(bf16[2,272,512]{2,1,0:T(8,128)(2,1)S(1)} %collective-permute-done.16.refs_13_.refs_17_), channel_id=1, source_target_pairs={{0,1},{1,0},{2,3},{3,2},{4,5},{5,4},{6,7},{7,6},{8,9},{9,8},{10,11... | collective-permute-start | bytes 1671176 | tf_op jit(solution)/shard_map/ppermute | solution.py:580
  147.7 10.1 %copy-start.27 = (bf16[2,256,512]{2,1,0:T(8,128)(2,1)}, bf16[2,256,512]{2,1,0:T(8,128)(2,1)S(1)}, u32[]{:S(2)}) copy-start(bf16[2,256,512]{2,1,0:T(8,128)(2,1)S(1)} %collective-permute-done.9.refs_6_.refs_10_) | copy-start | bytes 1572868
  147.7 9.5 %collective-permute-start.17 = (bf16[2,256,512]{2,1,0:T(8,128)(2,1)S(1)}, bf16[2,256,512]{2,1,0:T(8,128)(2,1)S(1)}, u32[]{:S(2)}, u32[]{:S(2)}) collective-permute-start(bf16[2,256,512]{2,1,0:T(8,128)(2,1)S(1)} %collective-permute-done.15.refs_12_.refs_16_), channel_id=1, source_target_pairs={{0,1},{1,0},{2,3},{3,2},{4,5},{5,4},{6,7},{7,6},{8,9},{9,8},{10,11... | collective-permute-start | bytes 1572872 | tf_op jit(solution)/shard_map/ppermute | solution.py:580
  148.2 11.2 %copy-start.18 = (bf16[2,272,512]{2,1,0:T(8,128)(2,1)}, bf16[2,272,512]{2,1,0:T(8,128)(2,1)S(1)}, u32[]{:S(2)}) copy-start(bf16[2,272,512]{2,1,0:T(8,128)(2,1)S(1)} %collective-permute-done.14.refs_11_.refs_15_) | copy-start | bytes 1671172
  148.2 23.5 %collective-permute-start.31 = (bf16[2,256,512]{2,1,0:T(8,128)(2,1)}, bf16[2,256,512]{2,1,0:T(8,128)(2,1)}, u32[]{:S(2)}, u32[]{:S(2)}) collective-permute-start(bf16[2,256,512]{2,1,0:T(8,128)(2,1)} %collective-permute-done.29.refs_24_.refs_11_.refs_28_), channel_id=1, source_target_pairs={{0,1},{1,0},{2,3},{3,2},{4,5},{5,4},{6,7},{7,6},{8,9},{9,8},{10,11... | collective-permute-start | bytes 1572872 | tf_op jit(solution)/shard_map/ppermute | solution.py:580
  148.3 11.1 %copy-start.19 = (bf16[2,272,512]{2,1,0:T(8,128)(2,1)}, bf16[2,272,512]{2,1,0:T(8,128)(2,1)S(1)}, u32[]{:S(2)}) copy-start(bf16[2,272,512]{2,1,0:T(8,128)(2,1)S(1)} %collective-permute-done.10.refs_7_.refs_11_) | copy-start | bytes 1671172
  148.3 22.6 %collective-permute-start.33 = (bf16[2,256,512]{2,1,0:T(8,128)(2,1)}, bf16[2,256,512]{2,1,0:T(8,128)(2,1)S(1)}, u32[]{:S(2)}, u32[]{:S(2)}) collective-permute-start(bf16[2,256,512]{2,1,0:T(8,128)(2,1)} %collective-permute-done.25.refs_20_.refs_7_.refs_24_), channel_id=1, source_target_pairs={{0,4},{2,6},{4,0},{6,2},{8,12},{10,14},{12,8},{14,10},{16,20},{18,... | collective-permute-start | bytes 1572872 | tf_op jit(solution)/shard_map/ppermute | solution.py:557
  157.2 15.9 %collective-permute-start.32 = (bf16[2,272,512]{2,1,0:T(8,128)(2,1)S(1)}, bf16[2,272,512]{2,1,0:T(8,128)(2,1)}, u32[]{:S(2)}, u32[]{:S(2)}) collective-permute-start(bf16[2,272,512]{2,1,0:T(8,128)(2,1)S(1)} %collective-permute-done.30.refs_25_.refs_12_.refs_29_), channel_id=1, source_target_pairs={{0,1},{1,0},{2,3},{3,2},{4,5},{5,4},{6,7},{7,6},{8,9},{9,8},{10,11... | collective-permute-start | bytes 1671176 | tf_op jit(solution)/shard_map/ppermute | solution.py:580
  157.3 15.9 %collective-permute-start.28 = (bf16[2,272,512]{2,1,0:T(8,128)(2,1)S(1)}, bf16[2,272,512]{2,1,0:T(8,128)(2,1)}, u32[]{:S(2)}, u32[]{:S(2)}) collective-permute-start(bf16[2,272,512]{2,1,0:T(8,128)(2,1)S(1)} %collective-permute-done.26.refs_21_.refs_8_.refs_25_), channel_id=1, source_target_pairs={{0,1},{1,0},{2,3},{3,2},{4,5},{5,4},{6,7},{7,6},{8,9},{9,8},{10,11... | collective-permute-start | bytes 1671176 | tf_op jit(solution)/shard_map/ppermute | solution.py:580
  158.8 14.3 %collective-permute-start.36 = (bf16[2,272,512]{2,1,0:T(8,128)(2,1)}, bf16[2,272,512]{2,1,0:T(8,128)(2,1)}, u32[]{:S(2)}, u32[]{:S(2)}) collective-permute-start(bf16[2,272,512]{2,1,0:T(8,128)(2,1)} %collective-permute-done.34.refs_29_.refs_16_.refs_33_), channel_id=1, source_target_pairs={{0,1},{1,0},{2,3},{3,2},{4,5},{5,4},{6,7},{7,6},{8,9},{9,8},{10,11... | collective-permute-start | bytes 1671176 | tf_op jit(solution)/shard_map/ppermute | solution.py:580
  170.9 2.2 collective-permute-start.27
  171.8 2.1 collective-permute-start.35
  174.7 61.2 %all-to-all-start = ((bf16[16,544,128]{2,1,0:T(8,128)(2,1)}), bf16[16,544,128]{2,1,0:T(8,128)(2,1)S(1)}, u32[]{:S(2)}, u32[]{:S(2)}) async-start(bf16[16,544,128]{2,1,0:T(8,128)(2,1)} %after.3), calls=%async_computation | async-start | bytes 4456448 | tf_op jit(solution)/shard_map/all_to_all | solution.py:626
  (9 other events, 10.9 us)

commit v3 on v2

--- a/solution.py
+++ b/solution.py
@@ -16,17 +16,18 @@
 
 def halo_kernel(tile_ref, own_ref, out_ref):
     block = own_ref.shape[0]
-    row = lax.broadcasted_iota(jnp.int32, (16, 48), 0)
-    col = lax.broadcasted_iota(jnp.int32, (16, 48), 1)
+    row = lax.broadcasted_iota(jnp.int32, (16, 24), 0)
+    col = lax.broadcasted_iota(jnp.int32, (16, 24), 1)
     dist = lax.div(row, 3)
-    source = jnp.where(tile_ref[0] == 0, 15 - dist, dist)
-    pick = jnp.where((row < 9) & (col == lax.rem(row, 3) * 16 + source), 1.0, 0.0).astype(BF16)
-    for base in range(0, block, 3):
+    source = jnp.where(tile_ref[0] == 0, 7 - dist, dist)
+    pick = jnp.where((row < 9) & (col == lax.rem(row, 3) * 8 + source), 1.0, 0.0).astype(BF16)
+    group = block // 3
+    for base in range(0, block, group):
         cells = jnp.concatenate(
-            [own_ref[base + k].reshape(48, 128) for k in range(3)], axis=1
-        )
+            [own_ref[base + k].astype(F32).reshape(24, 128) for k in range(group)], axis=1
+        ).astype(BF16)
         rows = jnp.dot(pick, cells, preferred_element_type=F32).astype(BF16)
-        for k in range(3):
+        for k in range(group):
             out_ref[base + k] = rows[:, 128 * k : 128 * (k + 1)]
 
 
@@ -35,19 +36,19 @@
     block = next(b for b in (57, 27, 9, 3) if count % b == 0)
     return pl.pallas_call(
         halo_kernel,
-        grid=(count // block,),
-        in_specs=[
-            pl.BlockSpec(memory_space=pltpu.SMEM),
-            pl.BlockSpec((block, 3, 16, 128), lambda i: (i, 0, 0, 0)),
-        ],
-        out_specs=pl.BlockSpec((block, 16, 128), lambda i: (i, 0, 0)),
+        grid_spec=pltpu.PrefetchScalarGridSpec(
+            num_scalar_prefetch=1,
+            grid=(count // block,),
+            in_specs=[pl.BlockSpec((block, 3, 8, 128), lambda i, tile: (i, 0, 1 - tile[0], 0))],
+            out_specs=pl.BlockSpec((block, 16, 128), lambda i, tile: (i, 0, 0)),
+        ),
         out_shape=jax.ShapeDtypeStruct((count, 16, 128), BF16),
         name="halo_rows",
     )(tile_idx, snapshots)
 
 
-GROUP = 32
-BLOCK = 32
+GROUP = 48
+BLOCK = 48
 
 
 def encode_kernel(
@@ -219,20 +220,21 @@
         at = 8 * home
         cols = [lanes(a[home], at + k) for k in range(8)]
         e = [[sublanes(cols[k], i) for k in range(i + 1)] for i in range(8)]
-        invert = []
+        root = []
         mult = [[None] * 8 for _ in range(8)]
         for k in range(8):
-            invert.append(1.0 / e[k][k])
+            root.append(lax.rsqrt(e[k][k]))
             for i in range(k + 1, 8):
-                mult[i][k] = e[i][k] * invert[k]
+                mult[i][k] = e[i][k] * root[k]
             for i in range(k + 1, 8):
                 for j in range(k + 1, i + 1):
-                    e[i][j] = e[i][j] - mult[i][k] * e[j][k]
+                    e[i][j] = e[i][j] - mult[i][k] * mult[j][k]
 
         def forward(rows):
             for k in range(8):
                 for m in range(k):
                     rows[k] = rows[k] - mult[k][m] * rows[m]
+                rows[k] = rows[k] * root[k]
             return rows
 
         def pack(rows):
@@ -245,15 +247,11 @@
         v = forward([sublanes(b[home], k) for k in range(8)])
         a[home] = pack(u)
         b[home] = pack(v)
-        if home + 1 == groups:
-            break
-        us = [u[k] * invert[k] for k in range(8)]
-        vs = [v[k] * invert[k] for k in range(8)]
         for g in range(home + 1, groups):
             c = forward([lanes(a[g], at + k) for k in range(8)])
             for k in range(8):
-                a[g] = a[g] - c[k] * us[k]
-                b[g] = b[g] - c[k] * vs[k]
+                a[g] = a[g] - c[k] * u[k]
+                b[g] = b[g] - c[k] * v[k]
     return jnp.concatenate(a, axis=0), jnp.concatenate(b, axis=0)
 
 
@@ -318,9 +316,12 @@
     pairs = [blocks_of(flip, refs) for refs in pieces]
     lead = jnp.concatenate([pair[0] for pair in pairs], axis=1)
     tail = jnp.concatenate([pair[1] for pair in pairs], axis=1)
-    low_ref[0:PANEL, 0:PANEL] += dot_nt(lead, lead)
     low_ref[PANEL:, 0:PANEL] += dot_nt(tail, lead)
-    low_ref[PANEL:, PANEL:] += dot_nt(tail, tail)
+    for base, part in ((0, lead), (PANEL, tail)):
+        low_ref[base : base + PANEL, base : base + HALF] += dot_nt(part, part[0:HALF])
+        low_ref[base + HALF : base + PANEL, base + HALF : base + PANEL] += dot_nt(
+            part[HALF:], part[HALF:]
+        )
     for refs in pieces:
         for ref in (refs[1], refs[3]):
             part = ref[0, HALF:, 0:EDGE].astype(F32)
@@ -392,11 +393,9 @@
 
     def step(k, carry):
         at = pl.ds(pl.multiple_of(k * EDGE, EDGE), EDGE)
-        upper, unit = factor_diag(low_ref[at, at], eye)
-        pivots = jnp.sum(jnp.where(row == col, upper, 0.0), axis=1, keepdims=True)
-        root = lax.rsqrt(pivots)
-        low_ref[at, at] = (jnp.where(col >= row, upper, 0.0) * root).T
-        inv_ref[at, :] = unit * root
+        upper, inverse = factor_diag(low_ref[at, at], eye)
+        low_ref[at, at] = jnp.where(col >= row, upper, 0.0).T
+        inv_ref[at, :] = inverse
         for static in range(blocks - 1):
             @pl.when(k == static)
             def _():
@@ -477,17 +476,20 @@
         values = enc_ref[source]
         packed = parts[k][1][0, HALF:, :].astype(F32)
         starts = (4.0 * packed[3:4] + packed[4:5]).astype(jnp.int32)
-        first = jnp.where(snap_idx == starts, 1.0, 0.0).astype(BF16)
-        second = jnp.where(snap_idx == starts + 1, 1.0, 0.0).astype(BF16)
-        picked.append(
-            jnp.concatenate(
+        hit = jnp.where(snap_idx == starts, 1.0, 0.0).astype(BF16)
+        following = pltpu.roll(values.astype(F32), snaps - 1, 0).astype(BF16)
+        if own % EDGE == 0:
+            wide = jnp.concatenate([values, following], axis=1)
+            rows = lax.dot_general(wide, hit, tn, preferred_element_type=F32)
+        else:
+            rows = jnp.concatenate(
                 [
-                    lax.dot_general(values, first, tn, preferred_element_type=F32),
-                    lax.dot_general(values, second, tn, preferred_element_type=F32),
+                    lax.dot_general(values, hit, tn, preferred_element_type=F32),
+                    lax.dot_general(following, hit, tn, preferred_element_type=F32),
                 ],
                 axis=0,
-            ).astype(BF16)
-        )
+            )
+        picked.append(rows.astype(BF16))
     both = [blocks_of(flip, part) for part in parts]
     picked = jnp.concatenate(picked, axis=1)
     sums_ref[:, 0:PANEL] += dot_nt(picked, jnp.concatenate([b[0] for b in both], axis=1))

time: 257 us -> 248 us (0.965)
  Pallas kernels: 125 us -> 117 us
    pallas_call x1, Pallas kernels: 52.4 us -> 49.2 us  [gram_factor(): pl.pallas_call(body, grid=(pieces[0].shape[0],), in_specs=[pl.BlockSpec(m...]
    unnamed x72 -> x70, local copies, waits for them, and re-layouts: 6.04 us -> 6.08 us
  transfers between devices with their start and end apart: 38 -> 38, of which waited for: 12 -> 12; matrix products, arithmetic and copies ran while one was open for 2% -> 2% of each run, Pallas kernels for 25% -> 24%
where the time goes in v3:
time: 248 us
  Pallas kernels  117 us (47%)
  waiting for transfers between devices  80.3 us (32%)
  starting transfers between devices  33.9 us (14%)
  local copies, waits for them, and re-layouts  10.5 us (4%)
  between operations  4.91 us (2%)
    ppermute x18, waiting for transfers between devices, across(): return [lax.ppermute(x, 'dp', pairs) for x in arrays]  76.6 us
    pallas_call x1, Pallas kernels, gram_factor(): pl.pallas_call(body, grid=(pieces[0].shape[0],), in_specs=[pl.BlockSpec(m...  49.2 us
    pallas_call x1, Pallas kernels, encode(): pl.pallas_call(body, grid=(pl.cdiv(count, BLOCK),), in_specs=[smem, smem,...  30.5 us
    ppermute x18, starting transfers between devices, across(): return [lax.ppermute(x, 'dp', pairs) for x in arrays]  24.2 us
    pallas_call x1, Pallas kernels, whiten_rows(): pl.pallas_call(body, grid=(pieces[0].shape[0],), in_specs=[pl.BlockSpec(m...  18 us
    pallas_call x1, Pallas kernels, gram_part(): pl.pallas_call(gram_kernel, grid=(pieces[0].shape[0],), in_specs=[pl.Bloc...  10.4 us
    pallas_call x1, Pallas kernels, halo_rows(): pl.pallas_call(halo_kernel, grid_spec=pltpu.PrefetchScalarGridSpec(num_sc...  7.14 us
    unnamed x70, local copies, waits for them, and re-layouts  6.08 us
  transfers between devices with their start and end apart: 38, of which 12 were waited for; matrix products, arithmetic and copies ran while one was open for 2% of the time, Pallas kernels for 24%

profile of v3, /device:TPU:0, one launch (start us, length us, event | category | flops | bytes accessed | tf_op | source)
XLA Modules:
  0.0 247.8 jit_solution(17068750264416181343)
XLA Ops:
  0.7 7.1 %halo_rows.1 = bf16[513,16,128]{2,1,0:T(8,128)(2,1)} custom-call(s32[1]{0:T(128)} %bitcast.tile_ref.refs_0_, bf16[513,3,16,128]{3,2,1,0:T(8,128)(2,1)} %refs_5_.1), custom_call_target="tpu_custom_call" | custom-call | tf_op jit(solution)/shard_map/halo_rows/pallas_call | solution.py:37
  7.8 0.5 collective-permute-start
  8.3 0.1 collective-permute-start.1
  8.3 0.6 fusion
  11.4 0.6 reshape.16.refs_2_
  12.0 0.7 reshape.17.refs_3_
  12.7 0.7 reshape.15.refs_1_
  13.4 0.6 copy-done.30
  14.0 1.3 copy-done.21
  15.3 30.5 %encode.1.enc_ref.value_ref = bf16[16,528,128]{2,1,0:T(8,128)(2,1)} custom-call(s32[1]{0:T(128)} %bitcast.tile_ref.refs_0_, f32[243]{0:T(256)} %reshape.15.refs_1_, f32[12]{0:T(128)} %reshape.16.refs_2_, f32[9]{0:T(128)} %reshape.17.refs_3_, f32[3]{0:T(128)} %refs_4_.1, bf16[513,3,16,128]{3,2,1,0:T(8,128)(2,1)} %refs_5_.1, bf16[513,16,128]{2,1,0:T(8,128)(2,1)} %copy-done.21, ...), custom_call_target="tpu_custom_call" | custom-call | tf_op jit(solution)/shard_map/encode/pallas_call | solution.py:164
  45.8 1.4 dynamic-slice_select_fusion
  47.2 0.5 collective-permute-start.2
  47.7 1.6 collective-permute-done.2.near_ref
  49.3 1.4 pick_pairs.1
  50.6 2.9 %collective-permute-start.3 = (bf16[1,256,512]{2,1,0:T(8,128)(2,1)S(1)}, bf16[1,256,512]{2,1,0:T(8,128)(2,1)S(1)}, u32[]{:S(2)}, u32[]{:S(2)}) collective-permute-start(bf16[1,256,512]{2,1,0:T(8,128)(2,1)S(1)} %bitcast.16), channel_id=1, source_target_pairs={{0,8},{2,10},{4,12},{6,14},{8,0},{10,2},{12,4},{14,6},{16,24},{18,... | collective-permute-start | bytes 786440 | tf_op jit(solution)/shard_map/ppermute | solution.py:559
  53.6 2.6 %collective-permute-start.19 = (bf16[1,256,512]{2,1,0:T(8,128)(2,1)S(1)}, bf16[1,256,512]{2,1,0:T(8,128)(2,1)S(1)}, u32[]{:S(2)}, u32[]{:S(2)}) collective-permute-start(bf16[1,256,512]{2,1,0:T(8,128)(2,1)S(1)} %bitcast.17), channel_id=1, source_target_pairs={{0,16},{2,18},{4,20},{6,22},{8,24},{10,26},{12,28},{14,30},{16,0},... | collective-permute-start | bytes 786440 | tf_op jit(solution)/shard_map/ppermute | solution.py:559
  56.2 0.3 collective-permute-start.21
  56.5 9.2 %collective-permute-done.3 = bf16[1,256,512]{2,1,0:T(8,128)(2,1)S(1)} collective-permute-done((bf16[1,256,512]{2,1,0:T(8,128)(2,1)S(1)}, bf16[1,256,512]{2,1,0:T(8,128)(2,1)S(1)}, u32[]{:S(2)}, u32[]{:S(2)}) %collective-permute-start.3) | collective-permute-done | bytes 262176 | tf_op jit(solution)/shard_map/ppermute | solution.py:559
  65.7 0.1 pad_maximum_fusion.1.refs_0_.refs_4_
  65.8 1.8 collective-permute-start.11
  67.5 12.8 %collective-permute-done.21 = bf16[1,272,512]{2,1,0:T(8,128)(2,1)S(1)} collective-permute-done((bf16[1,272,512]{2,1,0:T(8,128)(2,1)S(1)}, bf16[1,272,512]{2,1,0:T(8,128)(2,1)S(1)}, u32[]{:S(2)}, u32[]{:S(2)}) %collective-permute-start.21) | collective-permute-done | bytes 278560 | tf_op jit(solution)/shard_map/ppermute | solution.py:559
  80.3 2.0 collective-permute-start.20
  82.3 1.5 collective-permute-start.7
  83.8 0.1 pad_maximum_fusion.refs_1_.refs_5_
  83.9 1.5 collective-permute-start.12
  85.4 8.1 %collective-permute-done.20 = bf16[1,256,512]{2,1,0:T(8,128)(2,1)S(1)} collective-permute-done((bf16[1,256,512]{2,1,0:T(8,128)(2,1)S(1)}, bf16[1,256,512]{2,1,0:T(8,128)(2,1)S(1)}, u32[]{:S(2)}, u32[]{:S(2)}) %collective-permute-start.20) | collective-permute-done | bytes 262176 | tf_op jit(solution)/shard_map/ppermute | solution.py:559
  93.4 1.5 collective-permute-start.8
  95.0 0.5 collective-permute-start.6
  95.6 1.5 collective-permute-start.29
  97.2 1.2 collective-permute-start.30
  98.3 0.6 collective-permute-start.25
  98.9 10.1 %collective-permute-done.8.refs_5_.refs_9_ = bf16[2,272,512]{2,1,0:T(8,128)(2,1)S(1)} collective-permute-done((bf16[2,272,512]{2,1,0:T(8,128)(2,1)S(1)}, bf16[2,272,512]{2,1,0:T(8,128)(2,1)S(1)}, u32[]{:S(2)}, u32[]{:S(2)}) %collective-permute-start.8) | collective-permute-done | bytes 557088 | tf_op jit(solution)/shard_map/ppermute | solution.py:559
  109.0 1.6 collective-permute-start.26
  110.6 0.2 collective-permute-start.24
  110.8 9.6 %collective-permute-done.25.refs_20_.refs_7_.refs_24_ = bf16[2,256,512]{2,1,0:T(8,128)(2,1)} collective-permute-done((bf16[2,256,512]{2,1,0:T(8,128)(2,1)S(1)}, bf16[2,256,512]{2,1,0:T(8,128)(2,1)}, u32[]{:S(2)}, u32[]{:S(2)}) %collective-permute-start.25) | collective-permute-done | bytes 524320 | tf_op jit(solution)/shard_map/ppermute | solution.py:559
  120.3 1.5 collective-permute-start.16
  121.9 1.5 collective-permute-start.15
  123.4 8.8 %collective-permute-done.26.refs_21_.refs_8_.refs_25_ = bf16[2,272,512]{2,1,0:T(8,128)(2,1)S(1)} collective-permute-done((bf16[2,272,512]{2,1,0:T(8,128)(2,1)S(1)}, bf16[2,272,512]{2,1,0:T(8,128)(2,1)S(1)}, u32[]{:S(2)}, u32[]{:S(2)}) %collective-permute-start.26) | collective-permute-done | bytes 557088 | tf_op jit(solution)/shard_map/ppermute | solution.py:559
  132.2 0.5 collective-permute-start.14
  132.7 0.1 collective-permute-start.10
  132.8 3.4 %collective-permute-done.15.refs_12_.refs_16_ = bf16[2,256,512]{2,1,0:T(8,128)(2,1)S(1)} collective-permute-done((bf16[2,256,512]{2,1,0:T(8,128)(2,1)S(1)}, bf16[2,256,512]{2,1,0:T(8,128)(2,1)S(1)}, u32[]{:S(2)}, u32[]{:S(2)}) %collective-permute-start.15) | collective-permute-done | bytes 524320 | tf_op jit(solution)/shard_map/ppermute | solution.py:559
  136.2 0.5 collective-permute-start.34
  136.7 7.4 %collective-permute-done.16.refs_13_.refs_17_ = bf16[2,272,512]{2,1,0:T(8,128)(2,1)S(1)} collective-permute-done((bf16[2,272,512]{2,1,0:T(8,128)(2,1)S(1)}, bf16[2,272,512]{2,1,0:T(8,128)(2,1)S(1)}, u32[]{:S(2)}, u32[]{:S(2)}) %collective-permute-start.16) | collective-permute-done | bytes 557088 | tf_op jit(solution)/shard_map/ppermute | solution.py:559
  144.1 0.5 collective-permute-start.17
  144.6 0.1 collective-permute-start.31
  144.7 1.6 collective-permute-start.33
  146.3 7.3 %collective-permute-done.34.refs_29_.refs_16_.refs_33_ = bf16[2,272,512]{2,1,0:T(8,128)(2,1)} collective-permute-done((bf16[2,272,512]{2,1,0:T(8,128)(2,1)S(1)}, bf16[2,272,512]{2,1,0:T(8,128)(2,1)}, u32[]{:S(2)}, u32[]{:S(2)}) %collective-permute-start.34) | collective-permute-done | bytes 557088 | tf_op jit(solution)/shard_map/ppermute | solution.py:559
  153.7 0.5 collective-permute-start.28
  154.2 0.3 copy-done.27
  154.5 0.8 copy-done.20
  155.3 0.5 collective-permute-start.36
  155.8 10.4 %gram_part.1 = (f32[1024,1024]{1,0:T(8,128)}, f32[8,128]{1,0:T(8,128)}) custom-call(s32[1]{0:T(128)} %bitcast.tile_ref.refs_0_, bf16[2,256,512]{2,1,0:T(8,128)(2,1)} %copy-done.13, bf16[2,272,512]{2,1,0:T(8,128)(2,1)} %copy-done.9, bf16[2,256,512]{2,1,0:T(8,128)(2,1)} %copy-done.24, bf16[2,272,512]{2,1,0:T(8,128)(2,1)} %copy-done.16, ...), custom_call_target="tpu_custom_call" | custom-call | flops 6442450944 | bytes 12845056 | tf_op jit(solution)/shard_map/gram_part/pallas_call | solution.py:424
  166.3 0.1 collective-permute-start.27
  166.4 0.7 copy-done.3
  167.1 1.4 collective-permute-done.27.refs_22_.refs_9_.refs_26_
  168.5 0.7 collective-permute-done.35.refs_30_.refs_17_.refs_34_
  169.2 0.0 copy-done.11
  169.3 0.8 copy-done.12
  170.1 5.8 %all-to-all-start = ((bf16[16,528,128]{2,1,0:T(8,128)(2,1)}), bf16[16,528,128]{2,1,0:T(8,128)(2,1)S(1)}, u32[]{:S(2)}, u32[]{:S(2)}) async-start(bf16[16,528,128]{2,1,0:T(8,128)(2,1)} %after.3), calls=%async_computation | async-start | bytes 4325376 | tf_op jit(solution)/shard_map/all_to_all | solution.py:628
  177.1 0.7 stack.31.refs_0_
  177.7 49.2 %gram_factor.1 = (f32[1024,1024]{1,0:T(8,128)}, f32[1024,128]{1,0:T(8,128)}, f32[8,128]{1,0:T(8,128)}) custom-call(s32[1]{0:T(128)} %bitcast.tile_ref.refs_0_, f32[1024,1024]{1,0:T(8,128)} %get-tuple-element.14.refs_0_.refs_1_, f32[8,128]{1,0:T(8,128)} %get-tuple-element.15.refs_1_.refs_2_, bf16[2,256,512]{2,1,0:T(8,128)(2,1)} %copy-done.5, ...), custom_call_target="tpu_custom_call" | custom-call | tf_op jit(solution)/shard_map/gram_factor/pallas_call | solution.py:444
  227.0 1.2 slice.15
  228.2 1.4 copy-done.2
  229.6 18.0 %whiten_rows.1 = (f32[128,1024]{1,0:T(8,128)}, f32[128,1024]{1,0:T(8,128)}) custom-call(s32[5]{0:T(128)} %stack.31.refs_0_, bf16[16,528,128]{2,1,0:T(8,128)(2,1)} %copy-done.2, f32[1024,1024]{1,0:T(8,128)} %get-tuple-element.16.refs_2_, f32[1024,128]{1,0:T(8,128)} %get-tuple-element.17.refs_3_, bf16[2,256,512]{2,1,0:T(8,128)(2,1)} %copy-done.13, ...), custom_call_target="tpu_custom_call" | custom-call | tf_op jit(solution)/shard_map/whiten_rows/pallas_call | solution.py:526
  (101 shorter events, 0.3 us)
Async XLA Ops:
  0.6 7.6 %copy-start.29 = (s32[16,128]{1,0:T(8,128)S(1)}, s32[16,128]{1,0:T(8,128)}, u32[]{:S(2)}) copy-start(s32[16,128]{1,0:T(8,128)} %refs_7_.1) | copy-start | bytes 24580
  0.6 7.7 %copy-start.33 = (s32[8]{0:T(128)S(1)}, s32[8]{0:T(128)}, u32[]{:S(2)}) copy-start(s32[8]{0:T(128)} %param.15) | copy-start | bytes 100
  0.7 10.8 %copy-start.31 = (f32[3,4]{1,0:T(4,128)S(1)}, f32[3,4]{1,0:T(4,128)}, u32[]{:S(2)}) copy-start(f32[3,4]{1,0:T(4,128)} %param.12) | copy-start | bytes 148
  0.7 11.3 %copy-start.32 = (f32[3,3]{1,0:T(4,128)S(1)}, f32[3,3]{1,0:T(4,128)}, u32[]{:S(2)}) copy-start(f32[3,3]{1,0:T(4,128)} %param.13) | copy-start | bytes 112
  0.7 12.0 %copy-start.28 = (f32[3,3,3,9]{3,2,1,0:T(4,128)S(1)}, f32[3,3,3,9]{3,2,1,0:T(4,128)}, u32[]{:S(2)}) copy-start(f32[3,3,3,9]{3,2,1,0:T(4,128)} %param.11) | copy-start | bytes 2920
  7.8 5.5 %collective-permute-start = (bf16[513,16,128]{2,1,0:T(8,128)(2,1)}, bf16[513,16,128]{2,1,0:T(8,128)(2,1)S(1)}, u32[]{:S(2)}, u32[]{:S(2)}) collective-permute-start(bf16[513,16,128]{2,1,0:T(8,128)(2,1)} %halo_rows.1), channel_id=1, source_target_pairs={{0,1},{1,0},{2,3},{3,2},{4,5},{5,4},{6,7},{7,6},{8,9},{9,8},{10,11... | collective-permute-start | bytes 6303752 | tf_op jit(solution)/shard_map/ppermute | solution.py:603
  8.3 5.1 %collective-permute-start.1 = (s32[16,128]{1,0:T(8,128)S(1)}, s32[16,128]{1,0:T(8,128)S(1)}, u32[]{:S(2)}, u32[]{:S(2)}) collective-permute-start(s32[16,128]{1,0:T(8,128)S(1)} %copy-done.29), channel_id=1, source_target_pairs={{0,1},{1,0},{2,3},{3,2},{4,5},{5,4},{6,7},{7,6},{8,9},{9,8},{10,11... | collective-permute-start | bytes 24584 | tf_op jit(solution)/shard_map/ppermute | solution.py:602
  45.7 3.5 %copy-start = (bf16[16,528,128]{2,1,0:T(8,128)(2,1)S(1)}, bf16[16,528,128]{2,1,0:T(8,128)(2,1)}, u32[]{:S(2)}) copy-start(bf16[16,528,128]{2,1,0:T(8,128)(2,1)} %encode.1.enc_ref.value_ref) | copy-start | bytes 6488068
  45.8 3.5 %copy-start.1 = (s32[512]{0:T(512)S(1)}, s32[512]{0:T(512)}, u32[]{:S(2)}) copy-start(s32[512]{0:T(512)} %param.9) | copy-start | bytes 6148
  47.2 2.1 collective-permute-start.2
  50.6 15.1 %collective-permute-start.3 = (bf16[1,256,512]{2,1,0:T(8,128)(2,1)S(1)}, bf16[1,256,512]{2,1,0:T(8,128)(2,1)S(1)}, u32[]{:S(2)}, u32[]{:S(2)}) collective-permute-start(bf16[1,256,512]{2,1,0:T(8,128)(2,1)S(1)} %bitcast.16), channel_id=1, source_target_pairs={{0,8},{2,10},{4,12},{6,14},{8,0},{10,2},{12,4},{14,6},{16,24},{18,... | collective-permute-start | bytes 786440 | tf_op jit(solution)/shard_map/ppermute | solution.py:559
  53.6 26.7 %collective-permute-start.19 = (bf16[1,256,512]{2,1,0:T(8,128)(2,1)S(1)}, bf16[1,256,512]{2,1,0:T(8,128)(2,1)S(1)}, u32[]{:S(2)}, u32[]{:S(2)}) collective-permute-start(bf16[1,256,512]{2,1,0:T(8,128)(2,1)S(1)} %bitcast.17), channel_id=1, source_target_pairs={{0,16},{2,18},{4,20},{6,22},{8,24},{10,26},{12,28},{14,30},{16,0},... | collective-permute-start | bytes 786440 | tf_op jit(solution)/shard_map/ppermute | solution.py:559
  56.2 24.1 %collective-permute-start.21 = (bf16[1,272,512]{2,1,0:T(8,128)(2,1)S(1)}, bf16[1,272,512]{2,1,0:T(8,128)(2,1)S(1)}, u32[]{:S(2)}, u32[]{:S(2)}) collective-permute-start(bf16[1,272,512]{2,1,0:T(8,128)(2,1)S(1)} %bitcast.13), channel_id=1, source_target_pairs={{0,16},{2,18},{4,20},{6,22},{8,24},{10,26},{12,28},{14,30},{16,0},... | collective-permute-start | bytes 835592 | tf_op jit(solution)/shard_map/ppermute | solution.py:559
  65.8 90.0 %copy-start.13 = (bf16[2,256,512]{2,1,0:T(8,128)(2,1)}, bf16[2,256,512]{2,1,0:T(8,128)(2,1)S(1)}, u32[]{:S(2)}) copy-start(bf16[2,256,512]{2,1,0:T(8,128)(2,1)S(1)} %pad_maximum_fusion.1.refs_0_.refs_4_) | copy-start | bytes 1572868
  65.8 29.2 %collective-permute-start.11 = (bf16[2,256,512]{2,1,0:T(8,128)(2,1)S(1)}, bf16[2,256,512]{2,1,0:T(8,128)(2,1)S(1)}, u32[]{:S(2)}, u32[]{:S(2)}) collective-permute-start(bf16[2,256,512]{2,1,0:T(8,128)(2,1)S(1)} %pad_maximum_fusion.1.refs_0_.refs_4_), channel_id=1, source_target_pairs={{0,4},{2,6},{4,0},{6,2},{8,12},{10,14},{12,8},{14,10},{16,20},{18,... | collective-permute-start | bytes 1572872 | tf_op jit(solution)/shard_map/ppermute | solution.py:559
  67.5 16.3 %collective-permute-start.4 = (bf16[1,272,512]{2,1,0:T(8,128)(2,1)S(1)}, bf16[1,272,512]{2,1,0:T(8,128)(2,1)S(1)}, u32[]{:S(2)}, u32[]{:S(2)}) collective-permute-start(bf16[1,272,512]{2,1,0:T(8,128)(2,1)S(1)} %bitcast.14), channel_id=1, source_target_pairs={{0,8},{2,10},{4,12},{6,14},{8,0},{10,2},{12,4},{14,6},{16,24},{18,... | collective-permute-start | bytes 835592 | tf_op jit(solution)/shard_map/ppermute | solution.py:559
  80.3 14.7 %collective-permute-start.22 = (bf16[1,272,512]{2,1,0:T(8,128)(2,1)S(1)}, bf16[1,272,512]{2,1,0:T(8,128)(2,1)S(1)}, u32[]{:S(2)}, u32[]{:S(2)}) collective-permute-start(bf16[1,272,512]{2,1,0:T(8,128)(2,1)S(1)} %collective-permute-done.21), channel_id=1, source_target_pairs={{0,8},{2,10},{4,12},{6,14},{8,0},{10,2},{12,4},{14,6},{16,24},{18,... | collective-permute-start | bytes 835592 | tf_op jit(solution)/shard_map/ppermute | solution.py:559
  80.3 13.2 %collective-permute-start.20 = (bf16[1,256,512]{2,1,0:T(8,128)(2,1)S(1)}, bf16[1,256,512]{2,1,0:T(8,128)(2,1)S(1)}, u32[]{:S(2)}, u32[]{:S(2)}) collective-permute-start(bf16[1,256,512]{2,1,0:T(8,128)(2,1)S(1)} %collective-permute-done.19), channel_id=1, source_target_pairs={{0,8},{2,10},{4,12},{6,14},{8,0},{10,2},{12,4},{14,6},{16,24},{18,... | collective-permute-start | bytes 786440 | tf_op jit(solution)/shard_map/ppermute | solution.py:559
  82.3 13.3 %collective-permute-start.7 = (bf16[2,256,512]{2,1,0:T(8,128)(2,1)S(1)}, bf16[2,256,512]{2,1,0:T(8,128)(2,1)S(1)}, u32[]{:S(2)}, u32[]{:S(2)}) collective-permute-start(bf16[2,256,512]{2,1,0:T(8,128)(2,1)S(1)} %pad_maximum_fusion.1.refs_0_.refs_4_), channel_id=1, source_target_pairs={{0,2},{2,0},{4,6},{6,4},{8,10},{10,8},{12,14},{14,12},{16,18},{18,... | collective-permute-start | bytes 1572872 | tf_op jit(solution)/shard_map/ppermute | solution.py:559
  83.9 71.9 %copy-start.9 = (bf16[2,272,512]{2,1,0:T(8,128)(2,1)}, bf16[2,272,512]{2,1,0:T(8,128)(2,1)S(1)}, u32[]{:S(2)}) copy-start(bf16[2,272,512]{2,1,0:T(8,128)(2,1)S(1)} %pad_maximum_fusion.refs_1_.refs_5_) | copy-start | bytes 1671172
  83.9 14.5 %collective-permute-start.12 = (bf16[2,272,512]{2,1,0:T(8,128)(2,1)S(1)}, bf16[2,272,512]{2,1,0:T(8,128)(2,1)S(1)}, u32[]{:S(2)}, u32[]{:S(2)}) collective-permute-start(bf16[2,272,512]{2,1,0:T(8,128)(2,1)S(1)} %pad_maximum_fusion.refs_1_.refs_5_), channel_id=1, source_target_pairs={{0,4},{2,6},{4,0},{6,2},{8,12},{10,14},{12,8},{14,10},{16,20},{18,... | collective-permute-start | bytes 1671176 | tf_op jit(solution)/shard_map/ppermute | solution.py:559
  93.4 15.6 %collective-permute-start.8 = (bf16[2,272,512]{2,1,0:T(8,128)(2,1)S(1)}, bf16[2,272,512]{2,1,0:T(8,128)(2,1)S(1)}, u32[]{:S(2)}, u32[]{:S(2)}) collective-permute-start(bf16[2,272,512]{2,1,0:T(8,128)(2,1)S(1)} %pad_maximum_fusion.refs_1_.refs_5_), channel_id=1, source_target_pairs={{0,2},{2,0},{4,6},{6,4},{8,10},{10,8},{12,14},{14,12},{16,18},{18,... | collective-permute-start | bytes 1671176 | tf_op jit(solution)/shard_map/ppermute | solution.py:559
  94.9 2.2 collective-permute-start.5
  95.0 60.8 %copy-start.22 = (bf16[2,256,512]{2,1,0:T(8,128)(2,1)}, bf16[2,256,512]{2,1,0:T(8,128)(2,1)S(1)}, u32[]{:S(2)}) copy-start(bf16[2,256,512]{2,1,0:T(8,128)(2,1)S(1)} %collective-permute-done.11.refs_8_.refs_12_) | copy-start | bytes 1572868
  95.0 14.0 %collective-permute-start.6 = (bf16[2,272,512]{2,1,0:T(8,128)(2,1)S(1)}, bf16[2,272,512]{2,1,0:T(8,128)(2,1)S(1)}, u32[]{:S(2)}, u32[]{:S(2)}) collective-permute-start(bf16[2,272,512]{2,1,0:T(8,128)(2,1)S(1)} %pad_maximum_fusion.refs_1_.refs_5_), channel_id=1, source_target_pairs={{0,1},{1,0},{2,3},{3,2},{4,5},{5,4},{6,7},{7,6},{8,9},{9,8},{10,11... | collective-permute-start | bytes 1671176 | tf_op jit(solution)/shard_map/ppermute | solution.py:582
  95.5 70.7 %copy-start.5 = (bf16[2,256,512]{2,1,0:T(8,128)(2,1)}, bf16[2,256,512]{2,1,0:T(8,128)(2,1)S(1)}, u32[]{:S(2)}) copy-start(bf16[2,256,512]{2,1,0:T(8,128)(2,1)S(1)} %constant_dynamic-update-slice_fusion.refs_16_.refs_3_.refs_20_) | copy-start | bytes 1572868
  95.6 49.2 %copy-start.23 = (bf16[2,256,512]{2,1,0:T(8,128)(2,1)}, bf16[2,256,512]{2,1,0:T(8,128)(2,1)S(1)}, u32[]{:S(2)}) copy-start(bf16[2,256,512]{2,1,0:T(8,128)(2,1)S(1)} %collective-permute-done.7.refs_4_.refs_8_) | copy-start | bytes 1572868
  95.6 15.0 %collective-permute-start.29 = (bf16[2,256,512]{2,1,0:T(8,128)(2,1)S(1)}, bf16[2,256,512]{2,1,0:T(8,128)(2,1)}, u32[]{:S(2)}, u32[]{:S(2)}) collective-permute-start(bf16[2,256,512]{2,1,0:T(8,128)(2,1)S(1)} %constant_dynamic-update-slice_fusion.refs_16_.refs_3_.refs_20_), channel_id=1, source_target_pairs={{0,4},{2,6},{4,0},{6,2},{8,12},{10,14},{12,8},{14,10},{16,20},{18,... | collective-permute-start | bytes 1572872 | tf_op jit(solution)/shard_map/ppermute | solution.py:559
  97.1 69.1 %copy-start.4 = (bf16[2,272,512]{2,1,0:T(8,128)(2,1)}, bf16[2,272,512]{2,1,0:T(8,128)(2,1)S(1)}, u32[]{:S(2)}) copy-start(bf16[2,272,512]{2,1,0:T(8,128)(2,1)S(1)} %constant_dynamic-update-slice_fusion.2.refs_17_.refs_4_.refs_21_) | copy-start | bytes 1671172
  97.2 1.8 copy-start.24
  97.2 24.7 %collective-permute-start.30 = (bf16[2,272,512]{2,1,0:T(8,128)(2,1)S(1)}, bf16[2,272,512]{2,1,0:T(8,128)(2,1)S(1)}, u32[]{:S(2)}, u32[]{:S(2)}) collective-permute-start(bf16[2,272,512]{2,1,0:T(8,128)(2,1)S(1)} %constant_dynamic-update-slice_fusion.2.refs_17_.refs_4_.refs_21_), channel_id=1, source_target_pairs={{0,4},{2,6},{4,0},{6,2},{8,12},{10,14},{12,8},{14,10},{16,20},{18,... | collective-permute-start | bytes 1671176 | tf_op jit(solution)/shard_map/ppermute | solution.py:559
  98.3 57.4 %copy-start.14 = (bf16[2,272,512]{2,1,0:T(8,128)(2,1)}, bf16[2,272,512]{2,1,0:T(8,128)(2,1)S(1)}, u32[]{:S(2)}) copy-start(bf16[2,272,512]{2,1,0:T(8,128)(2,1)S(1)} %collective-permute-done.12.refs_9_.refs_13_) | copy-start | bytes 1671172
  98.3 22.0 %collective-permute-start.25 = (bf16[2,256,512]{2,1,0:T(8,128)(2,1)S(1)}, bf16[2,256,512]{2,1,0:T(8,128)(2,1)}, u32[]{:S(2)}, u32[]{:S(2)}) collective-permute-start(bf16[2,256,512]{2,1,0:T(8,128)(2,1)S(1)} %constant_dynamic-update-slice_fusion.refs_16_.refs_3_.refs_20_), channel_id=1, source_target_pairs={{0,2},{2,0},{4,6},{6,4},{8,10},{10,8},{12,14},{14,12},{16,18},{18,... | collective-permute-start | bytes 1572872 | tf_op jit(solution)/shard_map/ppermute | solution.py:559
  109.0 46.8 %copy-start.15 = (bf16[2,272,512]{2,1,0:T(8,128)(2,1)}, bf16[2,272,512]{2,1,0:T(8,128)(2,1)S(1)}, u32[]{:S(2)}) copy-start(bf16[2,272,512]{2,1,0:T(8,128)(2,1)S(1)} %collective-permute-done.8.refs_5_.refs_9_) | copy-start | bytes 1671172
  109.0 12.8 %collective-permute-start.23 = (bf16[2,256,512]{2,1,0:T(8,128)(2,1)S(1)}, bf16[2,256,512]{2,1,0:T(8,128)(2,1)S(1)}, u32[]{:S(2)}, u32[]{:S(2)}) collective-permute-start(bf16[2,256,512]{2,1,0:T(8,128)(2,1)S(1)} %constant_dynamic-update-slice_fusion.refs_16_.refs_3_.refs_20_), channel_id=1, source_target_pairs={{0,1},{1,0},{2,3},{3,2},{4,5},{5,4},{6,7},{7,6},{8,9},{9,8},{10,11... | collective-permute-start | bytes 1572872 | tf_op jit(solution)/shard_map/ppermute | solution.py:582
  109.0 46.8 %copy-start.16 = (bf16[2,272,512]{2,1,0:T(8,128)(2,1)}, bf16[2,272,512]{2,1,0:T(8,128)(2,1)S(1)}, u32[]{:S(2)}) copy-start(bf16[2,272,512]{2,1,0:T(8,128)(2,1)S(1)} %collective-permute-done.6.refs_3_.refs_7_) | copy-start | bytes 1671172
  109.0 23.2 %collective-permute-start.26 = (bf16[2,272,512]{2,1,0:T(8,128)(2,1)S(1)}, bf16[2,272,512]{2,1,0:T(8,128)(2,1)S(1)}, u32[]{:S(2)}, u32[]{:S(2)}) collective-permute-start(bf16[2,272,512]{2,1,0:T(8,128)(2,1)S(1)} %constant_dynamic-update-slice_fusion.2.refs_17_.refs_4_.refs_21_), channel_id=1, source_target_pairs={{0,2},{2,0},{4,6},{6,4},{8,10},{10,8},{12,14},{14,12},{16,18},{18,... | collective-permute-start | bytes 1671176 | tf_op jit(solution)/shard_map/ppermute | solution.py:559
  110.6 21.6 %collective-permute-start.24 = (bf16[2,272,512]{2,1,0:T(8,128)(2,1)S(1)}, bf16[2,272,512]{2,1,0:T(8,128)(2,1)S(1)}, u32[]{:S(2)}, u32[]{:S(2)}) collective-permute-start(bf16[2,272,512]{2,1,0:T(8,128)(2,1)S(1)} %constant_dynamic-update-slice_fusion.2.refs_17_.refs_4_.refs_21_), channel_id=1, source_target_pairs={{0,1},{1,0},{2,3},{3,2},{4,5},{5,4},{6,7},{7,6},{8,9},{9,8},{10,11... | collective-permute-start | bytes 1671176 | tf_op jit(solution)/shard_map/ppermute | solution.py:582
  120.3 23.8 %collective-permute-start.16 = (bf16[2,272,512]{2,1,0:T(8,128)(2,1)S(1)}, bf16[2,272,512]{2,1,0:T(8,128)(2,1)S(1)}, u32[]{:S(2)}, u32[]{:S(2)}) collective-permute-start(bf16[2,272,512]{2,1,0:T(8,128)(2,1)S(1)} %collective-permute-done.12.refs_9_.refs_13_), channel_id=1, source_target_pairs={{0,2},{2,0},{4,6},{6,4},{8,10},{10,8},{12,14},{14,12},{16,18},{18,... | collective-permute-start | bytes 1671176 | tf_op jit(solution)/shard_map/ppermute | solution.py:559
  121.8 44.4 %copy-start.10 = (bf16[2,256,512]{2,1,0:T(8,128)(2,1)}, bf16[2,256,512]{2,1,0:T(8,128)(2,1)S(1)}, u32[]{:S(2)}) copy-start(bf16[2,256,512]{2,1,0:T(8,128)(2,1)S(1)} %collective-permute-done.23.refs_18_.refs_5_.refs_22_) | copy-start | bytes 1572868
  121.9 10.8 %collective-permute-start.13 = (bf16[2,256,512]{2,1,0:T(8,128)(2,1)S(1)}, bf16[2,256,512]{2,1,0:T(8,128)(2,1)}, u32[]{:S(2)}, u32[]{:S(2)}) collective-permute-start(bf16[2,256,512]{2,1,0:T(8,128)(2,1)S(1)} %collective-permute-done.11.refs_8_.refs_12_), channel_id=1, source_target_pairs={{0,1},{1,0},{2,3},{3,2},{4,5},{5,4},{6,7},{7,6},{8,9},{9,8},{10,11... | collective-permute-start | bytes 1572872 | tf_op jit(solution)/shard_map/ppermute | solution.py:582
  121.9 44.4 %copy-start.6 = (bf16[2,272,512]{2,1,0:T(8,128)(2,1)}, bf16[2,272,512]{2,1,0:T(8,128)(2,1)S(1)}, u32[]{:S(2)}) copy-start(bf16[2,272,512]{2,1,0:T(8,128)(2,1)S(1)} %collective-permute-done.30.refs_25_.refs_12_.refs_29_) | copy-start | bytes 1671172
  121.9 14.3 %collective-permute-start.15 = (bf16[2,256,512]{2,1,0:T(8,128)(2,1)S(1)}, bf16[2,256,512]{2,1,0:T(8,128)(2,1)S(1)}, u32[]{:S(2)}, u32[]{:S(2)}) collective-permute-start(bf16[2,256,512]{2,1,0:T(8,128)(2,1)S(1)} %collective-permute-done.7.refs_4_.refs_8_), channel_id=1, source_target_pairs={{0,4},{2,6},{4,0},{6,2},{8,12},{10,14},{12,8},{14,10},{16,20},{18,... | collective-permute-start | bytes 1572872 | tf_op jit(solution)/shard_map/ppermute | solution.py:559
  132.2 34.1 %copy-start.7 = (bf16[2,272,512]{2,1,0:T(8,128)(2,1)}, bf16[2,272,512]{2,1,0:T(8,128)(2,1)S(1)}, u32[]{:S(2)}) copy-start(bf16[2,272,512]{2,1,0:T(8,128)(2,1)S(1)} %collective-permute-done.26.refs_21_.refs_8_.refs_25_) | copy-start | bytes 1671172
  132.2 11.9 %collective-permute-start.9 = (bf16[2,256,512]{2,1,0:T(8,128)(2,1)S(1)}, bf16[2,256,512]{2,1,0:T(8,128)(2,1)S(1)}, u32[]{:S(2)}, u32[]{:S(2)}) collective-permute-start(bf16[2,256,512]{2,1,0:T(8,128)(2,1)S(1)} %collective-permute-done.7.refs_4_.refs_8_), channel_id=1, source_target_pairs={{0,1},{1,0},{2,3},{3,2},{4,5},{5,4},{6,7},{7,6},{8,9},{9,8},{10,11... | collective-permute-start | bytes 1572872 | tf_op jit(solution)/shard_map/ppermute | solution.py:582
  132.2 12.5 %copy-start.8 = (bf16[2,272,512]{2,1,0:T(8,128)(2,1)}, bf16[2,272,512]{2,1,0:T(8,128)(2,1)S(1)}, u32[]{:S(2)}) copy-start(bf16[2,272,512]{2,1,0:T(8,128)(2,1)S(1)} %collective-permute-done.24.refs_19_.refs_6_.refs_23_) | copy-start | bytes 1671172
  132.2 12.4 %collective-permute-start.14 = (bf16[2,272,512]{2,1,0:T(8,128)(2,1)S(1)}, bf16[2,272,512]{2,1,0:T(8,128)(2,1)S(1)}, u32[]{:S(2)}, u32[]{:S(2)}) collective-permute-start(bf16[2,272,512]{2,1,0:T(8,128)(2,1)S(1)} %collective-permute-done.12.refs_9_.refs_13_), channel_id=1, source_target_pairs={{0,1},{1,0},{2,3},{3,2},{4,5},{5,4},{6,7},{7,6},{8,9},{9,8},{10,11... | collective-permute-start | bytes 1671176 | tf_op jit(solution)/shard_map/ppermute | solution.py:582
  132.7 12.0 %collective-permute-start.10 = (bf16[2,272,512]{2,1,0:T(8,128)(2,1)S(1)}, bf16[2,272,512]{2,1,0:T(8,128)(2,1)S(1)}, u32[]{:S(2)}, u32[]{:S(2)}) collective-permute-start(bf16[2,272,512]{2,1,0:T(8,128)(2,1)S(1)} %collective-permute-done.8.refs_5_.refs_9_), channel_id=1, source_target_pairs={{0,1},{1,0},{2,3},{3,2},{4,5},{5,4},{6,7},{7,6},{8,9},{9,8},{10,11... | collective-permute-start | bytes 1671176 | tf_op jit(solution)/shard_map/ppermute | solution.py:582
  136.2 18.0 %copy-start.25 = (bf16[2,256,512]{2,1,0:T(8,128)(2,1)}, bf16[2,256,512]{2,1,0:T(8,128)(2,1)S(1)}, u32[]{:S(2)}) copy-start(bf16[2,256,512]{2,1,0:T(8,128)(2,1)S(1)} %collective-permute-done.15.refs_12_.refs_16_) | copy-start | bytes 1572868
  136.2 17.4 %collective-permute-start.34 = (bf16[2,272,512]{2,1,0:T(8,128)(2,1)S(1)}, bf16[2,272,512]{2,1,0:T(8,128)(2,1)}, u32[]{:S(2)}, u32[]{:S(2)}) collective-permute-start(bf16[2,272,512]{2,1,0:T(8,128)(2,1)S(1)} %collective-permute-done.30.refs_25_.refs_12_.refs_29_), channel_id=1, source_target_pairs={{0,2},{2,0},{4,6},{6,4},{8,10},{10,8},{12,14},{14,12},{16,18},{18,... | collective-permute-start | bytes 1671176 | tf_op jit(solution)/shard_map/ppermute | solution.py:559
  144.1 11.7 %copy-start.17 = (bf16[2,272,512]{2,1,0:T(8,128)(2,1)}, bf16[2,272,512]{2,1,0:T(8,128)(2,1)S(1)}, u32[]{:S(2)}) copy-start(bf16[2,272,512]{2,1,0:T(8,128)(2,1)S(1)} %collective-permute-done.16.refs_13_.refs_17_) | copy-start | bytes 1671172
  144.1 10.1 %collective-permute-start.18 = (bf16[2,272,512]{2,1,0:T(8,128)(2,1)S(1)}, bf16[2,272,512]{2,1,0:T(8,128)(2,1)S(1)}, u32[]{:S(2)}, u32[]{:S(2)}) collective-permute-start(bf16[2,272,512]{2,1,0:T(8,128)(2,1)S(1)} %collective-permute-done.16.refs_13_.refs_17_), channel_id=1, source_target_pairs={{0,1},{1,0},{2,3},{3,2},{4,5},{5,4},{6,7},{7,6},{8,9},{9,8},{10,11... | collective-permute-start | bytes 1671176 | tf_op jit(solution)/shard_map/ppermute | solution.py:582
  144.1 10.0 %copy-start.26 = (bf16[2,256,512]{2,1,0:T(8,128)(2,1)}, bf16[2,256,512]{2,1,0:T(8,128)(2,1)S(1)}, u32[]{:S(2)}) copy-start(bf16[2,256,512]{2,1,0:T(8,128)(2,1)S(1)} %collective-permute-done.9.refs_6_.refs_10_) | copy-start | bytes 1572868
  144.1 9.5 %collective-permute-start.17 = (bf16[2,256,512]{2,1,0:T(8,128)(2,1)S(1)}, bf16[2,256,512]{2,1,0:T(8,128)(2,1)S(1)}, u32[]{:S(2)}, u32[]{:S(2)}) collective-permute-start(bf16[2,256,512]{2,1,0:T(8,128)(2,1)S(1)} %collective-permute-done.15.refs_12_.refs_16_), channel_id=1, source_target_pairs={{0,1},{1,0},{2,3},{3,2},{4,5},{5,4},{6,7},{7,6},{8,9},{9,8},{10,11... | collective-permute-start | bytes 1572872 | tf_op jit(solution)/shard_map/ppermute | solution.py:582
  144.6 11.2 %copy-start.18 = (bf16[2,272,512]{2,1,0:T(8,128)(2,1)}, bf16[2,272,512]{2,1,0:T(8,128)(2,1)S(1)}, u32[]{:S(2)}) copy-start(bf16[2,272,512]{2,1,0:T(8,128)(2,1)S(1)} %collective-permute-done.14.refs_11_.refs_15_) | copy-start | bytes 1671172
  144.6 22.5 %collective-permute-start.31 = (bf16[2,256,512]{2,1,0:T(8,128)(2,1)}, bf16[2,256,512]{2,1,0:T(8,128)(2,1)}, u32[]{:S(2)}, u32[]{:S(2)}) collective-permute-start(bf16[2,256,512]{2,1,0:T(8,128)(2,1)} %collective-permute-done.29.refs_24_.refs_11_.refs_28_), channel_id=1, source_target_pairs={{0,1},{1,0},{2,3},{3,2},{4,5},{5,4},{6,7},{7,6},{8,9},{9,8},{10,11... | collective-permute-start | bytes 1572872 | tf_op jit(solution)/shard_map/ppermute | solution.py:582
  144.7 9.4 %copy-start.19 = (bf16[2,272,512]{2,1,0:T(8,128)(2,1)}, bf16[2,272,512]{2,1,0:T(8,128)(2,1)S(1)}, u32[]{:S(2)}) copy-start(bf16[2,272,512]{2,1,0:T(8,128)(2,1)S(1)} %collective-permute-done.10.refs_7_.refs_11_) | copy-start | bytes 1671172
  144.7 21.5 %collective-permute-start.33 = (bf16[2,256,512]{2,1,0:T(8,128)(2,1)}, bf16[2,256,512]{2,1,0:T(8,128)(2,1)S(1)}, u32[]{:S(2)}, u32[]{:S(2)}) collective-permute-start(bf16[2,256,512]{2,1,0:T(8,128)(2,1)} %collective-permute-done.25.refs_20_.refs_7_.refs_24_), channel_id=1, source_target_pairs={{0,4},{2,6},{4,0},{6,2},{8,12},{10,14},{12,8},{14,10},{16,20},{18,... | collective-permute-start | bytes 1572872 | tf_op jit(solution)/shard_map/ppermute | solution.py:559
  153.7 14.8 %collective-permute-start.32 = (bf16[2,272,512]{2,1,0:T(8,128)(2,1)S(1)}, bf16[2,272,512]{2,1,0:T(8,128)(2,1)}, u32[]{:S(2)}, u32[]{:S(2)}) collective-permute-start(bf16[2,272,512]{2,1,0:T(8,128)(2,1)S(1)} %collective-permute-done.30.refs_25_.refs_12_.refs_29_), channel_id=1, source_target_pairs={{0,1},{1,0},{2,3},{3,2},{4,5},{5,4},{6,7},{7,6},{8,9},{9,8},{10,11... | collective-permute-start | bytes 1671176 | tf_op jit(solution)/shard_map/ppermute | solution.py:582
  153.7 14.8 %collective-permute-start.28 = (bf16[2,272,512]{2,1,0:T(8,128)(2,1)S(1)}, bf16[2,272,512]{2,1,0:T(8,128)(2,1)}, u32[]{:S(2)}, u32[]{:S(2)}) collective-permute-start(bf16[2,272,512]{2,1,0:T(8,128)(2,1)S(1)} %collective-permute-done.26.refs_21_.refs_8_.refs_25_), channel_id=1, source_target_pairs={{0,1},{1,0},{2,3},{3,2},{4,5},{5,4},{6,7},{7,6},{8,9},{9,8},{10,11... | collective-permute-start | bytes 1671176 | tf_op jit(solution)/shard_map/ppermute | solution.py:582
  155.3 13.2 %collective-permute-start.36 = (bf16[2,272,512]{2,1,0:T(8,128)(2,1)}, bf16[2,272,512]{2,1,0:T(8,128)(2,1)}, u32[]{:S(2)}, u32[]{:S(2)}) collective-permute-start(bf16[2,272,512]{2,1,0:T(8,128)(2,1)} %collective-permute-done.34.refs_29_.refs_16_.refs_33_), channel_id=1, source_target_pairs={{0,1},{1,0},{2,3},{3,2},{4,5},{5,4},{6,7},{7,6},{8,9},{9,8},{10,11... | collective-permute-start | bytes 1671176 | tf_op jit(solution)/shard_map/ppermute | solution.py:582
  166.3 2.2 collective-permute-start.27
  167.1 2.1 collective-permute-start.35
  170.1 58.1 %all-to-all-start = ((bf16[16,528,128]{2,1,0:T(8,128)(2,1)}), bf16[16,528,128]{2,1,0:T(8,128)(2,1)S(1)}, u32[]{:S(2)}, u32[]{:S(2)}) async-start(bf16[16,528,128]{2,1,0:T(8,128)(2,1)} %after.3), calls=%async_computation | async-start | bytes 4325376 | tf_op jit(solution)/shard_map/all_to_all | solution.py:628
  (8 other events, 7.3 us)

commit v4 on v3

--- a/solution.py
+++ b/solution.py
@@ -322,11 +322,14 @@
         low_ref[base + HALF : base + PANEL, base + HALF : base + PANEL] += dot_nt(
             part[HALF:], part[HALF:]
         )
-    for refs in pieces:
-        for ref in (refs[1], refs[3]):
-            part = ref[0, HALF:, 0:EDGE].astype(F32)
-            part = part[0:1] + part[1:2] + part[2:3]
-            power_ref[...] += jnp.broadcast_to(part, power_ref.shape)
+
+    @pl.when(pl.program_id(1) == 0)
+    def _():
+        for refs in pieces:
+            for ref in (refs[1], refs[3]):
+                part = ref[0, HALF:, 0:EDGE].astype(F32)
+                part = part[0:1] + part[1:2] + part[2:3]
+                power_ref[...] += jnp.broadcast_to(part, power_ref.shape)
 
 
 def grouped(refs):
@@ -336,7 +339,7 @@
 def gram_kernel(tile_ref, *refs):
     pieces, (low_ref, power_ref) = refs[:-2], refs[-2:]
 
-    @pl.when(pl.program_id(0) == 0)
+    @pl.when(at_step(0, 0))
     def _():
         low_ref[...] = jnp.zeros(low_ref.shape, F32)
         power_ref[...] = jnp.zeros(power_ref.shape, F32)
@@ -345,19 +348,19 @@
 
 
 def factor_kernel(tile_ref, sums_ref, energy_ref, *refs, pairs_total, obs):
-    pieces, (low_ref, inv_ref, shift_ref) = refs[:-3], refs[-3:]
-
-    @pl.when(pl.program_id(0) == 0)
+    pieces, (low_ref, inv_ref, out_ref, shift_ref) = refs[:-4], refs[-4:]
+
+    @pl.when(at_step(0, 0))
     def _():
         low_ref[...] = sums_ref[...]
         shift_ref[...] = energy_ref[...]
 
     gram_step(tile_ref, grouped(pieces), low_ref, shift_ref)
 
-    @pl.when(pl.program_id(0) == pl.num_programs(0) - 1)
+    @pl.when(at_step(pl.num_programs(0) - 1, SPLIT - 1))
     def _():
         shift = 0.5 * (shift_ref[...] / pairs_total) / float(obs)
-        shift_ref[...] = shift
+        out_ref[0, 0] = shift[0, 0]
         factor(low_ref, inv_ref, shift, 1.0 / pairs_total)
 
 
@@ -407,12 +410,22 @@
         low_ref[EDGE * i : EDGE * (i + 1), EDGE * (i + 1) : EDGE * (i + 2)] = jnp.zeros((EDGE, EDGE), F32)
 
 
+SPLIT = 2
+
+
 def whole(shape):
-    return pl.BlockSpec(shape, lambda i: (0,) * len(shape))
+    return pl.BlockSpec(shape, lambda i, j: (0,) * len(shape))
 
 
 def piece_specs(pieces):
-    return [pl.BlockSpec((1,) + piece.shape[1:], lambda i: (i, 0, 0)) for piece in pieces]
+    return [
+        pl.BlockSpec((1, piece.shape[1], piece.shape[2] // SPLIT), lambda i, j: (i, 0, j))
+        for piece in pieces
+    ]
+
+
+def at_step(i, j):
+    return (pl.program_id(0) == i) & (pl.program_id(1) == j)
 
 
 SUMS = jax.ShapeDtypeStruct((2 * PANEL, 2 * PANEL), F32)
@@ -423,7 +436,7 @@
 def gram_part(tile_idx, pieces):
     return pl.pallas_call(
         gram_kernel,
-        grid=(pieces[0].shape[0],),
+        grid=(pieces[0].shape[0], SPLIT),
         in_specs=[pl.BlockSpec(memory_space=pltpu.SMEM)] + piece_specs(pieces),
         out_specs=[whole(SUMS.shape), whole(POWER.shape)],
         out_shape=[SUMS, POWER],
@@ -443,11 +456,20 @@
 
     return pl.pallas_call(
         body,
-        grid=(pieces[0].shape[0],),
+        grid=(pieces[0].shape[0], SPLIT),
         in_specs=[pl.BlockSpec(memory_space=pltpu.SMEM), whole(SUMS.shape), whole(POWER.shape)]
         + piece_specs(pieces),
-        out_specs=[whole(SUMS.shape), whole((2 * PANEL, EDGE)), whole(POWER.shape)],
-        out_shape=[SUMS, jax.ShapeDtypeStruct((2 * PANEL, EDGE), F32), POWER],
+        out_specs=[
+            whole(SUMS.shape),
+            whole((2 * PANEL, EDGE)),
+            pl.BlockSpec(memory_space=pltpu.SMEM),
+        ],
+        out_shape=[
+            SUMS,
+            jax.ShapeDtypeStruct((2 * PANEL, EDGE), F32),
+            jax.ShapeDtypeStruct((1, 1), F32),
+        ],
+        scratch_shapes=[pltpu.VMEM(POWER.shape, F32)],
         compiler_params=LIMIT,
         name="gram_factor",
     )(tile_idx, sums, energy, *pieces)
@@ -459,7 +481,7 @@
     own = chol_ref.shape[0]
     width = 2 * PANEL
 
-    @pl.when(step == 0)
+    @pl.when(at_step(0, 0))
     def _():
         sums_ref[...] = jnp.zeros(sums_ref.shape, F32)
 
@@ -495,7 +517,7 @@
     sums_ref[:, 0:PANEL] += dot_nt(picked, jnp.concatenate([b[0] for b in both], axis=1))
     sums_ref[:, PANEL:] += dot_nt(picked, jnp.concatenate([b[1] for b in both], axis=1))
 
-    @pl.when(step == pl.num_programs(0) - 1)
+    @pl.when(at_step(pl.num_programs(0) - 1, SPLIT - 1))
     def _():
         sums_ref[...] = sums_ref[...] * (1.0 / pairs_total)
         for k in range(width // EDGE):
@@ -525,7 +547,7 @@
 
     return pl.pallas_call(
         body,
-        grid=(pieces[0].shape[0],),
+        grid=(pieces[0].shape[0], SPLIT),
         in_specs=[pl.BlockSpec(memory_space=pltpu.SMEM)]
         + [whole(x.shape) for x in (enc, low, inv)]
         + piece_specs(pieces),
@@ -645,7 +667,7 @@
     factor_rows, whitened = whiten_rows(
         info, own_enc, low, inv, chunks[0] + chunks[1], pairs_total
     )
-    return (factor_rows[None], whitened[None], shift[0, 0])
+    return (factor_rows[None], whitened[None], shift.reshape(()))
 
 
 def solution(mesh):

time: 248 us -> 247 us (level)
  transfers between devices with their start and end apart: 38 -> 38, of which waited for: 12 -> 12; matrix products, arithmetic and copies ran while one was open for 2% -> 1% of each run, Pallas kernels for 24% -> 24%
where the time goes in v4:
time: 247 us
  Pallas kernels  117 us (47%)
  waiting for transfers between devices  80.3 us (33%)
  starting transfers between devices  33.9 us (14%)
  local copies, waits for them, and re-layouts  9.21 us (4%)
  between operations  4.92 us (2%)
    ppermute x18, waiting for transfers between devices, across(): return [lax.ppermute(x, 'dp', pairs) for x in arrays]  76.6 us
    pallas_call x1, Pallas kernels, gram_factor(): pl.pallas_call(body, grid=(pieces[0].shape[0], SPLIT), in_specs=[pl.Block...  49.4 us
    pallas_call x1, Pallas kernels, encode(): pl.pallas_call(body, grid=(pl.cdiv(count, BLOCK),), in_specs=[smem, smem,...  30.5 us
    ppermute x18, starting transfers between devices, across(): return [lax.ppermute(x, 'dp', pairs) for x in arrays]  24.1 us
    pallas_call x1, Pallas kernels, whiten_rows(): pl.pallas_call(body, grid=(pieces[0].shape[0], SPLIT), in_specs=[pl.Block...  17.9 us
    pallas_call x1, Pallas kernels, gram_part(): pl.pallas_call(gram_kernel, grid=(pieces[0].shape[0], SPLIT), in_specs=[p...  10.5 us
    pallas_call x1, Pallas kernels, halo_rows(): pl.pallas_call(halo_kernel, grid_spec=pltpu.PrefetchScalarGridSpec(num_sc...  7.14 us
    unnamed x70, local copies, waits for them, and re-layouts  6.08 us
  transfers between devices with their start and end apart: 38, of which 12 were waited for; matrix products, arithmetic and copies ran while one was open for 1% of the time, Pallas kernels for 24%

profile of v4, /device:TPU:0, one launch (start us, length us, event | category | flops | bytes accessed | tf_op | source)
XLA Modules:
  0.0 246.6 jit_solution(16395400363473107819)
XLA Ops:
  0.7 7.1 %halo_rows.1 = bf16[513,16,128]{2,1,0:T(8,128)(2,1)} custom-call(s32[1]{0:T(128)} %bitcast.tile_ref.refs_0_, bf16[513,3,16,128]{3,2,1,0:T(8,128)(2,1)} %refs_5_.1), custom_call_target="tpu_custom_call" | custom-call | tf_op jit(solution)/shard_map/halo_rows/pallas_call | solution.py:37
  7.8 0.5 collective-permute-start
  8.3 0.1 collective-permute-start.1
  8.3 0.6 fusion
  11.4 0.6 reshape.19.refs_2_
  12.0 0.6 reshape.20.refs_3_
  12.6 0.7 reshape.18.refs_1_
  13.3 0.6 copy-done.30
  13.9 1.3 copy-done.21
  15.2 30.5 %encode.1.enc_ref.value_ref = bf16[16,528,128]{2,1,0:T(8,128)(2,1)} custom-call(s32[1]{0:T(128)} %bitcast.tile_ref.refs_0_, f32[243]{0:T(256)} %reshape.18.refs_1_, f32[12]{0:T(128)} %reshape.19.refs_2_, f32[9]{0:T(128)} %reshape.20.refs_3_, f32[3]{0:T(128)} %refs_4_.1, bf16[513,3,16,128]{3,2,1,0:T(8,128)(2,1)} %refs_5_.1, bf16[513,16,128]{2,1,0:T(8,128)(2,1)} %copy-done.21, ...), custom_call_target="tpu_custom_call" | custom-call | tf_op jit(solution)/shard_map/encode/pallas_call | solution.py:164
  45.7 1.4 dynamic-slice_select_fusion
  47.1 0.5 collective-permute-start.2
  47.7 1.6 collective-permute-done.2.near_ref
  49.2 1.4 pick_pairs.1
  50.6 2.9 %collective-permute-start.3 = (bf16[1,256,512]{2,1,0:T(8,128)(2,1)S(1)}, bf16[1,256,512]{2,1,0:T(8,128)(2,1)S(1)}, u32[]{:S(2)}, u32[]{:S(2)}) collective-permute-start(bf16[1,256,512]{2,1,0:T(8,128)(2,1)S(1)} %bitcast.16), channel_id=1, source_target_pairs={{0,8},{2,10},{4,12},{6,14},{8,0},{10,2},{12,4},{14,6},{16,24},{18,... | collective-permute-start | bytes 786440 | tf_op jit(solution)/shard_map/ppermute | solution.py:581
  53.5 2.6 %collective-permute-start.19 = (bf16[1,256,512]{2,1,0:T(8,128)(2,1)S(1)}, bf16[1,256,512]{2,1,0:T(8,128)(2,1)S(1)}, u32[]{:S(2)}, u32[]{:S(2)}) collective-permute-start(bf16[1,256,512]{2,1,0:T(8,128)(2,1)S(1)} %bitcast.17), channel_id=1, source_target_pairs={{0,16},{2,18},{4,20},{6,22},{8,24},{10,26},{12,28},{14,30},{16,0},... | collective-permute-start | bytes 786440 | tf_op jit(solution)/shard_map/ppermute | solution.py:581
  56.1 0.3 collective-permute-start.21
  56.4 9.2 %collective-permute-done.3 = bf16[1,256,512]{2,1,0:T(8,128)(2,1)S(1)} collective-permute-done((bf16[1,256,512]{2,1,0:T(8,128)(2,1)S(1)}, bf16[1,256,512]{2,1,0:T(8,128)(2,1)S(1)}, u32[]{:S(2)}, u32[]{:S(2)}) %collective-permute-start.3) | collective-permute-done | bytes 262176 | tf_op jit(solution)/shard_map/ppermute | solution.py:581
  65.7 0.1 pad_maximum_fusion.1.refs_0_.refs_4_
  65.7 1.7 collective-permute-start.11
  67.5 12.8 %collective-permute-done.21 = bf16[1,272,512]{2,1,0:T(8,128)(2,1)S(1)} collective-permute-done((bf16[1,272,512]{2,1,0:T(8,128)(2,1)S(1)}, bf16[1,272,512]{2,1,0:T(8,128)(2,1)S(1)}, u32[]{:S(2)}, u32[]{:S(2)}) %collective-permute-start.21) | collective-permute-done | bytes 278560 | tf_op jit(solution)/shard_map/ppermute | solution.py:581
  80.2 2.0 collective-permute-start.20
  82.2 1.5 collective-permute-start.7
  83.7 0.1 pad_maximum_fusion.refs_1_.refs_5_
  83.8 1.5 collective-permute-start.12
  85.3 8.1 %collective-permute-done.20 = bf16[1,256,512]{2,1,0:T(8,128)(2,1)S(1)} collective-permute-done((bf16[1,256,512]{2,1,0:T(8,128)(2,1)S(1)}, bf16[1,256,512]{2,1,0:T(8,128)(2,1)S(1)}, u32[]{:S(2)}, u32[]{:S(2)}) %collective-permute-start.20) | collective-permute-done | bytes 262176 | tf_op jit(solution)/shard_map/ppermute | solution.py:581
  93.4 1.5 collective-permute-start.8
  94.9 0.5 collective-permute-start.6
  95.5 1.5 collective-permute-start.29
  97.1 1.2 collective-permute-start.30
  98.3 0.6 collective-permute-start.25
  98.9 10.1 %collective-permute-done.8.refs_5_.refs_9_ = bf16[2,272,512]{2,1,0:T(8,128)(2,1)S(1)} collective-permute-done((bf16[2,272,512]{2,1,0:T(8,128)(2,1)S(1)}, bf16[2,272,512]{2,1,0:T(8,128)(2,1)S(1)}, u32[]{:S(2)}, u32[]{:S(2)}) %collective-permute-start.8) | collective-permute-done | bytes 557088 | tf_op jit(solution)/shard_map/ppermute | solution.py:581
  109.0 1.6 collective-permute-start.26
  110.5 0.2 collective-permute-start.24
  110.7 9.6 %collective-permute-done.25.refs_20_.refs_7_.refs_24_ = bf16[2,256,512]{2,1,0:T(8,128)(2,1)} collective-permute-done((bf16[2,256,512]{2,1,0:T(8,128)(2,1)S(1)}, bf16[2,256,512]{2,1,0:T(8,128)(2,1)}, u32[]{:S(2)}, u32[]{:S(2)}) %collective-permute-start.25) | collective-permute-done | bytes 524320 | tf_op jit(solution)/shard_map/ppermute | solution.py:581
  120.3 1.5 collective-permute-start.16
  121.8 1.5 collective-permute-start.15
  123.4 8.8 %collective-permute-done.26.refs_21_.refs_8_.refs_25_ = bf16[2,272,512]{2,1,0:T(8,128)(2,1)S(1)} collective-permute-done((bf16[2,272,512]{2,1,0:T(8,128)(2,1)S(1)}, bf16[2,272,512]{2,1,0:T(8,128)(2,1)S(1)}, u32[]{:S(2)}, u32[]{:S(2)}) %collective-permute-start.26) | collective-permute-done | bytes 557088 | tf_op jit(solution)/shard_map/ppermute | solution.py:581
  132.1 0.5 collective-permute-start.14
  132.6 0.1 collective-permute-start.10
  132.7 3.4 %collective-permute-done.15.refs_12_.refs_16_ = bf16[2,256,512]{2,1,0:T(8,128)(2,1)S(1)} collective-permute-done((bf16[2,256,512]{2,1,0:T(8,128)(2,1)S(1)}, bf16[2,256,512]{2,1,0:T(8,128)(2,1)S(1)}, u32[]{:S(2)}, u32[]{:S(2)}) %collective-permute-start.15) | collective-permute-done | bytes 524320 | tf_op jit(solution)/shard_map/ppermute | solution.py:581
  136.2 0.5 collective-permute-start.34
  136.7 7.4 %collective-permute-done.16.refs_13_.refs_17_ = bf16[2,272,512]{2,1,0:T(8,128)(2,1)S(1)} collective-permute-done((bf16[2,272,512]{2,1,0:T(8,128)(2,1)S(1)}, bf16[2,272,512]{2,1,0:T(8,128)(2,1)S(1)}, u32[]{:S(2)}, u32[]{:S(2)}) %collective-permute-start.16) | collective-permute-done | bytes 557088 | tf_op jit(solution)/shard_map/ppermute | solution.py:581
  144.1 0.5 collective-permute-start.17
  144.6 0.1 collective-permute-start.31
  144.7 1.6 collective-permute-start.33
  146.3 7.3 %collective-permute-done.34.refs_29_.refs_16_.refs_33_ = bf16[2,272,512]{2,1,0:T(8,128)(2,1)} collective-permute-done((bf16[2,272,512]{2,1,0:T(8,128)(2,1)S(1)}, bf16[2,272,512]{2,1,0:T(8,128)(2,1)}, u32[]{:S(2)}, u32[]{:S(2)}) %collective-permute-start.34) | collective-permute-done | bytes 557088 | tf_op jit(solution)/shard_map/ppermute | solution.py:581
  153.6 0.5 collective-permute-start.28
  154.1 0.3 copy-done.27
  154.4 0.8 copy-done.20
  155.2 0.5 collective-permute-start.36
  155.8 10.5 %gram_part.1 = (f32[1024,1024]{1,0:T(8,128)}, f32[8,128]{1,0:T(8,128)}) custom-call(s32[1]{0:T(128)} %bitcast.tile_ref.refs_0_, bf16[2,256,512]{2,1,0:T(8,128)(2,1)} %copy-done.13, bf16[2,272,512]{2,1,0:T(8,128)(2,1)} %copy-done.9, bf16[2,256,512]{2,1,0:T(8,128)(2,1)} %copy-done.24, bf16[2,272,512]{2,1,0:T(8,128)(2,1)} %copy-done.16, ...), custom_call_target="tpu_custom_call" | custom-call | flops 6442450944 | bytes 12845056 | tf_op jit(solution)/shard_map/gram_part/pallas_call | solution.py:437
  166.3 0.1 collective-permute-start.27
  166.4 0.7 copy-done.3
  167.1 0.0 collective-permute-start.35
  167.1 1.4 collective-permute-done.27.refs_22_.refs_9_.refs_26_
  168.5 0.7 collective-permute-done.35.refs_30_.refs_17_.refs_34_
  169.3 0.0 copy-done.11
  169.3 0.8 copy-done.12
  170.1 5.8 %all-to-all-start = ((bf16[16,528,128]{2,1,0:T(8,128)(2,1)}), bf16[16,528,128]{2,1,0:T(8,128)(2,1)S(1)}, u32[]{:S(2)}, u32[]{:S(2)}) async-start(bf16[16,528,128]{2,1,0:T(8,128)(2,1)} %after.3), calls=%async_computation | async-start | bytes 4325376 | tf_op jit(solution)/shard_map/all_to_all | solution.py:650
  177.1 0.6 stack.31.refs_0_
  177.7 49.4 %gram_factor.1 = (f32[1024,1024]{1,0:T(8,128)}, f32[1024,128]{1,0:T(8,128)}, f32[1,1]{1,0:T(1,128)}) custom-call(s32[1]{0:T(128)} %bitcast.tile_ref.refs_0_, f32[1024,1024]{1,0:T(8,128)} %get-tuple-element.14.refs_0_.refs_1_, f32[8,128]{1,0:T(8,128)} %get-tuple-element.15.refs_1_.refs_2_, bf16[2,256,512]{2,1,0:T(8,128)(2,1)} %copy-done.5, ...), custom_call_target="tpu_custom_call" | custom-call | tf_op jit(solution)/shard_map/gram_factor/pallas_call | solution.py:457
  227.1 1.4 copy-done.2
  228.5 17.9 %whiten_rows.1 = (f32[128,1024]{1,0:T(8,128)}, f32[128,1024]{1,0:T(8,128)}) custom-call(s32[5]{0:T(128)} %stack.31.refs_0_, bf16[16,528,128]{2,1,0:T(8,128)(2,1)} %copy-done.2, f32[1024,1024]{1,0:T(8,128)} %get-tuple-element.16.refs_2_, f32[1024,128]{1,0:T(8,128)} %get-tuple-element.17.refs_3_, bf16[2,256,512]{2,1,0:T(8,128)(2,1)} %copy-done.13, ...), custom_call_target="tpu_custom_call" | custom-call | tf_op jit(solution)/shard_map/whiten_rows/pallas_call | solution.py:548
  (100 shorter events, 0.3 us)
Async XLA Ops:
  0.6 7.6 %copy-start.29 = (s32[16,128]{1,0:T(8,128)S(1)}, s32[16,128]{1,0:T(8,128)}, u32[]{:S(2)}) copy-start(s32[16,128]{1,0:T(8,128)} %refs_7_.1) | copy-start | bytes 24580
  0.6 7.7 %copy-start.33 = (s32[8]{0:T(128)S(1)}, s32[8]{0:T(128)}, u32[]{:S(2)}) copy-start(s32[8]{0:T(128)} %param.15) | copy-start | bytes 100
  0.7 10.8 %copy-start.31 = (f32[3,4]{1,0:T(4,128)S(1)}, f32[3,4]{1,0:T(4,128)}, u32[]{:S(2)}) copy-start(f32[3,4]{1,0:T(4,128)} %param.12) | copy-start | bytes 148
  0.7 11.3 %copy-start.32 = (f32[3,3]{1,0:T(4,128)S(1)}, f32[3,3]{1,0:T(4,128)}, u32[]{:S(2)}) copy-start(f32[3,3]{1,0:T(4,128)} %param.13) | copy-start | bytes 112
  0.7 12.0 %copy-start.28 = (f32[3,3,3,9]{3,2,1,0:T(4,128)S(1)}, f32[3,3,3,9]{3,2,1,0:T(4,128)}, u32[]{:S(2)}) copy-start(f32[3,3,3,9]{3,2,1,0:T(4,128)} %param.11) | copy-start | bytes 2920
  7.8 5.5 %collective-permute-start = (bf16[513,16,128]{2,1,0:T(8,128)(2,1)}, bf16[513,16,128]{2,1,0:T(8,128)(2,1)S(1)}, u32[]{:S(2)}, u32[]{:S(2)}) collective-permute-start(bf16[513,16,128]{2,1,0:T(8,128)(2,1)} %halo_rows.1), channel_id=1, source_target_pairs={{0,1},{1,0},{2,3},{3,2},{4,5},{5,4},{6,7},{7,6},{8,9},{9,8},{10,11... | collective-permute-start | bytes 6303752 | tf_op jit(solution)/shard_map/ppermute | solution.py:625
  8.3 5.0 %collective-permute-start.1 = (s32[16,128]{1,0:T(8,128)S(1)}, s32[16,128]{1,0:T(8,128)S(1)}, u32[]{:S(2)}, u32[]{:S(2)}) collective-permute-start(s32[16,128]{1,0:T(8,128)S(1)} %copy-done.29), channel_id=1, source_target_pairs={{0,1},{1,0},{2,3},{3,2},{4,5},{5,4},{6,7},{7,6},{8,9},{9,8},{10,11... | collective-permute-start | bytes 24584 | tf_op jit(solution)/shard_map/ppermute | solution.py:624
  45.7 3.5 %copy-start = (bf16[16,528,128]{2,1,0:T(8,128)(2,1)S(1)}, bf16[16,528,128]{2,1,0:T(8,128)(2,1)}, u32[]{:S(2)}) copy-start(bf16[16,528,128]{2,1,0:T(8,128)(2,1)} %encode.1.enc_ref.value_ref) | copy-start | bytes 6488068
  45.7 3.5 %copy-start.1 = (s32[512]{0:T(512)S(1)}, s32[512]{0:T(512)}, u32[]{:S(2)}) copy-start(s32[512]{0:T(512)} %param.9) | copy-start | bytes 6148
  47.1 2.1 collective-permute-start.2
  50.6 15.1 %collective-permute-start.3 = (bf16[1,256,512]{2,1,0:T(8,128)(2,1)S(1)}, bf16[1,256,512]{2,1,0:T(8,128)(2,1)S(1)}, u32[]{:S(2)}, u32[]{:S(2)}) collective-permute-start(bf16[1,256,512]{2,1,0:T(8,128)(2,1)S(1)} %bitcast.16), channel_id=1, source_target_pairs={{0,8},{2,10},{4,12},{6,14},{8,0},{10,2},{12,4},{14,6},{16,24},{18,... | collective-permute-start | bytes 786440 | tf_op jit(solution)/shard_map/ppermute | solution.py:581
  53.5 26.7 %collective-permute-start.19 = (bf16[1,256,512]{2,1,0:T(8,128)(2,1)S(1)}, bf16[1,256,512]{2,1,0:T(8,128)(2,1)S(1)}, u32[]{:S(2)}, u32[]{:S(2)}) collective-permute-start(bf16[1,256,512]{2,1,0:T(8,128)(2,1)S(1)} %bitcast.17), channel_id=1, source_target_pairs={{0,16},{2,18},{4,20},{6,22},{8,24},{10,26},{12,28},{14,30},{16,0},... | collective-permute-start | bytes 786440 | tf_op jit(solution)/shard_map/ppermute | solution.py:581
  56.1 24.1 %collective-permute-start.21 = (bf16[1,272,512]{2,1,0:T(8,128)(2,1)S(1)}, bf16[1,272,512]{2,1,0:T(8,128)(2,1)S(1)}, u32[]{:S(2)}, u32[]{:S(2)}) collective-permute-start(bf16[1,272,512]{2,1,0:T(8,128)(2,1)S(1)} %bitcast.13), channel_id=1, source_target_pairs={{0,16},{2,18},{4,20},{6,22},{8,24},{10,26},{12,28},{14,30},{16,0},... | collective-permute-start | bytes 835592 | tf_op jit(solution)/shard_map/ppermute | solution.py:581
  65.7 90.0 %copy-start.13 = (bf16[2,256,512]{2,1,0:T(8,128)(2,1)}, bf16[2,256,512]{2,1,0:T(8,128)(2,1)S(1)}, u32[]{:S(2)}) copy-start(bf16[2,256,512]{2,1,0:T(8,128)(2,1)S(1)} %pad_maximum_fusion.1.refs_0_.refs_4_) | copy-start | bytes 1572868
  65.7 29.2 %collective-permute-start.11 = (bf16[2,256,512]{2,1,0:T(8,128)(2,1)S(1)}, bf16[2,256,512]{2,1,0:T(8,128)(2,1)S(1)}, u32[]{:S(2)}, u32[]{:S(2)}) collective-permute-start(bf16[2,256,512]{2,1,0:T(8,128)(2,1)S(1)} %pad_maximum_fusion.1.refs_0_.refs_4_), channel_id=1, source_target_pairs={{0,4},{2,6},{4,0},{6,2},{8,12},{10,14},{12,8},{14,10},{16,20},{18,... | collective-permute-start | bytes 1572872 | tf_op jit(solution)/shard_map/ppermute | solution.py:581
  67.5 16.3 %collective-permute-start.4 = (bf16[1,272,512]{2,1,0:T(8,128)(2,1)S(1)}, bf16[1,272,512]{2,1,0:T(8,128)(2,1)S(1)}, u32[]{:S(2)}, u32[]{:S(2)}) collective-permute-start(bf16[1,272,512]{2,1,0:T(8,128)(2,1)S(1)} %bitcast.14), channel_id=1, source_target_pairs={{0,8},{2,10},{4,12},{6,14},{8,0},{10,2},{12,4},{14,6},{16,24},{18,... | collective-permute-start | bytes 835592 | tf_op jit(solution)/shard_map/ppermute | solution.py:581
  80.2 14.7 %collective-permute-start.22 = (bf16[1,272,512]{2,1,0:T(8,128)(2,1)S(1)}, bf16[1,272,512]{2,1,0:T(8,128)(2,1)S(1)}, u32[]{:S(2)}, u32[]{:S(2)}) collective-permute-start(bf16[1,272,512]{2,1,0:T(8,128)(2,1)S(1)} %collective-permute-done.21), channel_id=1, source_target_pairs={{0,8},{2,10},{4,12},{6,14},{8,0},{10,2},{12,4},{14,6},{16,24},{18,... | collective-permute-start | bytes 835592 | tf_op jit(solution)/shard_map/ppermute | solution.py:581
  80.2 13.2 %collective-permute-start.20 = (bf16[1,256,512]{2,1,0:T(8,128)(2,1)S(1)}, bf16[1,256,512]{2,1,0:T(8,128)(2,1)S(1)}, u32[]{:S(2)}, u32[]{:S(2)}) collective-permute-start(bf16[1,256,512]{2,1,0:T(8,128)(2,1)S(1)} %collective-permute-done.19), channel_id=1, source_target_pairs={{0,8},{2,10},{4,12},{6,14},{8,0},{10,2},{12,4},{14,6},{16,24},{18,... | collective-permute-start | bytes 786440 | tf_op jit(solution)/shard_map/ppermute | solution.py:581
  82.2 13.3 %collective-permute-start.7 = (bf16[2,256,512]{2,1,0:T(8,128)(2,1)S(1)}, bf16[2,256,512]{2,1,0:T(8,128)(2,1)S(1)}, u32[]{:S(2)}, u32[]{:S(2)}) collective-permute-start(bf16[2,256,512]{2,1,0:T(8,128)(2,1)S(1)} %pad_maximum_fusion.1.refs_0_.refs_4_), channel_id=1, source_target_pairs={{0,2},{2,0},{4,6},{6,4},{8,10},{10,8},{12,14},{14,12},{16,18},{18,... | collective-permute-start | bytes 1572872 | tf_op jit(solution)/shard_map/ppermute | solution.py:581
  83.8 71.9 %copy-start.9 = (bf16[2,272,512]{2,1,0:T(8,128)(2,1)}, bf16[2,272,512]{2,1,0:T(8,128)(2,1)S(1)}, u32[]{:S(2)}) copy-start(bf16[2,272,512]{2,1,0:T(8,128)(2,1)S(1)} %pad_maximum_fusion.refs_1_.refs_5_) | copy-start | bytes 1671172
  83.8 14.5 %collective-permute-start.12 = (bf16[2,272,512]{2,1,0:T(8,128)(2,1)S(1)}, bf16[2,272,512]{2,1,0:T(8,128)(2,1)S(1)}, u32[]{:S(2)}, u32[]{:S(2)}) collective-permute-start(bf16[2,272,512]{2,1,0:T(8,128)(2,1)S(1)} %pad_maximum_fusion.refs_1_.refs_5_), channel_id=1, source_target_pairs={{0,4},{2,6},{4,0},{6,2},{8,12},{10,14},{12,8},{14,10},{16,20},{18,... | collective-permute-start | bytes 1671176 | tf_op jit(solution)/shard_map/ppermute | solution.py:581
  93.4 15.6 %collective-permute-start.8 = (bf16[2,272,512]{2,1,0:T(8,128)(2,1)S(1)}, bf16[2,272,512]{2,1,0:T(8,128)(2,1)S(1)}, u32[]{:S(2)}, u32[]{:S(2)}) collective-permute-start(bf16[2,272,512]{2,1,0:T(8,128)(2,1)S(1)} %pad_maximum_fusion.refs_1_.refs_5_), channel_id=1, source_target_pairs={{0,2},{2,0},{4,6},{6,4},{8,10},{10,8},{12,14},{14,12},{16,18},{18,... | collective-permute-start | bytes 1671176 | tf_op jit(solution)/shard_map/ppermute | solution.py:581
  94.9 2.2 collective-permute-start.5
  94.9 60.8 %copy-start.22 = (bf16[2,256,512]{2,1,0:T(8,128)(2,1)}, bf16[2,256,512]{2,1,0:T(8,128)(2,1)S(1)}, u32[]{:S(2)}) copy-start(bf16[2,256,512]{2,1,0:T(8,128)(2,1)S(1)} %collective-permute-done.11.refs_8_.refs_12_) | copy-start | bytes 1572868
  94.9 14.0 %collective-permute-start.6 = (bf16[2,272,512]{2,1,0:T(8,128)(2,1)S(1)}, bf16[2,272,512]{2,1,0:T(8,128)(2,1)S(1)}, u32[]{:S(2)}, u32[]{:S(2)}) collective-permute-start(bf16[2,272,512]{2,1,0:T(8,128)(2,1)S(1)} %pad_maximum_fusion.refs_1_.refs_5_), channel_id=1, source_target_pairs={{0,1},{1,0},{2,3},{3,2},{4,5},{5,4},{6,7},{7,6},{8,9},{9,8},{10,11... | collective-permute-start | bytes 1671176 | tf_op jit(solution)/shard_map/ppermute | solution.py:604
  95.5 70.8 %copy-start.5 = (bf16[2,256,512]{2,1,0:T(8,128)(2,1)}, bf16[2,256,512]{2,1,0:T(8,128)(2,1)S(1)}, u32[]{:S(2)}) copy-start(bf16[2,256,512]{2,1,0:T(8,128)(2,1)S(1)} %constant_dynamic-update-slice_fusion.refs_16_.refs_3_.refs_20_) | copy-start | bytes 1572868
  95.5 49.2 %copy-start.23 = (bf16[2,256,512]{2,1,0:T(8,128)(2,1)}, bf16[2,256,512]{2,1,0:T(8,128)(2,1)S(1)}, u32[]{:S(2)}) copy-start(bf16[2,256,512]{2,1,0:T(8,128)(2,1)S(1)} %collective-permute-done.7.refs_4_.refs_8_) | copy-start | bytes 1572868
  95.5 15.0 %collective-permute-start.29 = (bf16[2,256,512]{2,1,0:T(8,128)(2,1)S(1)}, bf16[2,256,512]{2,1,0:T(8,128)(2,1)}, u32[]{:S(2)}, u32[]{:S(2)}) collective-permute-start(bf16[2,256,512]{2,1,0:T(8,128)(2,1)S(1)} %constant_dynamic-update-slice_fusion.refs_16_.refs_3_.refs_20_), channel_id=1, source_target_pairs={{0,4},{2,6},{4,0},{6,2},{8,12},{10,14},{12,8},{14,10},{16,20},{18,... | collective-permute-start | bytes 1572872 | tf_op jit(solution)/shard_map/ppermute | solution.py:581
  97.1 69.2 %copy-start.4 = (bf16[2,272,512]{2,1,0:T(8,128)(2,1)}, bf16[2,272,512]{2,1,0:T(8,128)(2,1)S(1)}, u32[]{:S(2)}) copy-start(bf16[2,272,512]{2,1,0:T(8,128)(2,1)S(1)} %constant_dynamic-update-slice_fusion.2.refs_17_.refs_4_.refs_21_) | copy-start | bytes 1671172
  97.1 1.8 copy-start.24
  97.1 24.7 %collective-permute-start.30 = (bf16[2,272,512]{2,1,0:T(8,128)(2,1)S(1)}, bf16[2,272,512]{2,1,0:T(8,128)(2,1)S(1)}, u32[]{:S(2)}, u32[]{:S(2)}) collective-permute-start(bf16[2,272,512]{2,1,0:T(8,128)(2,1)S(1)} %constant_dynamic-update-slice_fusion.2.refs_17_.refs_4_.refs_21_), channel_id=1, source_target_pairs={{0,4},{2,6},{4,0},{6,2},{8,12},{10,14},{12,8},{14,10},{16,20},{18,... | collective-permute-start | bytes 1671176 | tf_op jit(solution)/shard_map/ppermute | solution.py:581
  98.3 57.4 %copy-start.14 = (bf16[2,272,512]{2,1,0:T(8,128)(2,1)}, bf16[2,272,512]{2,1,0:T(8,128)(2,1)S(1)}, u32[]{:S(2)}) copy-start(bf16[2,272,512]{2,1,0:T(8,128)(2,1)S(1)} %collective-permute-done.12.refs_9_.refs_13_) | copy-start | bytes 1671172
  98.3 22.0 %collective-permute-start.25 = (bf16[2,256,512]{2,1,0:T(8,128)(2,1)S(1)}, bf16[2,256,512]{2,1,0:T(8,128)(2,1)}, u32[]{:S(2)}, u32[]{:S(2)}) collective-permute-start(bf16[2,256,512]{2,1,0:T(8,128)(2,1)S(1)} %constant_dynamic-update-slice_fusion.refs_16_.refs_3_.refs_20_), channel_id=1, source_target_pairs={{0,2},{2,0},{4,6},{6,4},{8,10},{10,8},{12,14},{14,12},{16,18},{18,... | collective-permute-start | bytes 1572872 | tf_op jit(solution)/shard_map/ppermute | solution.py:581
  108.9 46.8 %copy-start.15 = (bf16[2,272,512]{2,1,0:T(8,128)(2,1)}, bf16[2,272,512]{2,1,0:T(8,128)(2,1)S(1)}, u32[]{:S(2)}) copy-start(bf16[2,272,512]{2,1,0:T(8,128)(2,1)S(1)} %collective-permute-done.8.refs_5_.refs_9_) | copy-start | bytes 1671172
  108.9 12.8 %collective-permute-start.23 = (bf16[2,256,512]{2,1,0:T(8,128)(2,1)S(1)}, bf16[2,256,512]{2,1,0:T(8,128)(2,1)S(1)}, u32[]{:S(2)}, u32[]{:S(2)}) collective-permute-start(bf16[2,256,512]{2,1,0:T(8,128)(2,1)S(1)} %constant_dynamic-update-slice_fusion.refs_16_.refs_3_.refs_20_), channel_id=1, source_target_pairs={{0,1},{1,0},{2,3},{3,2},{4,5},{5,4},{6,7},{7,6},{8,9},{9,8},{10,11... | collective-permute-start | bytes 1572872 | tf_op jit(solution)/shard_map/ppermute | solution.py:604
  109.0 46.8 %copy-start.16 = (bf16[2,272,512]{2,1,0:T(8,128)(2,1)}, bf16[2,272,512]{2,1,0:T(8,128)(2,1)S(1)}, u32[]{:S(2)}) copy-start(bf16[2,272,512]{2,1,0:T(8,128)(2,1)S(1)} %collective-permute-done.6.refs_3_.refs_7_) | copy-start | bytes 1671172
  109.0 23.2 %collective-permute-start.26 = (bf16[2,272,512]{2,1,0:T(8,128)(2,1)S(1)}, bf16[2,272,512]{2,1,0:T(8,128)(2,1)S(1)}, u32[]{:S(2)}, u32[]{:S(2)}) collective-permute-start(bf16[2,272,512]{2,1,0:T(8,128)(2,1)S(1)} %constant_dynamic-update-slice_fusion.2.refs_17_.refs_4_.refs_21_), channel_id=1, source_target_pairs={{0,2},{2,0},{4,6},{6,4},{8,10},{10,8},{12,14},{14,12},{16,18},{18,... | collective-permute-start | bytes 1671176 | tf_op jit(solution)/shard_map/ppermute | solution.py:581
  110.5 21.6 %collective-permute-start.24 = (bf16[2,272,512]{2,1,0:T(8,128)(2,1)S(1)}, bf16[2,272,512]{2,1,0:T(8,128)(2,1)S(1)}, u32[]{:S(2)}, u32[]{:S(2)}) collective-permute-start(bf16[2,272,512]{2,1,0:T(8,128)(2,1)S(1)} %constant_dynamic-update-slice_fusion.2.refs_17_.refs_4_.refs_21_), channel_id=1, source_target_pairs={{0,1},{1,0},{2,3},{3,2},{4,5},{5,4},{6,7},{7,6},{8,9},{9,8},{10,11... | collective-permute-start | bytes 1671176 | tf_op jit(solution)/shard_map/ppermute | solution.py:604
  120.3 23.8 %collective-permute-start.16 = (bf16[2,272,512]{2,1,0:T(8,128)(2,1)S(1)}, bf16[2,272,512]{2,1,0:T(8,128)(2,1)S(1)}, u32[]{:S(2)}, u32[]{:S(2)}) collective-permute-start(bf16[2,272,512]{2,1,0:T(8,128)(2,1)S(1)} %collective-permute-done.12.refs_9_.refs_13_), channel_id=1, source_target_pairs={{0,2},{2,0},{4,6},{6,4},{8,10},{10,8},{12,14},{14,12},{16,18},{18,... | collective-permute-start | bytes 1671176 | tf_op jit(solution)/shard_map/ppermute | solution.py:581
  121.8 44.5 %copy-start.10 = (bf16[2,256,512]{2,1,0:T(8,128)(2,1)}, bf16[2,256,512]{2,1,0:T(8,128)(2,1)S(1)}, u32[]{:S(2)}) copy-start(bf16[2,256,512]{2,1,0:T(8,128)(2,1)S(1)} %collective-permute-done.23.refs_18_.refs_5_.refs_22_) | copy-start | bytes 1572868
  121.8 10.8 %collective-permute-start.13 = (bf16[2,256,512]{2,1,0:T(8,128)(2,1)S(1)}, bf16[2,256,512]{2,1,0:T(8,128)(2,1)}, u32[]{:S(2)}, u32[]{:S(2)}) collective-permute-start(bf16[2,256,512]{2,1,0:T(8,128)(2,1)S(1)} %collective-permute-done.11.refs_8_.refs_12_), channel_id=1, source_target_pairs={{0,1},{1,0},{2,3},{3,2},{4,5},{5,4},{6,7},{7,6},{8,9},{9,8},{10,11... | collective-permute-start | bytes 1572872 | tf_op jit(solution)/shard_map/ppermute | solution.py:604
  121.8 44.5 %copy-start.6 = (bf16[2,272,512]{2,1,0:T(8,128)(2,1)}, bf16[2,272,512]{2,1,0:T(8,128)(2,1)S(1)}, u32[]{:S(2)}) copy-start(bf16[2,272,512]{2,1,0:T(8,128)(2,1)S(1)} %collective-permute-done.30.refs_25_.refs_12_.refs_29_) | copy-start | bytes 1671172
  121.8 14.3 %collective-permute-start.15 = (bf16[2,256,512]{2,1,0:T(8,128)(2,1)S(1)}, bf16[2,256,512]{2,1,0:T(8,128)(2,1)S(1)}, u32[]{:S(2)}, u32[]{:S(2)}) collective-permute-start(bf16[2,256,512]{2,1,0:T(8,128)(2,1)S(1)} %collective-permute-done.7.refs_4_.refs_8_), channel_id=1, source_target_pairs={{0,4},{2,6},{4,0},{6,2},{8,12},{10,14},{12,8},{14,10},{16,20},{18,... | collective-permute-start | bytes 1572872 | tf_op jit(solution)/shard_map/ppermute | solution.py:581
  132.1 34.2 %copy-start.7 = (bf16[2,272,512]{2,1,0:T(8,128)(2,1)}, bf16[2,272,512]{2,1,0:T(8,128)(2,1)S(1)}, u32[]{:S(2)}) copy-start(bf16[2,272,512]{2,1,0:T(8,128)(2,1)S(1)} %collective-permute-done.26.refs_21_.refs_8_.refs_25_) | copy-start | bytes 1671172
  132.1 11.9 %collective-permute-start.9 = (bf16[2,256,512]{2,1,0:T(8,128)(2,1)S(1)}, bf16[2,256,512]{2,1,0:T(8,128)(2,1)S(1)}, u32[]{:S(2)}, u32[]{:S(2)}) collective-permute-start(bf16[2,256,512]{2,1,0:T(8,128)(2,1)S(1)} %collective-permute-done.7.refs_4_.refs_8_), channel_id=1, source_target_pairs={{0,1},{1,0},{2,3},{3,2},{4,5},{5,4},{6,7},{7,6},{8,9},{9,8},{10,11... | collective-permute-start | bytes 1572872 | tf_op jit(solution)/shard_map/ppermute | solution.py:604
  132.1 12.5 %copy-start.8 = (bf16[2,272,512]{2,1,0:T(8,128)(2,1)}, bf16[2,272,512]{2,1,0:T(8,128)(2,1)S(1)}, u32[]{:S(2)}) copy-start(bf16[2,272,512]{2,1,0:T(8,128)(2,1)S(1)} %collective-permute-done.24.refs_19_.refs_6_.refs_23_) | copy-start | bytes 1671172
  132.1 12.4 %collective-permute-start.14 = (bf16[2,272,512]{2,1,0:T(8,128)(2,1)S(1)}, bf16[2,272,512]{2,1,0:T(8,128)(2,1)S(1)}, u32[]{:S(2)}, u32[]{:S(2)}) collective-permute-start(bf16[2,272,512]{2,1,0:T(8,128)(2,1)S(1)} %collective-permute-done.12.refs_9_.refs_13_), channel_id=1, source_target_pairs={{0,1},{1,0},{2,3},{3,2},{4,5},{5,4},{6,7},{7,6},{8,9},{9,8},{10,11... | collective-permute-start | bytes 1671176 | tf_op jit(solution)/shard_map/ppermute | solution.py:604
  132.6 12.0 %collective-permute-start.10 = (bf16[2,272,512]{2,1,0:T(8,128)(2,1)S(1)}, bf16[2,272,512]{2,1,0:T(8,128)(2,1)S(1)}, u32[]{:S(2)}, u32[]{:S(2)}) collective-permute-start(bf16[2,272,512]{2,1,0:T(8,128)(2,1)S(1)} %collective-permute-done.8.refs_5_.refs_9_), channel_id=1, source_target_pairs={{0,1},{1,0},{2,3},{3,2},{4,5},{5,4},{6,7},{7,6},{8,9},{9,8},{10,11... | collective-permute-start | bytes 1671176 | tf_op jit(solution)/shard_map/ppermute | solution.py:604
  136.2 18.0 %copy-start.25 = (bf16[2,256,512]{2,1,0:T(8,128)(2,1)}, bf16[2,256,512]{2,1,0:T(8,128)(2,1)S(1)}, u32[]{:S(2)}) copy-start(bf16[2,256,512]{2,1,0:T(8,128)(2,1)S(1)} %collective-permute-done.15.refs_12_.refs_16_) | copy-start | bytes 1572868
  136.2 17.4 %collective-permute-start.34 = (bf16[2,272,512]{2,1,0:T(8,128)(2,1)S(1)}, bf16[2,272,512]{2,1,0:T(8,128)(2,1)}, u32[]{:S(2)}, u32[]{:S(2)}) collective-permute-start(bf16[2,272,512]{2,1,0:T(8,128)(2,1)S(1)} %collective-permute-done.30.refs_25_.refs_12_.refs_29_), channel_id=1, source_target_pairs={{0,2},{2,0},{4,6},{6,4},{8,10},{10,8},{12,14},{14,12},{16,18},{18,... | collective-permute-start | bytes 1671176 | tf_op jit(solution)/shard_map/ppermute | solution.py:581
  144.1 11.7 %copy-start.17 = (bf16[2,272,512]{2,1,0:T(8,128)(2,1)}, bf16[2,272,512]{2,1,0:T(8,128)(2,1)S(1)}, u32[]{:S(2)}) copy-start(bf16[2,272,512]{2,1,0:T(8,128)(2,1)S(1)} %collective-permute-done.16.refs_13_.refs_17_) | copy-start | bytes 1671172
  144.1 10.1 %collective-permute-start.18 = (bf16[2,272,512]{2,1,0:T(8,128)(2,1)S(1)}, bf16[2,272,512]{2,1,0:T(8,128)(2,1)S(1)}, u32[]{:S(2)}, u32[]{:S(2)}) collective-permute-start(bf16[2,272,512]{2,1,0:T(8,128)(2,1)S(1)} %collective-permute-done.16.refs_13_.refs_17_), channel_id=1, source_target_pairs={{0,1},{1,0},{2,3},{3,2},{4,5},{5,4},{6,7},{7,6},{8,9},{9,8},{10,11... | collective-permute-start | bytes 1671176 | tf_op jit(solution)/shard_map/ppermute | solution.py:604
  144.1 10.0 %copy-start.26 = (bf16[2,256,512]{2,1,0:T(8,128)(2,1)}, bf16[2,256,512]{2,1,0:T(8,128)(2,1)S(1)}, u32[]{:S(2)}) copy-start(bf16[2,256,512]{2,1,0:T(8,128)(2,1)S(1)} %collective-permute-done.9.refs_6_.refs_10_) | copy-start | bytes 1572868
  144.1 9.5 %collective-permute-start.17 = (bf16[2,256,512]{2,1,0:T(8,128)(2,1)S(1)}, bf16[2,256,512]{2,1,0:T(8,128)(2,1)S(1)}, u32[]{:S(2)}, u32[]{:S(2)}) collective-permute-start(bf16[2,256,512]{2,1,0:T(8,128)(2,1)S(1)} %collective-permute-done.15.refs_12_.refs_16_), channel_id=1, source_target_pairs={{0,1},{1,0},{2,3},{3,2},{4,5},{5,4},{6,7},{7,6},{8,9},{9,8},{10,11... | collective-permute-start | bytes 1572872 | tf_op jit(solution)/shard_map/ppermute | solution.py:604
  144.6 11.2 %copy-start.18 = (bf16[2,272,512]{2,1,0:T(8,128)(2,1)}, bf16[2,272,512]{2,1,0:T(8,128)(2,1)S(1)}, u32[]{:S(2)}) copy-start(bf16[2,272,512]{2,1,0:T(8,128)(2,1)S(1)} %collective-permute-done.14.refs_11_.refs_15_) | copy-start | bytes 1671172
  144.6 22.5 %collective-permute-start.31 = (bf16[2,256,512]{2,1,0:T(8,128)(2,1)}, bf16[2,256,512]{2,1,0:T(8,128)(2,1)}, u32[]{:S(2)}, u32[]{:S(2)}) collective-permute-start(bf16[2,256,512]{2,1,0:T(8,128)(2,1)} %collective-permute-done.29.refs_24_.refs_11_.refs_28_), channel_id=1, source_target_pairs={{0,1},{1,0},{2,3},{3,2},{4,5},{5,4},{6,7},{7,6},{8,9},{9,8},{10,11... | collective-permute-start | bytes 1572872 | tf_op jit(solution)/shard_map/ppermute | solution.py:604
  144.7 9.4 %copy-start.19 = (bf16[2,272,512]{2,1,0:T(8,128)(2,1)}, bf16[2,272,512]{2,1,0:T(8,128)(2,1)S(1)}, u32[]{:S(2)}) copy-start(bf16[2,272,512]{2,1,0:T(8,128)(2,1)S(1)} %collective-permute-done.10.refs_7_.refs_11_) | copy-start | bytes 1671172
  144.7 21.6 %collective-permute-start.33 = (bf16[2,256,512]{2,1,0:T(8,128)(2,1)}, bf16[2,256,512]{2,1,0:T(8,128)(2,1)S(1)}, u32[]{:S(2)}, u32[]{:S(2)}) collective-permute-start(bf16[2,256,512]{2,1,0:T(8,128)(2,1)} %collective-permute-done.25.refs_20_.refs_7_.refs_24_), channel_id=1, source_target_pairs={{0,4},{2,6},{4,0},{6,2},{8,12},{10,14},{12,8},{14,10},{16,20},{18,... | collective-permute-start | bytes 1572872 | tf_op jit(solution)/shard_map/ppermute | solution.py:581
  153.6 14.9 %collective-permute-start.32 = (bf16[2,272,512]{2,1,0:T(8,128)(2,1)S(1)}, bf16[2,272,512]{2,1,0:T(8,128)(2,1)}, u32[]{:S(2)}, u32[]{:S(2)}) collective-permute-start(bf16[2,272,512]{2,1,0:T(8,128)(2,1)S(1)} %collective-permute-done.30.refs_25_.refs_12_.refs_29_), channel_id=1, source_target_pairs={{0,1},{1,0},{2,3},{3,2},{4,5},{5,4},{6,7},{7,6},{8,9},{9,8},{10,11... | collective-permute-start | bytes 1671176 | tf_op jit(solution)/shard_map/ppermute | solution.py:604
  153.6 14.9 %collective-permute-start.28 = (bf16[2,272,512]{2,1,0:T(8,128)(2,1)S(1)}, bf16[2,272,512]{2,1,0:T(8,128)(2,1)}, u32[]{:S(2)}, u32[]{:S(2)}) collective-permute-start(bf16[2,272,512]{2,1,0:T(8,128)(2,1)S(1)} %collective-permute-done.26.refs_21_.refs_8_.refs_25_), channel_id=1, source_target_pairs={{0,1},{1,0},{2,3},{3,2},{4,5},{5,4},{6,7},{7,6},{8,9},{9,8},{10,11... | collective-permute-start | bytes 1671176 | tf_op jit(solution)/shard_map/ppermute | solution.py:604
  155.2 13.3 %collective-permute-start.36 = (bf16[2,272,512]{2,1,0:T(8,128)(2,1)}, bf16[2,272,512]{2,1,0:T(8,128)(2,1)}, u32[]{:S(2)}, u32[]{:S(2)}) collective-permute-start(bf16[2,272,512]{2,1,0:T(8,128)(2,1)} %collective-permute-done.34.refs_29_.refs_16_.refs_33_), channel_id=1, source_target_pairs={{0,1},{1,0},{2,3},{3,2},{4,5},{5,4},{6,7},{7,6},{8,9},{9,8},{10,11... | collective-permute-start | bytes 1671176 | tf_op jit(solution)/shard_map/ppermute | solution.py:604
  166.3 2.2 collective-permute-start.27
  167.1 2.1 collective-permute-start.35
  170.1 57.0 %all-to-all-start = ((bf16[16,528,128]{2,1,0:T(8,128)(2,1)}), bf16[16,528,128]{2,1,0:T(8,128)(2,1)S(1)}, u32[]{:S(2)}, u32[]{:S(2)}) async-start(bf16[16,528,128]{2,1,0:T(8,128)(2,1)} %after.3), calls=%async_computation | async-start | bytes 4325376 | tf_op jit(solution)/shard_map/all_to_all | solution.py:650
  (8 other events, 7.3 us)

commit v5 on v4

--- a/solution.py
+++ b/solution.py
@@ -410,7 +410,7 @@
         low_ref[EDGE * i : EDGE * (i + 1), EDGE * (i + 1) : EDGE * (i + 2)] = jnp.zeros((EDGE, EDGE), F32)
 
 
-SPLIT = 2
+SPLIT = 1
 
 
 def whole(shape):

time: 247 us -> 247 us (level)
  no operation moved by 1% of the time
where the time goes in v5:
time: 247 us
  Pallas kernels  117 us (47%)
  waiting for transfers between devices  80.3 us (33%)
  starting transfers between devices  33.9 us (14%)
  local copies, waits for them, and re-layouts  9.2 us (4%)
  between operations  4.92 us (2%)
    ppermute x18, waiting for transfers between devices, across(): return [lax.ppermute(x, 'dp', pairs) for x in arrays]  76.6 us
    pallas_call x1, Pallas kernels, gram_factor(): pl.pallas_call(body, grid=(pieces[0].shape[0], SPLIT), in_specs=[pl.Block...  49.3 us
    pallas_call x1, Pallas kernels, encode(): pl.pallas_call(body, grid=(pl.cdiv(count, BLOCK),), in_specs=[smem, smem,...  30.5 us
    ppermute x18, starting transfers between devices, across(): return [lax.ppermute(x, 'dp', pairs) for x in arrays]  24.1 us
    pallas_call x1, Pallas kernels, whiten_rows(): pl.pallas_call(body, grid=(pieces[0].shape[0], SPLIT), in_specs=[pl.Block...  18 us
    pallas_call x1, Pallas kernels, gram_part(): pl.pallas_call(gram_kernel, grid=(pieces[0].shape[0], SPLIT), in_specs=[p...  10.4 us
    pallas_call x1, Pallas kernels, halo_rows(): pl.pallas_call(halo_kernel, grid_spec=pltpu.PrefetchScalarGridSpec(num_sc...  7.14 us
    unnamed x70, local copies, waits for them, and re-layouts  6.07 us
  transfers between devices with their start and end apart: 38, of which 12 were waited for; matrix products, arithmetic and copies ran while one was open for 1% of the time, Pallas kernels for 24%

profile of v5, /device:TPU:0, one launch (start us, length us, event | category | flops | bytes accessed | tf_op | source)
XLA Modules:
  0.0 246.5 jit_solution(12028177959073689532)
XLA Ops:
  0.7 7.1 %halo_rows.1 = bf16[513,16,128]{2,1,0:T(8,128)(2,1)} custom-call(s32[1]{0:T(128)} %bitcast.tile_ref.refs_0_, bf16[513,3,16,128]{3,2,1,0:T(8,128)(2,1)} %refs_5_.1), custom_call_target="tpu_custom_call" | custom-call | tf_op jit(solution)/shard_map/halo_rows/pallas_call | solution.py:37
  7.8 0.5 collective-permute-start
  8.3 0.1 collective-permute-start.1
  8.3 0.6 fusion
  11.4 0.6 reshape.19.refs_2_
  12.0 0.6 reshape.20.refs_3_
  12.6 0.7 reshape.18.refs_1_
  13.3 0.6 copy-done.30
  13.9 1.3 copy-done.21
  15.2 30.5 %encode.1.enc_ref.value_ref = bf16[16,528,128]{2,1,0:T(8,128)(2,1)} custom-call(s32[1]{0:T(128)} %bitcast.tile_ref.refs_0_, f32[243]{0:T(256)} %reshape.18.refs_1_, f32[12]{0:T(128)} %reshape.19.refs_2_, f32[9]{0:T(128)} %reshape.20.refs_3_, f32[3]{0:T(128)} %refs_4_.1, bf16[513,3,16,128]{3,2,1,0:T(8,128)(2,1)} %refs_5_.1, bf16[513,16,128]{2,1,0:T(8,128)(2,1)} %copy-done.21, ...), custom_call_target="tpu_custom_call" | custom-call | tf_op jit(solution)/shard_map/encode/pallas_call | solution.py:164
  45.7 1.4 dynamic-slice_select_fusion
  47.1 0.5 collective-permute-start.2
  47.7 1.6 collective-permute-done.2.near_ref
  49.2 1.4 pick_pairs.1
  50.6 2.9 %collective-permute-start.3 = (bf16[1,256,512]{2,1,0:T(8,128)(2,1)S(1)}, bf16[1,256,512]{2,1,0:T(8,128)(2,1)S(1)}, u32[]{:S(2)}, u32[]{:S(2)}) collective-permute-start(bf16[1,256,512]{2,1,0:T(8,128)(2,1)S(1)} %bitcast.16), channel_id=1, source_target_pairs={{0,8},{2,10},{4,12},{6,14},{8,0},{10,2},{12,4},{14,6},{16,24},{18,... | collective-permute-start | bytes 786440 | tf_op jit(solution)/shard_map/ppermute | solution.py:581
  53.5 2.6 %collective-permute-start.19 = (bf16[1,256,512]{2,1,0:T(8,128)(2,1)S(1)}, bf16[1,256,512]{2,1,0:T(8,128)(2,1)S(1)}, u32[]{:S(2)}, u32[]{:S(2)}) collective-permute-start(bf16[1,256,512]{2,1,0:T(8,128)(2,1)S(1)} %bitcast.17), channel_id=1, source_target_pairs={{0,16},{2,18},{4,20},{6,22},{8,24},{10,26},{12,28},{14,30},{16,0},... | collective-permute-start | bytes 786440 | tf_op jit(solution)/shard_map/ppermute | solution.py:581
  56.1 0.3 collective-permute-start.21
  56.4 9.2 %collective-permute-done.3 = bf16[1,256,512]{2,1,0:T(8,128)(2,1)S(1)} collective-permute-done((bf16[1,256,512]{2,1,0:T(8,128)(2,1)S(1)}, bf16[1,256,512]{2,1,0:T(8,128)(2,1)S(1)}, u32[]{:S(2)}, u32[]{:S(2)}) %collective-permute-start.3) | collective-permute-done | bytes 262176 | tf_op jit(solution)/shard_map/ppermute | solution.py:581
  65.7 0.1 pad_maximum_fusion.1.refs_0_.refs_4_
  65.7 1.7 collective-permute-start.11
  67.5 12.8 %collective-permute-done.21 = bf16[1,272,512]{2,1,0:T(8,128)(2,1)S(1)} collective-permute-done((bf16[1,272,512]{2,1,0:T(8,128)(2,1)S(1)}, bf16[1,272,512]{2,1,0:T(8,128)(2,1)S(1)}, u32[]{:S(2)}, u32[]{:S(2)}) %collective-permute-start.21) | collective-permute-done | bytes 278560 | tf_op jit(solution)/shard_map/ppermute | solution.py:581
  80.2 2.0 collective-permute-start.20
  82.2 1.5 collective-permute-start.7
  83.7 0.1 pad_maximum_fusion.refs_1_.refs_5_
  83.8 1.5 collective-permute-start.12
  85.3 8.1 %collective-permute-done.20 = bf16[1,256,512]{2,1,0:T(8,128)(2,1)S(1)} collective-permute-done((bf16[1,256,512]{2,1,0:T(8,128)(2,1)S(1)}, bf16[1,256,512]{2,1,0:T(8,128)(2,1)S(1)}, u32[]{:S(2)}, u32[]{:S(2)}) %collective-permute-start.20) | collective-permute-done | bytes 262176 | tf_op jit(solution)/shard_map/ppermute | solution.py:581
  93.4 1.5 collective-permute-start.8
  94.9 0.5 collective-permute-start.6
  95.5 1.5 collective-permute-start.29
  97.1 1.2 collective-permute-start.30
  98.3 0.6 collective-permute-start.25
  98.9 10.1 %collective-permute-done.8.refs_5_.refs_9_ = bf16[2,272,512]{2,1,0:T(8,128)(2,1)S(1)} collective-permute-done((bf16[2,272,512]{2,1,0:T(8,128)(2,1)S(1)}, bf16[2,272,512]{2,1,0:T(8,128)(2,1)S(1)}, u32[]{:S(2)}, u32[]{:S(2)}) %collective-permute-start.8) | collective-permute-done | bytes 557088 | tf_op jit(solution)/shard_map/ppermute | solution.py:581
  109.0 1.6 collective-permute-start.26
  110.5 0.2 collective-permute-start.24
  110.7 9.6 %collective-permute-done.25.refs_20_.refs_7_.refs_24_ = bf16[2,256,512]{2,1,0:T(8,128)(2,1)} collective-permute-done((bf16[2,256,512]{2,1,0:T(8,128)(2,1)S(1)}, bf16[2,256,512]{2,1,0:T(8,128)(2,1)}, u32[]{:S(2)}, u32[]{:S(2)}) %collective-permute-start.25) | collective-permute-done | bytes 524320 | tf_op jit(solution)/shard_map/ppermute | solution.py:581
  120.3 1.5 collective-permute-start.16
  121.8 1.5 collective-permute-start.15
  123.4 8.8 %collective-permute-done.26.refs_21_.refs_8_.refs_25_ = bf16[2,272,512]{2,1,0:T(8,128)(2,1)S(1)} collective-permute-done((bf16[2,272,512]{2,1,0:T(8,128)(2,1)S(1)}, bf16[2,272,512]{2,1,0:T(8,128)(2,1)S(1)}, u32[]{:S(2)}, u32[]{:S(2)}) %collective-permute-start.26) | collective-permute-done | bytes 557088 | tf_op jit(solution)/shard_map/ppermute | solution.py:581
  132.1 0.5 collective-permute-start.14
  132.6 0.1 collective-permute-start.10
  132.7 3.4 %collective-permute-done.15.refs_12_.refs_16_ = bf16[2,256,512]{2,1,0:T(8,128)(2,1)S(1)} collective-permute-done((bf16[2,256,512]{2,1,0:T(8,128)(2,1)S(1)}, bf16[2,256,512]{2,1,0:T(8,128)(2,1)S(1)}, u32[]{:S(2)}, u32[]{:S(2)}) %collective-permute-start.15) | collective-permute-done | bytes 524320 | tf_op jit(solution)/shard_map/ppermute | solution.py:581
  136.2 0.5 collective-permute-start.34
  136.7 7.4 %collective-permute-done.16.refs_13_.refs_17_ = bf16[2,272,512]{2,1,0:T(8,128)(2,1)S(1)} collective-permute-done((bf16[2,272,512]{2,1,0:T(8,128)(2,1)S(1)}, bf16[2,272,512]{2,1,0:T(8,128)(2,1)S(1)}, u32[]{:S(2)}, u32[]{:S(2)}) %collective-permute-start.16) | collective-permute-done | bytes 557088 | tf_op jit(solution)/shard_map/ppermute | solution.py:581
  144.1 0.5 collective-permute-start.17
  144.6 0.1 collective-permute-start.31
  144.7 1.6 collective-permute-start.33
  146.3 7.3 %collective-permute-done.34.refs_29_.refs_16_.refs_33_ = bf16[2,272,512]{2,1,0:T(8,128)(2,1)} collective-permute-done((bf16[2,272,512]{2,1,0:T(8,128)(2,1)S(1)}, bf16[2,272,512]{2,1,0:T(8,128)(2,1)}, u32[]{:S(2)}, u32[]{:S(2)}) %collective-permute-start.34) | collective-permute-done | bytes 557088 | tf_op jit(solution)/shard_map/ppermute | solution.py:581
  153.6 0.5 collective-permute-start.28
  154.1 0.3 copy-done.27
  154.4 0.8 copy-done.20
  155.2 0.5 collective-permute-start.36
  155.8 10.4 %gram_part.1 = (f32[1024,1024]{1,0:T(8,128)}, f32[8,128]{1,0:T(8,128)}) custom-call(s32[1]{0:T(128)} %bitcast.tile_ref.refs_0_, bf16[2,256,512]{2,1,0:T(8,128)(2,1)} %copy-done.13, bf16[2,272,512]{2,1,0:T(8,128)(2,1)} %copy-done.9, bf16[2,256,512]{2,1,0:T(8,128)(2,1)} %copy-done.24, bf16[2,272,512]{2,1,0:T(8,128)(2,1)} %copy-done.16, ...), custom_call_target="tpu_custom_call" | custom-call | flops 6442450944 | bytes 12845056 | tf_op jit(solution)/shard_map/gram_part/pallas_call | solution.py:437
  166.2 0.1 collective-permute-start.27
  166.3 0.7 copy-done.3
  167.0 0.0 collective-permute-start.35
  167.1 1.4 collective-permute-done.27.refs_22_.refs_9_.refs_26_
  168.5 0.7 collective-permute-done.35.refs_30_.refs_17_.refs_34_
  169.2 0.0 copy-done.11
  169.2 0.8 copy-done.12
  170.0 5.7 %all-to-all-start = ((bf16[16,528,128]{2,1,0:T(8,128)(2,1)}), bf16[16,528,128]{2,1,0:T(8,128)(2,1)S(1)}, u32[]{:S(2)}, u32[]{:S(2)}) async-start(bf16[16,528,128]{2,1,0:T(8,128)(2,1)} %after.3), calls=%async_computation | async-start | bytes 4325376 | tf_op jit(solution)/shard_map/all_to_all | solution.py:650
  177.0 0.6 stack.31.refs_0_
  177.6 49.3 %gram_factor.1 = (f32[1024,1024]{1,0:T(8,128)}, f32[1024,128]{1,0:T(8,128)}, f32[1,1]{1,0:T(1,128)}) custom-call(s32[1]{0:T(128)} %bitcast.tile_ref.refs_0_, f32[1024,1024]{1,0:T(8,128)} %get-tuple-element.14.refs_0_.refs_1_, f32[8,128]{1,0:T(8,128)} %get-tuple-element.15.refs_1_.refs_2_, bf16[2,256,512]{2,1,0:T(8,128)(2,1)} %copy-done.5, ...), custom_call_target="tpu_custom_call" | custom-call | tf_op jit(solution)/shard_map/gram_factor/pallas_call | solution.py:457
  226.9 1.4 copy-done.2
  228.3 18.0 %whiten_rows.1 = (f32[128,1024]{1,0:T(8,128)}, f32[128,1024]{1,0:T(8,128)}) custom-call(s32[5]{0:T(128)} %stack.31.refs_0_, bf16[16,528,128]{2,1,0:T(8,128)(2,1)} %copy-done.2, f32[1024,1024]{1,0:T(8,128)} %get-tuple-element.16.refs_2_, f32[1024,128]{1,0:T(8,128)} %get-tuple-element.17.refs_3_, bf16[2,256,512]{2,1,0:T(8,128)(2,1)} %copy-done.13, ...), custom_call_target="tpu_custom_call" | custom-call | tf_op jit(solution)/shard_map/whiten_rows/pallas_call | solution.py:548
  (100 shorter events, 0.3 us)
Async XLA Ops:
  0.6 7.6 %copy-start.29 = (s32[16,128]{1,0:T(8,128)S(1)}, s32[16,128]{1,0:T(8,128)}, u32[]{:S(2)}) copy-start(s32[16,128]{1,0:T(8,128)} %refs_7_.1) | copy-start | bytes 24580
  0.6 7.7 %copy-start.33 = (s32[8]{0:T(128)S(1)}, s32[8]{0:T(128)}, u32[]{:S(2)}) copy-start(s32[8]{0:T(128)} %param.15) | copy-start | bytes 100
  0.7 10.8 %copy-start.31 = (f32[3,4]{1,0:T(4,128)S(1)}, f32[3,4]{1,0:T(4,128)}, u32[]{:S(2)}) copy-start(f32[3,4]{1,0:T(4,128)} %param.12) | copy-start | bytes 148
  0.7 11.3 %copy-start.32 = (f32[3,3]{1,0:T(4,128)S(1)}, f32[3,3]{1,0:T(4,128)}, u32[]{:S(2)}) copy-start(f32[3,3]{1,0:T(4,128)} %param.13) | copy-start | bytes 112
  0.7 12.0 %copy-start.28 = (f32[3,3,3,9]{3,2,1,0:T(4,128)S(1)}, f32[3,3,3,9]{3,2,1,0:T(4,128)}, u32[]{:S(2)}) copy-start(f32[3,3,3,9]{3,2,1,0:T(4,128)} %param.11) | copy-start | bytes 2920
  7.8 5.5 %collective-permute-start = (bf16[513,16,128]{2,1,0:T(8,128)(2,1)}, bf16[513,16,128]{2,1,0:T(8,128)(2,1)S(1)}, u32[]{:S(2)}, u32[]{:S(2)}) collective-permute-start(bf16[513,16,128]{2,1,0:T(8,128)(2,1)} %halo_rows.1), channel_id=1, source_target_pairs={{0,1},{1,0},{2,3},{3,2},{4,5},{5,4},{6,7},{7,6},{8,9},{9,8},{10,11... | collective-permute-start | bytes 6303752 | tf_op jit(solution)/shard_map/ppermute | solution.py:625
  8.3 5.0 %collective-permute-start.1 = (s32[16,128]{1,0:T(8,128)S(1)}, s32[16,128]{1,0:T(8,128)S(1)}, u32[]{:S(2)}, u32[]{:S(2)}) collective-permute-start(s32[16,128]{1,0:T(8,128)S(1)} %copy-done.29), channel_id=1, source_target_pairs={{0,1},{1,0},{2,3},{3,2},{4,5},{5,4},{6,7},{7,6},{8,9},{9,8},{10,11... | collective-permute-start | bytes 24584 | tf_op jit(solution)/shard_map/ppermute | solution.py:624
  45.7 3.5 %copy-start = (bf16[16,528,128]{2,1,0:T(8,128)(2,1)S(1)}, bf16[16,528,128]{2,1,0:T(8,128)(2,1)}, u32[]{:S(2)}) copy-start(bf16[16,528,128]{2,1,0:T(8,128)(2,1)} %encode.1.enc_ref.value_ref) | copy-start | bytes 6488068
  45.7 3.5 %copy-start.1 = (s32[512]{0:T(512)S(1)}, s32[512]{0:T(512)}, u32[]{:S(2)}) copy-start(s32[512]{0:T(512)} %param.9) | copy-start | bytes 6148
  47.1 2.1 collective-permute-start.2
  50.6 15.1 %collective-permute-start.3 = (bf16[1,256,512]{2,1,0:T(8,128)(2,1)S(1)}, bf16[1,256,512]{2,1,0:T(8,128)(2,1)S(1)}, u32[]{:S(2)}, u32[]{:S(2)}) collective-permute-start(bf16[1,256,512]{2,1,0:T(8,128)(2,1)S(1)} %bitcast.16), channel_id=1, source_target_pairs={{0,8},{2,10},{4,12},{6,14},{8,0},{10,2},{12,4},{14,6},{16,24},{18,... | collective-permute-start | bytes 786440 | tf_op jit(solution)/shard_map/ppermute | solution.py:581
  53.5 26.7 %collective-permute-start.19 = (bf16[1,256,512]{2,1,0:T(8,128)(2,1)S(1)}, bf16[1,256,512]{2,1,0:T(8,128)(2,1)S(1)}, u32[]{:S(2)}, u32[]{:S(2)}) collective-permute-start(bf16[1,256,512]{2,1,0:T(8,128)(2,1)S(1)} %bitcast.17), channel_id=1, source_target_pairs={{0,16},{2,18},{4,20},{6,22},{8,24},{10,26},{12,28},{14,30},{16,0},... | collective-permute-start | bytes 786440 | tf_op jit(solution)/shard_map/ppermute | solution.py:581
  56.1 24.1 %collective-permute-start.21 = (bf16[1,272,512]{2,1,0:T(8,128)(2,1)S(1)}, bf16[1,272,512]{2,1,0:T(8,128)(2,1)S(1)}, u32[]{:S(2)}, u32[]{:S(2)}) collective-permute-start(bf16[1,272,512]{2,1,0:T(8,128)(2,1)S(1)} %bitcast.13), channel_id=1, source_target_pairs={{0,16},{2,18},{4,20},{6,22},{8,24},{10,26},{12,28},{14,30},{16,0},... | collective-permute-start | bytes 835592 | tf_op jit(solution)/shard_map/ppermute | solution.py:581
  65.7 90.0 %copy-start.13 = (bf16[2,256,512]{2,1,0:T(8,128)(2,1)}, bf16[2,256,512]{2,1,0:T(8,128)(2,1)S(1)}, u32[]{:S(2)}) copy-start(bf16[2,256,512]{2,1,0:T(8,128)(2,1)S(1)} %pad_maximum_fusion.1.refs_0_.refs_4_) | copy-start | bytes 1572868
  65.7 29.2 %collective-permute-start.11 = (bf16[2,256,512]{2,1,0:T(8,128)(2,1)S(1)}, bf16[2,256,512]{2,1,0:T(8,128)(2,1)S(1)}, u32[]{:S(2)}, u32[]{:S(2)}) collective-permute-start(bf16[2,256,512]{2,1,0:T(8,128)(2,1)S(1)} %pad_maximum_fusion.1.refs_0_.refs_4_), channel_id=1, source_target_pairs={{0,4},{2,6},{4,0},{6,2},{8,12},{10,14},{12,8},{14,10},{16,20},{18,... | collective-permute-start | bytes 1572872 | tf_op jit(solution)/shard_map/ppermute | solution.py:581
  67.5 16.3 %collective-permute-start.4 = (bf16[1,272,512]{2,1,0:T(8,128)(2,1)S(1)}, bf16[1,272,512]{2,1,0:T(8,128)(2,1)S(1)}, u32[]{:S(2)}, u32[]{:S(2)}) collective-permute-start(bf16[1,272,512]{2,1,0:T(8,128)(2,1)S(1)} %bitcast.14), channel_id=1, source_target_pairs={{0,8},{2,10},{4,12},{6,14},{8,0},{10,2},{12,4},{14,6},{16,24},{18,... | collective-permute-start | bytes 835592 | tf_op jit(solution)/shard_map/ppermute | solution.py:581
  80.2 14.7 %collective-permute-start.22 = (bf16[1,272,512]{2,1,0:T(8,128)(2,1)S(1)}, bf16[1,272,512]{2,1,0:T(8,128)(2,1)S(1)}, u32[]{:S(2)}, u32[]{:S(2)}) collective-permute-start(bf16[1,272,512]{2,1,0:T(8,128)(2,1)S(1)} %collective-permute-done.21), channel_id=1, source_target_pairs={{0,8},{2,10},{4,12},{6,14},{8,0},{10,2},{12,4},{14,6},{16,24},{18,... | collective-permute-start | bytes 835592 | tf_op jit(solution)/shard_map/ppermute | solution.py:581
  80.2 13.2 %collective-permute-start.20 = (bf16[1,256,512]{2,1,0:T(8,128)(2,1)S(1)}, bf16[1,256,512]{2,1,0:T(8,128)(2,1)S(1)}, u32[]{:S(2)}, u32[]{:S(2)}) collective-permute-start(bf16[1,256,512]{2,1,0:T(8,128)(2,1)S(1)} %collective-permute-done.19), channel_id=1, source_target_pairs={{0,8},{2,10},{4,12},{6,14},{8,0},{10,2},{12,4},{14,6},{16,24},{18,... | collective-permute-start | bytes 786440 | tf_op jit(solution)/shard_map/ppermute | solution.py:581
  82.2 13.3 %collective-permute-start.7 = (bf16[2,256,512]{2,1,0:T(8,128)(2,1)S(1)}, bf16[2,256,512]{2,1,0:T(8,128)(2,1)S(1)}, u32[]{:S(2)}, u32[]{:S(2)}) collective-permute-start(bf16[2,256,512]{2,1,0:T(8,128)(2,1)S(1)} %pad_maximum_fusion.1.refs_0_.refs_4_), channel_id=1, source_target_pairs={{0,2},{2,0},{4,6},{6,4},{8,10},{10,8},{12,14},{14,12},{16,18},{18,... | collective-permute-start | bytes 1572872 | tf_op jit(solution)/shard_map/ppermute | solution.py:581
  83.8 71.9 %copy-start.9 = (bf16[2,272,512]{2,1,0:T(8,128)(2,1)}, bf16[2,272,512]{2,1,0:T(8,128)(2,1)S(1)}, u32[]{:S(2)}) copy-start(bf16[2,272,512]{2,1,0:T(8,128)(2,1)S(1)} %pad_maximum_fusion.refs_1_.refs_5_) | copy-start | bytes 1671172
  83.8 14.5 %collective-permute-start.12 = (bf16[2,272,512]{2,1,0:T(8,128)(2,1)S(1)}, bf16[2,272,512]{2,1,0:T(8,128)(2,1)S(1)}, u32[]{:S(2)}, u32[]{:S(2)}) collective-permute-start(bf16[2,272,512]{2,1,0:T(8,128)(2,1)S(1)} %pad_maximum_fusion.refs_1_.refs_5_), channel_id=1, source_target_pairs={{0,4},{2,6},{4,0},{6,2},{8,12},{10,14},{12,8},{14,10},{16,20},{18,... | collective-permute-start | bytes 1671176 | tf_op jit(solution)/shard_map/ppermute | solution.py:581
  93.4 15.6 %collective-permute-start.8 = (bf16[2,272,512]{2,1,0:T(8,128)(2,1)S(1)}, bf16[2,272,512]{2,1,0:T(8,128)(2,1)S(1)}, u32[]{:S(2)}, u32[]{:S(2)}) collective-permute-start(bf16[2,272,512]{2,1,0:T(8,128)(2,1)S(1)} %pad_maximum_fusion.refs_1_.refs_5_), channel_id=1, source_target_pairs={{0,2},{2,0},{4,6},{6,4},{8,10},{10,8},{12,14},{14,12},{16,18},{18,... | collective-permute-start | bytes 1671176 | tf_op jit(solution)/shard_map/ppermute | solution.py:581
  94.9 2.2 collective-permute-start.5
  94.9 60.8 %copy-start.22 = (bf16[2,256,512]{2,1,0:T(8,128)(2,1)}, bf16[2,256,512]{2,1,0:T(8,128)(2,1)S(1)}, u32[]{:S(2)}) copy-start(bf16[2,256,512]{2,1,0:T(8,128)(2,1)S(1)} %collective-permute-done.11.refs_8_.refs_12_) | copy-start | bytes 1572868
  94.9 14.0 %collective-permute-start.6 = (bf16[2,272,512]{2,1,0:T(8,128)(2,1)S(1)}, bf16[2,272,512]{2,1,0:T(8,128)(2,1)S(1)}, u32[]{:S(2)}, u32[]{:S(2)}) collective-permute-start(bf16[2,272,512]{2,1,0:T(8,128)(2,1)S(1)} %pad_maximum_fusion.refs_1_.refs_5_), channel_id=1, source_target_pairs={{0,1},{1,0},{2,3},{3,2},{4,5},{5,4},{6,7},{7,6},{8,9},{9,8},{10,11... | collective-permute-start | bytes 1671176 | tf_op jit(solution)/shard_map/ppermute | solution.py:604
  95.5 70.7 %copy-start.5 = (bf16[2,256,512]{2,1,0:T(8,128)(2,1)}, bf16[2,256,512]{2,1,0:T(8,128)(2,1)S(1)}, u32[]{:S(2)}) copy-start(bf16[2,256,512]{2,1,0:T(8,128)(2,1)S(1)} %constant_dynamic-update-slice_fusion.refs_16_.refs_3_.refs_20_) | copy-start | bytes 1572868
  95.5 49.2 %copy-start.23 = (bf16[2,256,512]{2,1,0:T(8,128)(2,1)}, bf16[2,256,512]{2,1,0:T(8,128)(2,1)S(1)}, u32[]{:S(2)}) copy-start(bf16[2,256,512]{2,1,0:T(8,128)(2,1)S(1)} %collective-permute-done.7.refs_4_.refs_8_) | copy-start | bytes 1572868
  95.5 15.0 %collective-permute-start.29 = (bf16[2,256,512]{2,1,0:T(8,128)(2,1)S(1)}, bf16[2,256,512]{2,1,0:T(8,128)(2,1)}, u32[]{:S(2)}, u32[]{:S(2)}) collective-permute-start(bf16[2,256,512]{2,1,0:T(8,128)(2,1)S(1)} %constant_dynamic-update-slice_fusion.refs_16_.refs_3_.refs_20_), channel_id=1, source_target_pairs={{0,4},{2,6},{4,0},{6,2},{8,12},{10,14},{12,8},{14,10},{16,20},{18,... | collective-permute-start | bytes 1572872 | tf_op jit(solution)/shard_map/ppermute | solution.py:581
  97.1 69.1 %copy-start.4 = (bf16[2,272,512]{2,1,0:T(8,128)(2,1)}, bf16[2,272,512]{2,1,0:T(8,128)(2,1)S(1)}, u32[]{:S(2)}) copy-start(bf16[2,272,512]{2,1,0:T(8,128)(2,1)S(1)} %constant_dynamic-update-slice_fusion.2.refs_17_.refs_4_.refs_21_) | copy-start | bytes 1671172
  97.1 1.8 copy-start.24
  97.1 24.7 %collective-permute-start.30 = (bf16[2,272,512]{2,1,0:T(8,128)(2,1)S(1)}, bf16[2,272,512]{2,1,0:T(8,128)(2,1)S(1)}, u32[]{:S(2)}, u32[]{:S(2)}) collective-permute-start(bf16[2,272,512]{2,1,0:T(8,128)(2,1)S(1)} %constant_dynamic-update-slice_fusion.2.refs_17_.refs_4_.refs_21_), channel_id=1, source_target_pairs={{0,4},{2,6},{4,0},{6,2},{8,12},{10,14},{12,8},{14,10},{16,20},{18,... | collective-permute-start | bytes 1671176 | tf_op jit(solution)/shard_map/ppermute | solution.py:581
  98.3 57.4 %copy-start.14 = (bf16[2,272,512]{2,1,0:T(8,128)(2,1)}, bf16[2,272,512]{2,1,0:T(8,128)(2,1)S(1)}, u32[]{:S(2)}) copy-start(bf16[2,272,512]{2,1,0:T(8,128)(2,1)S(1)} %collective-permute-done.12.refs_9_.refs_13_) | copy-start | bytes 1671172
  98.3 22.0 %collective-permute-start.25 = (bf16[2,256,512]{2,1,0:T(8,128)(2,1)S(1)}, bf16[2,256,512]{2,1,0:T(8,128)(2,1)}, u32[]{:S(2)}, u32[]{:S(2)}) collective-permute-start(bf16[2,256,512]{2,1,0:T(8,128)(2,1)S(1)} %constant_dynamic-update-slice_fusion.refs_16_.refs_3_.refs_20_), channel_id=1, source_target_pairs={{0,2},{2,0},{4,6},{6,4},{8,10},{10,8},{12,14},{14,12},{16,18},{18,... | collective-permute-start | bytes 1572872 | tf_op jit(solution)/shard_map/ppermute | solution.py:581
  108.9 46.8 %copy-start.15 = (bf16[2,272,512]{2,1,0:T(8,128)(2,1)}, bf16[2,272,512]{2,1,0:T(8,128)(2,1)S(1)}, u32[]{:S(2)}) copy-start(bf16[2,272,512]{2,1,0:T(8,128)(2,1)S(1)} %collective-permute-done.8.refs_5_.refs_9_) | copy-start | bytes 1671172
  108.9 12.8 %collective-permute-start.23 = (bf16[2,256,512]{2,1,0:T(8,128)(2,1)S(1)}, bf16[2,256,512]{2,1,0:T(8,128)(2,1)S(1)}, u32[]{:S(2)}, u32[]{:S(2)}) collective-permute-start(bf16[2,256,512]{2,1,0:T(8,128)(2,1)S(1)} %constant_dynamic-update-slice_fusion.refs_16_.refs_3_.refs_20_), channel_id=1, source_target_pairs={{0,1},{1,0},{2,3},{3,2},{4,5},{5,4},{6,7},{7,6},{8,9},{9,8},{10,11... | collective-permute-start | bytes 1572872 | tf_op jit(solution)/shard_map/ppermute | solution.py:604
  109.0 46.8 %copy-start.16 = (bf16[2,272,512]{2,1,0:T(8,128)(2,1)}, bf16[2,272,512]{2,1,0:T(8,128)(2,1)S(1)}, u32[]{:S(2)}) copy-start(bf16[2,272,512]{2,1,0:T(8,128)(2,1)S(1)} %collective-permute-done.6.refs_3_.refs_7_) | copy-start | bytes 1671172
  109.0 23.2 %collective-permute-start.26 = (bf16[2,272,512]{2,1,0:T(8,128)(2,1)S(1)}, bf16[2,272,512]{2,1,0:T(8,128)(2,1)S(1)}, u32[]{:S(2)}, u32[]{:S(2)}) collective-permute-start(bf16[2,272,512]{2,1,0:T(8,128)(2,1)S(1)} %constant_dynamic-update-slice_fusion.2.refs_17_.refs_4_.refs_21_), channel_id=1, source_target_pairs={{0,2},{2,0},{4,6},{6,4},{8,10},{10,8},{12,14},{14,12},{16,18},{18,... | collective-permute-start | bytes 1671176 | tf_op jit(solution)/shard_map/ppermute | solution.py:581
  110.5 21.6 %collective-permute-start.24 = (bf16[2,272,512]{2,1,0:T(8,128)(2,1)S(1)}, bf16[2,272,512]{2,1,0:T(8,128)(2,1)S(1)}, u32[]{:S(2)}, u32[]{:S(2)}) collective-permute-start(bf16[2,272,512]{2,1,0:T(8,128)(2,1)S(1)} %constant_dynamic-update-slice_fusion.2.refs_17_.refs_4_.refs_21_), channel_id=1, source_target_pairs={{0,1},{1,0},{2,3},{3,2},{4,5},{5,4},{6,7},{7,6},{8,9},{9,8},{10,11... | collective-permute-start | bytes 1671176 | tf_op jit(solution)/shard_map/ppermute | solution.py:604
  120.3 23.8 %collective-permute-start.16 = (bf16[2,272,512]{2,1,0:T(8,128)(2,1)S(1)}, bf16[2,272,512]{2,1,0:T(8,128)(2,1)S(1)}, u32[]{:S(2)}, u32[]{:S(2)}) collective-permute-start(bf16[2,272,512]{2,1,0:T(8,128)(2,1)S(1)} %collective-permute-done.12.refs_9_.refs_13_), channel_id=1, source_target_pairs={{0,2},{2,0},{4,6},{6,4},{8,10},{10,8},{12,14},{14,12},{16,18},{18,... | collective-permute-start | bytes 1671176 | tf_op jit(solution)/shard_map/ppermute | solution.py:581
  121.8 44.4 %copy-start.10 = (bf16[2,256,512]{2,1,0:T(8,128)(2,1)}, bf16[2,256,512]{2,1,0:T(8,128)(2,1)S(1)}, u32[]{:S(2)}) copy-start(bf16[2,256,512]{2,1,0:T(8,128)(2,1)S(1)} %collective-permute-done.23.refs_18_.refs_5_.refs_22_) | copy-start | bytes 1572868
  121.8 10.8 %collective-permute-start.13 = (bf16[2,256,512]{2,1,0:T(8,128)(2,1)S(1)}, bf16[2,256,512]{2,1,0:T(8,128)(2,1)}, u32[]{:S(2)}, u32[]{:S(2)}) collective-permute-start(bf16[2,256,512]{2,1,0:T(8,128)(2,1)S(1)} %collective-permute-done.11.refs_8_.refs_12_), channel_id=1, source_target_pairs={{0,1},{1,0},{2,3},{3,2},{4,5},{5,4},{6,7},{7,6},{8,9},{9,8},{10,11... | collective-permute-start | bytes 1572872 | tf_op jit(solution)/shard_map/ppermute | solution.py:604
  121.8 44.4 %copy-start.6 = (bf16[2,272,512]{2,1,0:T(8,128)(2,1)}, bf16[2,272,512]{2,1,0:T(8,128)(2,1)S(1)}, u32[]{:S(2)}) copy-start(bf16[2,272,512]{2,1,0:T(8,128)(2,1)S(1)} %collective-permute-done.30.refs_25_.refs_12_.refs_29_) | copy-start | bytes 1671172
  121.8 14.3 %collective-permute-start.15 = (bf16[2,256,512]{2,1,0:T(8,128)(2,1)S(1)}, bf16[2,256,512]{2,1,0:T(8,128)(2,1)S(1)}, u32[]{:S(2)}, u32[]{:S(2)}) collective-permute-start(bf16[2,256,512]{2,1,0:T(8,128)(2,1)S(1)} %collective-permute-done.7.refs_4_.refs_8_), channel_id=1, source_target_pairs={{0,4},{2,6},{4,0},{6,2},{8,12},{10,14},{12,8},{14,10},{16,20},{18,... | collective-permute-start | bytes 1572872 | tf_op jit(solution)/shard_map/ppermute | solution.py:581
  132.1 34.1 %copy-start.7 = (bf16[2,272,512]{2,1,0:T(8,128)(2,1)}, bf16[2,272,512]{2,1,0:T(8,128)(2,1)S(1)}, u32[]{:S(2)}) copy-start(bf16[2,272,512]{2,1,0:T(8,128)(2,1)S(1)} %collective-permute-done.26.refs_21_.refs_8_.refs_25_) | copy-start | bytes 1671172
  132.1 11.9 %collective-permute-start.9 = (bf16[2,256,512]{2,1,0:T(8,128)(2,1)S(1)}, bf16[2,256,512]{2,1,0:T(8,128)(2,1)S(1)}, u32[]{:S(2)}, u32[]{:S(2)}) collective-permute-start(bf16[2,256,512]{2,1,0:T(8,128)(2,1)S(1)} %collective-permute-done.7.refs_4_.refs_8_), channel_id=1, source_target_pairs={{0,1},{1,0},{2,3},{3,2},{4,5},{5,4},{6,7},{7,6},{8,9},{9,8},{10,11... | collective-permute-start | bytes 1572872 | tf_op jit(solution)/shard_map/ppermute | solution.py:604
  132.1 12.5 %copy-start.8 = (bf16[2,272,512]{2,1,0:T(8,128)(2,1)}, bf16[2,272,512]{2,1,0:T(8,128)(2,1)S(1)}, u32[]{:S(2)}) copy-start(bf16[2,272,512]{2,1,0:T(8,128)(2,1)S(1)} %collective-permute-done.24.refs_19_.refs_6_.refs_23_) | copy-start | bytes 1671172
  132.1 12.4 %collective-permute-start.14 = (bf16[2,272,512]{2,1,0:T(8,128)(2,1)S(1)}, bf16[2,272,512]{2,1,0:T(8,128)(2,1)S(1)}, u32[]{:S(2)}, u32[]{:S(2)}) collective-permute-start(bf16[2,272,512]{2,1,0:T(8,128)(2,1)S(1)} %collective-permute-done.12.refs_9_.refs_13_), channel_id=1, source_target_pairs={{0,1},{1,0},{2,3},{3,2},{4,5},{5,4},{6,7},{7,6},{8,9},{9,8},{10,11... | collective-permute-start | bytes 1671176 | tf_op jit(solution)/shard_map/ppermute | solution.py:604
  132.6 12.0 %collective-permute-start.10 = (bf16[2,272,512]{2,1,0:T(8,128)(2,1)S(1)}, bf16[2,272,512]{2,1,0:T(8,128)(2,1)S(1)}, u32[]{:S(2)}, u32[]{:S(2)}) collective-permute-start(bf16[2,272,512]{2,1,0:T(8,128)(2,1)S(1)} %collective-permute-done.8.refs_5_.refs_9_), channel_id=1, source_target_pairs={{0,1},{1,0},{2,3},{3,2},{4,5},{5,4},{6,7},{7,6},{8,9},{9,8},{10,11... | collective-permute-start | bytes 1671176 | tf_op jit(solution)/shard_map/ppermute | solution.py:604
  136.2 18.0 %copy-start.25 = (bf16[2,256,512]{2,1,0:T(8,128)(2,1)}, bf16[2,256,512]{2,1,0:T(8,128)(2,1)S(1)}, u32[]{:S(2)}) copy-start(bf16[2,256,512]{2,1,0:T(8,128)(2,1)S(1)} %collective-permute-done.15.refs_12_.refs_16_) | copy-start | bytes 1572868
  136.2 17.4 %collective-permute-start.34 = (bf16[2,272,512]{2,1,0:T(8,128)(2,1)S(1)}, bf16[2,272,512]{2,1,0:T(8,128)(2,1)}, u32[]{:S(2)}, u32[]{:S(2)}) collective-permute-start(bf16[2,272,512]{2,1,0:T(8,128)(2,1)S(1)} %collective-permute-done.30.refs_25_.refs_12_.refs_29_), channel_id=1, source_target_pairs={{0,2},{2,0},{4,6},{6,4},{8,10},{10,8},{12,14},{14,12},{16,18},{18,... | collective-permute-start | bytes 1671176 | tf_op jit(solution)/shard_map/ppermute | solution.py:581
  144.1 11.7 %copy-start.17 = (bf16[2,272,512]{2,1,0:T(8,128)(2,1)}, bf16[2,272,512]{2,1,0:T(8,128)(2,1)S(1)}, u32[]{:S(2)}) copy-start(bf16[2,272,512]{2,1,0:T(8,128)(2,1)S(1)} %collective-permute-done.16.refs_13_.refs_17_) | copy-start | bytes 1671172
  144.1 10.1 %collective-permute-start.18 = (bf16[2,272,512]{2,1,0:T(8,128)(2,1)S(1)}, bf16[2,272,512]{2,1,0:T(8,128)(2,1)S(1)}, u32[]{:S(2)}, u32[]{:S(2)}) collective-permute-start(bf16[2,272,512]{2,1,0:T(8,128)(2,1)S(1)} %collective-permute-done.16.refs_13_.refs_17_), channel_id=1, source_target_pairs={{0,1},{1,0},{2,3},{3,2},{4,5},{5,4},{6,7},{7,6},{8,9},{9,8},{10,11... | collective-permute-start | bytes 1671176 | tf_op jit(solution)/shard_map/ppermute | solution.py:604
  144.1 10.0 %copy-start.26 = (bf16[2,256,512]{2,1,0:T(8,128)(2,1)}, bf16[2,256,512]{2,1,0:T(8,128)(2,1)S(1)}, u32[]{:S(2)}) copy-start(bf16[2,256,512]{2,1,0:T(8,128)(2,1)S(1)} %collective-permute-done.9.refs_6_.refs_10_) | copy-start | bytes 1572868
  144.1 9.5 %collective-permute-start.17 = (bf16[2,256,512]{2,1,0:T(8,128)(2,1)S(1)}, bf16[2,256,512]{2,1,0:T(8,128)(2,1)S(1)}, u32[]{:S(2)}, u32[]{:S(2)}) collective-permute-start(bf16[2,256,512]{2,1,0:T(8,128)(2,1)S(1)} %collective-permute-done.15.refs_12_.refs_16_), channel_id=1, source_target_pairs={{0,1},{1,0},{2,3},{3,2},{4,5},{5,4},{6,7},{7,6},{8,9},{9,8},{10,11... | collective-permute-start | bytes 1572872 | tf_op jit(solution)/shard_map/ppermute | solution.py:604
  144.6 11.2 %copy-start.18 = (bf16[2,272,512]{2,1,0:T(8,128)(2,1)}, bf16[2,272,512]{2,1,0:T(8,128)(2,1)S(1)}, u32[]{:S(2)}) copy-start(bf16[2,272,512]{2,1,0:T(8,128)(2,1)S(1)} %collective-permute-done.14.refs_11_.refs_15_) | copy-start | bytes 1671172
  144.6 22.5 %collective-permute-start.31 = (bf16[2,256,512]{2,1,0:T(8,128)(2,1)}, bf16[2,256,512]{2,1,0:T(8,128)(2,1)}, u32[]{:S(2)}, u32[]{:S(2)}) collective-permute-start(bf16[2,256,512]{2,1,0:T(8,128)(2,1)} %collective-permute-done.29.refs_24_.refs_11_.refs_28_), channel_id=1, source_target_pairs={{0,1},{1,0},{2,3},{3,2},{4,5},{5,4},{6,7},{7,6},{8,9},{9,8},{10,11... | collective-permute-start | bytes 1572872 | tf_op jit(solution)/shard_map/ppermute | solution.py:604
  144.7 9.4 %copy-start.19 = (bf16[2,272,512]{2,1,0:T(8,128)(2,1)}, bf16[2,272,512]{2,1,0:T(8,128)(2,1)S(1)}, u32[]{:S(2)}) copy-start(bf16[2,272,512]{2,1,0:T(8,128)(2,1)S(1)} %collective-permute-done.10.refs_7_.refs_11_) | copy-start | bytes 1671172
  144.7 21.5 %collective-permute-start.33 = (bf16[2,256,512]{2,1,0:T(8,128)(2,1)}, bf16[2,256,512]{2,1,0:T(8,128)(2,1)S(1)}, u32[]{:S(2)}, u32[]{:S(2)}) collective-permute-start(bf16[2,256,512]{2,1,0:T(8,128)(2,1)} %collective-permute-done.25.refs_20_.refs_7_.refs_24_), channel_id=1, source_target_pairs={{0,4},{2,6},{4,0},{6,2},{8,12},{10,14},{12,8},{14,10},{16,20},{18,... | collective-permute-start | bytes 1572872 | tf_op jit(solution)/shard_map/ppermute | solution.py:581
  153.6 14.8 %collective-permute-start.32 = (bf16[2,272,512]{2,1,0:T(8,128)(2,1)S(1)}, bf16[2,272,512]{2,1,0:T(8,128)(2,1)}, u32[]{:S(2)}, u32[]{:S(2)}) collective-permute-start(bf16[2,272,512]{2,1,0:T(8,128)(2,1)S(1)} %collective-permute-done.30.refs_25_.refs_12_.refs_29_), channel_id=1, source_target_pairs={{0,1},{1,0},{2,3},{3,2},{4,5},{5,4},{6,7},{7,6},{8,9},{9,8},{10,11... | collective-permute-start | bytes 1671176 | tf_op jit(solution)/shard_map/ppermute | solution.py:604
  153.6 14.8 %collective-permute-start.28 = (bf16[2,272,512]{2,1,0:T(8,128)(2,1)S(1)}, bf16[2,272,512]{2,1,0:T(8,128)(2,1)}, u32[]{:S(2)}, u32[]{:S(2)}) collective-permute-start(bf16[2,272,512]{2,1,0:T(8,128)(2,1)S(1)} %collective-permute-done.26.refs_21_.refs_8_.refs_25_), channel_id=1, source_target_pairs={{0,1},{1,0},{2,3},{3,2},{4,5},{5,4},{6,7},{7,6},{8,9},{9,8},{10,11... | collective-permute-start | bytes 1671176 | tf_op jit(solution)/shard_map/ppermute | solution.py:604
  155.2 13.2 %collective-permute-start.36 = (bf16[2,272,512]{2,1,0:T(8,128)(2,1)}, bf16[2,272,512]{2,1,0:T(8,128)(2,1)}, u32[]{:S(2)}, u32[]{:S(2)}) collective-permute-start(bf16[2,272,512]{2,1,0:T(8,128)(2,1)} %collective-permute-done.34.refs_29_.refs_16_.refs_33_), channel_id=1, source_target_pairs={{0,1},{1,0},{2,3},{3,2},{4,5},{5,4},{6,7},{7,6},{8,9},{9,8},{10,11... | collective-permute-start | bytes 1671176 | tf_op jit(solution)/shard_map/ppermute | solution.py:604
  166.2 2.2 collective-permute-start.27
  167.0 2.1 collective-permute-start.35
  170.0 56.9 %all-to-all-start = ((bf16[16,528,128]{2,1,0:T(8,128)(2,1)}), bf16[16,528,128]{2,1,0:T(8,128)(2,1)S(1)}, u32[]{:S(2)}, u32[]{:S(2)}) async-start(bf16[16,528,128]{2,1,0:T(8,128)(2,1)} %after.3), calls=%async_computation | async-start | bytes 4325376 | tf_op jit(solution)/shard_map/all_to_all | solution.py:650
  (8 other events, 7.3 us)
